TPU v7x, 256 devices: a whole 4x4x8 slice. The times are simulated.
256 devices in a mesh: row: 8 (over z_lo, core), col: 16 (over y, x), samp: 2 (over z_hi).
Axes of the slice: x: 4, y: 4, z: 8 (z_hi: 2, z_lo: 4; z = z_hi * 4 + z_lo), core: 2. Of those that a mesh axis runs over, the one named last changes fastest.
Arguments:
- pair_in: bfloat16 [512, 512, 128], P('row', 'col'), may hold values from -6 to 6
- residue_index: int32 [512], replicated, may hold values from 0 to 47
- chain_index: int32 [512], replicated, may hold values from 0 to 2
- token_mask: int32 [512], replicated, may hold values 0 or 1
- relpos_weight: bfloat16 [66, 128], replicated, may hold values from -5 to 5
- tri_proj: bfloat16 [128, 640], replicated, may hold values from -0.5 to 0.5
- tri_out: bfloat16 [128, 128], replicated, may hold values from -0.5 to 0.5
- bias_proj: bfloat16 [128, 16], replicated, may hold values from -0.5 to 0.5
- single: bfloat16 [512, 384], P('row'), may hold values from -6 to 6
- ada_proj: bfloat16 [384, 2304], replicated, may hold values from -0.3125 to 0.3125
- noisy: bfloat16 [16, 512, 768], P('samp', 'row'), may hold values from -6 to 6
- qkv_proj: bfloat16 [768, 3, 768], P(None, None, 'col'), may hold values from -0.21875 to 0.21875
- out_proj: bfloat16 [768, 768], P('col'), may hold values from -0.21875 to 0.21875
- cotangent: bfloat16 [16, 512, 768], P('samp', 'row', 'col'), may hold values from -6 to 6
Outputs:
- pair_out: bfloat16 [512, 512, 128], P('row', 'col')
- block_out: bfloat16 [16, 512, 768], P('samp', 'row', 'col')
- grad_pair: float32 [512, 512, 128], P('row', 'col')
- grad_single: float32 [512, 384], P('row')
All inputs are finite; a program needn't handle non-finite values.
Results may differ from a plain program's by a relative error of at most 0.012.
The roundings to bfloat16 on the way count: a program that leaves them out, or rounds other values in their place, can miss the bound.
Values may be sent and summed in bfloat16 or wider, within the bound.
A program may use at most 128 MiB of HBM per device.

v0:
```python
import jax
import jax.numpy as jnp
from jax import lax
from jax.sharding import PartitionSpec as P

HEAD_DIM = 48
REL_BINS = 66


EPSILON = 1e-05
HIGHEST = lax.Precision.HIGHEST


def joined_along(blocks, dim):
    dims = list(blocks.shape[1:])
    dims[dim] *= blocks.shape[0]
    return jnp.moveaxis(blocks, 0, dim).reshape(dims)


def sent_to_all(array, axis):
    copies = jnp.broadcast_to(array, (lax.axis_size(axis), *array.shape))
    return lax.all_to_all(copies, axis, split_axis=0, concat_axis=0, tiled=True)


def collect(array, axis, dim):
    return joined_along(sent_to_all(array, axis), dim)


def split_up(array, dim, size):
    dims = array.shape
    blocks = array.reshape(*dims[:dim], size, dims[dim] // size, *dims[dim + 1 :])
    return jnp.moveaxis(blocks, dim, 0)


def sent_and_summed(array, axis, dim):
    size = lax.axis_size(axis)
    blocks = lax.all_to_all(split_up(array, dim, size), axis, 0, 0, tiled=True)
    return jnp.sum(blocks, axis=0)


def gathered_total(array, axis):
    return lax.all_gather(array, axis).sum(0)


def taken_together(array, axis):
    return sent_to_all(array, axis).sum(axis=0)


def normalize(values_in):
    average = jnp.mean(values_in, -1, keepdims=True)
    centered = values_in - average
    variance = jnp.mean(centered * centered, -1, keepdims=True)
    return centered * lax.rsqrt(variance + EPSILON)


def normalize_grad(values_in, upstream):
    average = jnp.mean(values_in, -1, keepdims=True)
    centered = values_in - average
    variance = jnp.mean(centered * centered, -1, keepdims=True)
    inv_std = lax.rsqrt(variance + EPSILON)
    unit_rows = centered * inv_std
    return inv_std * (
        upstream
        - jnp.mean(upstream, -1, keepdims=True)
        - unit_rows * jnp.mean(upstream * unit_rows, -1, keepdims=True)
    )


def relative_embedding(res_rows, res_cols, chain_rows, chain_cols, relpos_weight):
    max_offset = (REL_BINS - 2) // 2
    offset = res_rows[:, None] - res_cols[None, :]
    bucket = jnp.where(
        chain_rows[:, None] == chain_cols[None, :],
        jnp.clip(offset + max_offset, 0, 2 * max_offset),
        REL_BINS - 1,
    )
    onehot = (bucket[:, :, None] == jnp.arange(REL_BINS, dtype=jnp.int32)[None, None, :]).astype(
        jnp.bfloat16
    )
    return jnp.einsum("ijr,rc->ijc", onehot, relpos_weight, preferred_element_type=jnp.float32)


def on_device(
    pair_in,
    residue_index,
    chain_index,
    token_mask,
    relpos_weight,
    tri_proj,
    tri_out,
    bias_proj,
    single,
    ada_proj,
    noisy,
    qkv_proj,
    out_proj,
    cotangent,
):
    tile_rows, tile_cols, pair_width = pair_in.shape
    row_at = lax.axis_index("row") * tile_rows
    col_at = lax.axis_index("col") * tile_cols
    res_rows = lax.dynamic_slice_in_dim(residue_index, row_at, tile_rows)
    res_cols = lax.dynamic_slice_in_dim(residue_index, col_at, tile_cols)
    chain_rows = lax.dynamic_slice_in_dim(chain_index, row_at, tile_rows)
    chain_cols = lax.dynamic_slice_in_dim(chain_index, col_at, tile_cols)
    pair_full = pair_in.astype(jnp.float32) + relative_embedding(
        res_rows, res_cols, chain_rows, chain_cols, relpos_weight
    )
    normed_pair = normalize(pair_full).astype(jnp.bfloat16)
    projected = jnp.dot(normed_pair, tri_proj, preferred_element_type=jnp.float32)
    mask_f = token_mask.astype(jnp.float32)
    mask_rows = lax.dynamic_slice_in_dim(mask_f, row_at, tile_rows)
    mask_cols = lax.dynamic_slice_in_dim(mask_f, col_at, tile_cols)
    pair_mask = (mask_rows[:, None] * mask_cols[None, :])[:, :, None]
    left_side = (
        jax.nn.sigmoid(projected[..., pair_width : 2 * pair_width])
        * projected[..., :pair_width]
        * pair_mask
    ).astype(jnp.bfloat16)
    right_side = (
        jax.nn.sigmoid(projected[..., 3 * pair_width : 4 * pair_width])
        * projected[..., 2 * pair_width : 3 * pair_width]
        * pair_mask
    ).astype(jnp.bfloat16)
    tri_gate = jax.nn.sigmoid(projected[..., 4 * pair_width :])
    right_all = lax.all_gather(right_side, "row", axis=0, tiled=True)
    triangle = jnp.swapaxes(
        lax.psum_scatter(
            jnp.einsum("jkc,ikc->jic", right_all, left_side, preferred_element_type=jnp.float32),
            "col",
            scatter_dimension=0,
            tiled=True,
        ),
        0,
        1,
    )
    update = jnp.dot(
        normalize(triangle).astype(jnp.bfloat16), tri_out, preferred_element_type=jnp.float32
    )
    pair_out = (pair_full + tri_gate * update).astype(jnp.bfloat16)
    head_count = qkv_proj.shape[2] // HEAD_DIM
    tile_bias = jnp.einsum(
        "ijc,ch->hij", pair_out, bias_proj, preferred_element_type=jnp.float32
    ).astype(jnp.bfloat16)
    head_bias = lax.all_to_all(tile_bias, "col", split_axis=0, concat_axis=2, tiled=True)
    model_width = noisy.shape[2]
    sample_count, tokens_here = (noisy.shape[0], noisy.shape[1])
    inner_width = qkv_proj.shape[2]
    cvec = normalize(single.astype(jnp.float32)).astype(jnp.bfloat16)
    conditioning = jnp.dot(cvec, ada_proj, preferred_element_type=jnp.float32)
    ada_scale = jax.nn.sigmoid(conditioning[:, :model_width])
    ada_shift = conditioning[:, model_width : 2 * model_width]
    out_gate = jax.nn.sigmoid(conditioning[:, 2 * model_width :])
    normed_in = normalize(noisy.astype(jnp.float32))
    hidden = (ada_scale * normed_in + ada_shift).astype(jnp.bfloat16)
    qkv_all = jnp.einsum(
        "std,dqe->stqe", hidden, qkv_proj, preferred_element_type=jnp.float32
    ).astype(jnp.bfloat16)
    keyval = collect(qkv_all[:, :, 1:], "row", 1)
    key_count = keyval.shape[1]
    queries = qkv_all[:, :, 0].reshape(sample_count, tokens_here, head_count, HEAD_DIM)
    key_rows = keyval[:, :, 0].reshape(sample_count, key_count, head_count, HEAD_DIM)
    value_rows = keyval[:, :, 1].reshape(sample_count, key_count, head_count, HEAD_DIM)
    score_scale = 1.0 / HEAD_DIM**0.5
    key_ok = token_mask > 0
    scores = (
        jnp.einsum("sihd,sjhd->shij", queries, key_rows, preferred_element_type=jnp.float32)
        * score_scale
    )
    scores = scores + head_bias.astype(jnp.float32)[None]
    scores = jnp.where(key_ok[None, None, None, :], scores, -1000000000.0)
    probs = jax.nn.softmax(scores, axis=-1)
    probs_b = probs.astype(jnp.bfloat16)
    attended = jnp.einsum(
        "shij,sjhd->sihd", probs_b, value_rows, preferred_element_type=jnp.float32
    ).astype(jnp.bfloat16)
    attended = attended.reshape(sample_count, tokens_here, inner_width)
    mixed_part = jnp.einsum("ste,ed->std", attended, out_proj, preferred_element_type=jnp.float32)
    mixed = sent_and_summed(mixed_part, "col", 2)
    feature_block = mixed.shape[2]
    feat_at = lax.axis_index("col") * feature_block
    gate_block = lax.dynamic_slice_in_dim(out_gate, feat_at, feature_block, 1)
    noisy_block = lax.dynamic_slice_in_dim(noisy, feat_at, feature_block, 2)
    block_out = (noisy_block.astype(jnp.float32) + gate_block * mixed).astype(jnp.bfloat16)
    grad_in = cotangent.astype(jnp.float32)
    d_mixed = (grad_in * gate_block).astype(jnp.bfloat16)
    d_gate = jnp.sum(grad_in * mixed, 0) * gate_block * (1.0 - gate_block)
    d_att = jnp.einsum(
        "std,ed->ste", collect(d_mixed, "col", 2), out_proj, preferred_element_type=jnp.float32
    )
    d_att = d_att.astype(jnp.bfloat16).reshape(sample_count, tokens_here, head_count, HEAD_DIM)
    d_probs = jnp.einsum("sihd,sjhd->shij", d_att, value_rows, preferred_element_type=jnp.float32)
    d_scores = probs * (d_probs - jnp.sum(probs * d_probs, -1, keepdims=True))
    d_scaled = (d_scores * score_scale).astype(jnp.bfloat16)
    d_query = jnp.einsum(
        "shij,sjhd->sihd", d_scaled, key_rows, preferred_element_type=jnp.float32
    ).astype(jnp.bfloat16)
    d_keys = jnp.einsum("shij,sihd->sjhd", d_scaled, queries, preferred_element_type=jnp.float32)
    d_values = jnp.einsum("shij,sihd->sjhd", probs_b, d_att, preferred_element_type=jnp.float32)
    d_keyval = jnp.stack(
        [
            d_keys.reshape(sample_count, key_count, inner_width),
            d_values.reshape(sample_count, key_count, inner_width),
        ],
        2,
    )
    d_keyval = sent_and_summed(d_keyval, "row", 1).astype(jnp.bfloat16)
    d_qkv = jnp.concatenate([d_query, d_keyval], 2)
    d_hidden = jnp.einsum("stqe,dqe->std", d_qkv, qkv_proj, preferred_element_type=jnp.float32)
    d_scale = jnp.sum(d_hidden * normed_in, 0)
    d_shift = jnp.sum(d_hidden, 0)
    w_ada = ada_proj.astype(jnp.float32)
    w_gate = lax.dynamic_slice_in_dim(w_ada, 2 * model_width + feat_at, feature_block, 1)
    d_cvec = jnp.dot(
        d_scale * ada_scale * (1.0 - ada_scale), w_ada[:, :model_width].T, precision=HIGHEST
    )
    d_cvec = d_cvec + jnp.dot(d_shift, w_ada[:, model_width : 2 * model_width].T, precision=HIGHEST)
    d_cvec = d_cvec + jnp.dot(d_gate, w_gate.T, precision=HIGHEST)
    d_cvec = gathered_total(d_cvec, ("col", "samp"))
    grad_single = normalize_grad(single.astype(jnp.float32), d_cvec)
    d_bias = jnp.sum(d_scores, 0)
    d_bias = taken_together(d_bias, "samp")
    d_tile = lax.all_to_all(d_bias, "col", split_axis=2, concat_axis=0, tiled=True)
    grad_pair = jnp.einsum("hij,ch->ijc", d_tile, bias_proj.astype(jnp.float32), precision=HIGHEST)
    return (pair_out, block_out, grad_pair, grad_single)


def solution(mesh):
    return jax.shard_map(
        on_device,
        mesh=mesh,
        in_specs=(
            P("row", "col", None),
            P(),
            P(),
            P(),
            P(),
            P(),
            P(),
            P(),
            P("row", None),
            P(),
            P("samp", "row", None),
            P(None, None, "col"),
            P("col", None),
            P("samp", "row", "col"),
        ),
        out_specs=(
            P("row", "col", None),
            P("samp", "row", "col"),
            P("row", "col", None),
            P("row", None),
        ),
        check_vma=False,
    )
```

profile of v0, /device:TPU:8, one launch (start us, length us, event | category | flops | bytes accessed | tf_op | source)
XLA Modules:
  0.0 503.9 jit_solution(2397835421734303942)
XLA Ops:
  19.5 55.8 %all-gather.4.cloned.1.call-done = bf16[512,32,128]{2,1,0:T(8,128)(2,1)} async-done(((bf16[64,32,128]{2,1,0:T(8,128)(2,1)}), bf16[512,32,128]{2,1,0:T(8,128)(2,1)}) %all-gather.4.cloned.1.call-update) | async-done | bytes 4194320 | tf_op jit(solution)/shard_map/all_gather | solution.py:126
  75.3 8.6 %copy.133 = bf16[512,32,128]{0,1,2:T(8,128)(2,1)} copy(bf16[512,32,128]{2,1,0:T(8,128)(2,1)} %all-gather.4.cloned.1.call-done) | data formatting | bytes 8388608 | tf_op jit(solution)/shard_map/all_gather | solution.py:126
  83.9 10.3 %convolution_bitcast_fusion = f32[512,64,128]{0,1,2:T(8,128)} fusion(bf16[64,32,128]{0,1,2:T(8,128)(2,1)S(1)} %copy.132, bf16[512,32,128]{0,1,2:T(8,128)(2,1)} %copy.133), kind=kOutput, calls=%fused_computation.2 | convolution fusion | flops 268435456 | bytes 21495808 | tf_op jit(solution)/shard_map/jkc,ikc->jic/dot_general | solution.py:129
  94.2 16.8 %copy.134 = f32[512,64,128]{2,1,0:T(8,128)} copy(f32[512,64,128]{0,1,2:T(8,128)} %convolution_bitcast_fusion) | data formatting | bytes 33554432 | tf_op jit(solution)/shard_map/jkc,ikc->jic/transpose | solution.py:129
  120.0 4.4 all-to-all-start
  124.6 20.7 %all-to-all-done = bf16[8,2,24576]{2,1,0:T(2,128)(2,1)} async-done(((bf16[8,2,24576]{2,1,0:T(2,128)(2,1)}), bf16[8,2,24576]{2,1,0:T(2,128)(2,1)}, u32[]{:S(2)}, u32[]{:S(2)}) %all-to-all-start) | async-done | bytes 786464 | tf_op jit(solution)/shard_map/all_to_all | solution.py:22
  147.6 77.5 %reduce-scatter.2.cloned.1.call-done = f32[32,64,128]{2,1,0:T(8,128)} async-done(((f32[512,64,128]{2,1,0:T(8,128)}), f32[32,64,128]{2,1,0:T(8,128)}) %reduce-scatter.2.cloned.1.call-update) | async-done | bytes 1048592 | tf_op jit(solution)/shard_map/reduce_scatter | solution.py:128
  232.6 5.8 %all-to-all-start.1 = ((bf16[16,2,1024]{2,1,0:T(2,128)(2,1)}), bf16[16,2,1024]{2,1,0:T(2,128)(2,1)S(1)}, u32[]{:S(2)}, u32[]{:S(2)}) async-start(bf16[16,2,1024]{2,1,0:T(2,128)(2,1)} %reshape.269), calls=%async_computation.2 | async-start | bytes 131072 | tf_op jit(solution)/shard_map/all_to_all | solution.py:145
  240.5 4.1 all-to-all-done.1
  252.1 2.9 reshape.271
  255.0 5.3 %all-to-all-start.2 = ((f32[16,1,24576]{2,1,0:T(1,128)}), f32[16,1,24576]{2,1,0:T(1,128)S(1)}, u32[]{:S(2)}, u32[]{:S(2)}) async-start(f32[16,1,24576]{2,1,0:T(1,128)} %reshape.271), calls=%async_computation.3 | async-start | bytes 3145728 | tf_op jit(solution)/shard_map/all_to_all | solution.py:37
  263.1 16.8 %all-to-all-done.2 = f32[16,1,24576]{2,1,0:T(1,128)S(1)} async-done(((f32[16,1,24576]{2,1,0:T(1,128)}), f32[16,1,24576]{2,1,0:T(1,128)S(1)}, u32[]{:S(2)}, u32[]{:S(2)}) %all-to-all-start.2) | async-done | bytes 1572896 | tf_op jit(solution)/shard_map/all_to_all | solution.py:37
  280.5 6.2 %reduce.12 = f32[16,24576]{1,0:T(8,128)} reduce(f32[16,1,24576]{2,1,0:T(1,128)S(1)} %all-to-all-done.2, f32[]{:T(128)} %broadcast.247), dimensions={1}, to_apply=%all_to_all.37.reduce_sub_computation | reduce | bytes 3145732 | tf_op jit(solution)/shard_map/all_to_all | solution.py:37
  292.8 17.0 %all_to_all.52 = bf16[16,2,12288]{2,1,0:T(2,128)(2,1)S(1)} all-to-all(bf16[16,2,12288]{2,1,0:T(2,128)(2,1)S(1)} %reshape.273), channel_id=1, replica_groups=mesh['row'=8,'col'=16,'samp'=2] {'col'}, dimensions={0} | all-to-all | bytes 1572864 | tf_op jit(solution)/shard_map/all_to_all | solution.py:22
  312.1 3.5 copy.144
  321.0 4.4 convolution_bitcast_fusion.3
  332.6 4.8 reshape.277
  337.4 4.9 all-to-all-start.6
  342.7 5.4 %fusion.20 = bf16[8,64,1,48]{1,3,2,0:T(8,128)(2,1)} fusion(bf16[8,512,2,48]{1,3,0,2:T(8,128)(2,1)S(1)} %copy-done.8, f32[8,64,512]{2,1,0:T(8,128)} %copy-done.11, f32[8,64,512]{2,1,0:T(8,128)} %copy-done.13, f32[8,64]{1,0:T(8,128)S(1)} %copy-done.33), kind=kOutput, calls=%fused_computation.37 | convolution fusion | flops 27026432 | bytes 4644864 | tf_op jit(solution)/shard_map/shij,sjhd->sihd/dot_general | solution.py:195
  348.2 32.0 %all-to-all-done.6 = f32[8,1,49152]{2,1,0:T(1,128)S(1)} async-done(((f32[8,1,49152]{2,1,0:T(1,128)}), f32[8,1,49152]{2,1,0:T(1,128)S(1)}, u32[]{:S(2)}, u32[]{:S(2)}) %all-to-all-start.6) | async-done | bytes 1572896 | tf_op jit(solution)/shard_map/all_to_all | solution.py:37
  380.1 6.3 %reduce.15 = f32[8,49152]{1,0:T(8,128)} reduce(f32[8,1,49152]{2,1,0:T(1,128)S(1)} %all-to-all-done.6, f32[]{:T(128)} %broadcast.247), dimensions={1}, to_apply=%all_to_all.44.reduce_sub_computation | reduce | bytes 3145732 | tf_op jit(solution)/shard_map/all_to_all | solution.py:37
  397.8 14.6 %all_to_all.53 = f32[2,1,64,512]{3,2,1,0:T(8,128)S(1)} all-to-all(f32[2,1,64,512]{3,2,1,0:T(8,128)S(1)} %broadcast_in_dim.23), channel_id=1, replica_groups=mesh['row'=8,'col'=16,'samp'=2] {'samp'}, dimensions={0} | all-to-all | bytes 524288 | tf_op jit(solution)/shard_map/all_to_all | solution.py:22
  414.1 12.9 %all_to_all.54 = f32[16,1,2048]{2,1,0:T(1,128)S(1)} all-to-all(f32[16,1,2048]{2,1,0:T(1,128)S(1)} %reshape.275), channel_id=1, replica_groups=mesh['row'=8,'col'=16,'samp'=2] {'col'}, dimensions={0} | all-to-all | bytes 262144 | tf_op jit(solution)/shard_map/all_to_all | solution.py:223
  430.6 62.2 %all-gather.6.cloned.1.call-done = f32[2048,384]{1,0:T(8,128)} async-done(((f32[64,384]{1,0:T(8,128)}), f32[2048,384]{1,0:T(8,128)}) %all-gather.6.cloned.1.call-update) | async-done | bytes 3145744 | tf_op jit(solution)/shard_map/all_gather | solution.py:42
  (176 shorter events, 85.6 us)
Async XLA Ops:
  7.2 109.1 %copy-start = (bf16[768,3,48]{0,2,1:T(8,128)(2,1)S(1)}, bf16[768,3,48]{0,2,1:T(8,128)(2,1)}, u32[]{:S(2)}) copy-start(bf16[768,3,48]{0,2,1:T(8,128)(2,1)} %param.25) | copy-start | bytes 663556
  7.2 6.9 %copy-start.19 = (bf16[128,640]{1,0:T(8,128)(2,1)S(1)}, bf16[128,640]{1,0:T(8,128)(2,1)}, u32[]{:S(2)}) copy-start(bf16[128,640]{1,0:T(8,128)(2,1)} %param.19) | copy-start | bytes 491524
  7.2 68.1 %all-gather.4.cloned.1.call-start = ((), (), s32[]{:S(2)}) async-start(), calls=%async_computation.8 | async-start | bytes 4718592 | tf_op jit(solution)/shard_map/all_gather | solution.py:126
  15.1 2.6 copy-start.1
  17.7 207.4 %reduce-scatter.2.cloned.1.call-start = ((), (), s32[]{:S(2)}) async-start(), calls=%async_computation.9 | async-start | bytes 17825792 | tf_op jit(solution)/shard_map/reduce_scatter | solution.py:128
  111.9 2.8 copy-start.25
  112.7 3.6 copy-start.28
  112.7 3.6 copy-start.30
  118.0 6.4 %copy-start.17 = (bf16[48,768]{1,0:T(8,128)(2,1)S(1)}, bf16[48,768]{1,0:T(8,128)(2,1)}, u32[]{:S(2)}) copy-start(bf16[48,768]{1,0:T(8,128)(2,1)} %param.26) | copy-start | bytes 221188
  118.0 6.6 %copy-start.27 = (s32[512]{0:T(512)S(1)}, s32[512]{0:T(512)}, u32[]{:S(2)}) copy-start(s32[512]{0:T(512)} %param.17) | copy-start | bytes 6148
  120.0 25.4 %all-to-all-start = ((bf16[8,2,24576]{2,1,0:T(2,128)(2,1)}), bf16[8,2,24576]{2,1,0:T(2,128)(2,1)}, u32[]{:S(2)}, u32[]{:S(2)}) async-start(bf16[8,2,24576]{2,1,0:T(2,128)(2,1)} %reshape.267), calls=%async_computation.1 | async-start | bytes 1572864 | tf_op jit(solution)/shard_map/all_to_all | solution.py:22
  228.1 2.7 copy-start.24
  232.6 12.0 %all-to-all-start.1 = ((bf16[16,2,1024]{2,1,0:T(2,128)(2,1)}), bf16[16,2,1024]{2,1,0:T(2,128)(2,1)S(1)}, u32[]{:S(2)}, u32[]{:S(2)}) async-start(bf16[16,2,1024]{2,1,0:T(2,128)(2,1)} %reshape.269), calls=%async_computation.2 | async-start | bytes 131072 | tf_op jit(solution)/shard_map/all_to_all | solution.py:145
  240.4 5.9 %copy-start.7 = (bf16[8,512,2,48]{1,3,0,2:T(8,128)(2,1)}, bf16[8,512,2,48]{1,3,0,2:T(8,128)(2,1)S(1)}, u32[]{:S(2)}) copy-start(bf16[8,512,2,48]{1,3,0,2:T(8,128)(2,1)S(1)} %reshape.246) | copy-start | bytes 2359300
  255.0 24.9 %all-to-all-start.2 = ((f32[16,1,24576]{2,1,0:T(1,128)}), f32[16,1,24576]{2,1,0:T(1,128)S(1)}, u32[]{:S(2)}, u32[]{:S(2)}) async-start(f32[16,1,24576]{2,1,0:T(1,128)} %reshape.271), calls=%async_computation.3 | async-start | bytes 3145728 | tf_op jit(solution)/shard_map/all_to_all | solution.py:37
  315.6 2.5 copy-start.18
  337.4 5.2 %copy-start.21 = (f32[64,48]{0,1:T(8,128)S(1)}, f32[64,48]{0,1:T(8,128)}, u32[]{:S(2)}) copy-start(f32[64,48]{0,1:T(8,128)} %get-tuple-element.11) | copy-start | bytes 36868
  337.4 5.3 %copy-start.8 = (bf16[8,512,2,48]{1,3,0,2:T(8,128)(2,1)S(1)}, bf16[8,512,2,48]{1,3,0,2:T(8,128)(2,1)}, u32[]{:S(2)}) copy-start(bf16[8,512,2,48]{1,3,0,2:T(8,128)(2,1)} %copy-done.7) | copy-start | bytes 2359300
  337.4 42.7 %all-to-all-start.6 = ((f32[8,1,49152]{2,1,0:T(1,128)}), f32[8,1,49152]{2,1,0:T(1,128)S(1)}, u32[]{:S(2)}, u32[]{:S(2)}) async-start(f32[8,1,49152]{2,1,0:T(1,128)} %reshape.277), calls=%async_computation.7 | async-start | bytes 3145728 | tf_op jit(solution)/shard_map/all_to_all | solution.py:37
  342.3 150.5 %all-gather.6.cloned.1.call-start = ((), (), s32[]{:S(2)}) async-start(), calls=%async_computation.10 | async-start | bytes 3244032 | tf_op jit(solution)/shard_map/all_gather | solution.py:42
  390.8 4.2 copy-start.12
  390.8 4.2 copy-start.15
  492.8 2.2 copy-start.29
  492.8 2.8 copy-start.2
  (19 other events, 22.7 us)
Sparse Core Ops, SparseCore 0:
  17.8 57.3 all-gather.3
  111.1 113.9 reduce-scatter.1
  395.1 97.6 all-gather.5
where the time goes:
time: 513 us; the launch traced here: 504 us
  waiting for transfers between devices  269 us (52%)
  local copies, waits for them, and re-layouts  80 us (16%)
  blocking collectives  44.5 us (9%)
  matrix products  40.1 us (8%)
  other arithmetic  34.2 us (7%)
  starting transfers between devices  20.8 us (4%)
  between operations  15.1 us (3%)
    reduce_scatter x1, waiting for transfers between devices, on_device(): lax.psum_scatter(jnp.einsum('jkc,ikc->jic', right_all, left_side, preferr...  77.5 us
    all_gather x1, waiting for transfers between devices, gathered_total(): return lax.all_gather(array, axis).sum(0)  62.2 us
    all_gather x1, waiting for transfers between devices, on_device(): right_all = lax.all_gather(right_side, 'row', axis=0, tiled=True)  55.8 us
    all_to_all x2, waiting for transfers between devices, sent_and_summed(): blocks = lax.all_to_all(split_up(array, dim, size), axis, 0, 0, tiled=True)  48.7 us
    all_to_all x2, blocking collectives, sent_to_all(): return lax.all_to_all(copies, axis, split_axis=0, concat_axis=0, tiled=True)  31.6 us
    unnamed x87, local copies, waits for them, and re-layouts  29.6 us
    all_to_all x1, waiting for transfers between devices, sent_to_all(): return lax.all_to_all(copies, axis, split_axis=0, concat_axis=0, tiled=True)  20.7 us
    transpose x1, local copies, waits for them, and re-layouts, on_device(): jnp.einsum('jkc,ikc->jic', right_all, left_side, preferred_element_type=j...  16.8 us
  transfers between devices with their start and end apart: 7, of which 7 were waited for; matrix products, arithmetic and copies ran while one was open for 6% of the time, Pallas kernels for 0%

commit v1 on v0

v1 whole, which is shorter than its diff:
```python
import jax
import jax.numpy as jnp
from jax import lax
from jax.experimental import pallas as pl
from jax.experimental.pallas import tpu as pltpu
from jax.sharding import PartitionSpec as P

HEAD_DIM = 48
REL_BINS = 66
EPSILON = 1e-05
HIGHEST = lax.Precision.HIGHEST
MESH = pl.DeviceIdType.MESH
F32 = jnp.float32
BF16 = jnp.bfloat16
NCOL = 16
NROW = 8


def dg(a, b, ca, cb, **kw):
    return lax.dot_general(a, b, (((ca,), (cb,)), ((), ())), preferred_element_type=F32, **kw)


def place():
    return lax.axis_index("row"), lax.axis_index("col"), lax.axis_index("samp")


def rmod(a, n):
    return lax.rem(a, n)


def ring_shift(oz, dest_core):
    if oz == 2:
        return 2 + 4 * dest_core
    return (0, 1, None, 7)[oz]


def row_dest(oz, cx):
    row, col, samp = place()
    z, core = samp * 4 + row // 2, rmod(row, 2)
    to_core = rmod(core + cx, 2)
    to_z = rmod(z + ring_shift(oz, to_core), 8)
    return rmod(to_z, 4) * 2 + to_core, col, to_z // 4


def row_source(oz, cx):
    row, col, samp = place()
    z, core = samp * 4 + row // 2, rmod(row, 2)
    from_core = rmod(core + cx, 2)
    from_z = rmod(z + 8 - ring_shift(oz, core), 8)
    return rmod(from_z, 4) * 2 + from_core, col, from_z // 4


ROW_IDS = [(oz, cx) for oz in range(4) for cx in range(2) if (oz, cx) != (0, 0)]


def remote(src, dst, ssem, rsem, to):
    return pltpu.make_async_remote_copy(
        src_ref=src, dst_ref=dst, send_sem=ssem, recv_sem=rsem, device_id=to, device_id_type=MESH
    )


def col_start(src_of, slot_of, ssem, rsem):
    row, col, samp = place()

    def one(o, _):
        to = rmod(col + o, NCOL)
        remote(src_of(to), slot_of(col), ssem.at[o], rsem.at[o], (row, to, samp)).start()
        return 0

    lax.fori_loop(1, NCOL, one, 0)


def col_wait(src_of, slot_of, ssem, rsem, recv=True, send=True):
    row, col, samp = place()

    def one(o, _):
        to = rmod(col + o, NCOL)
        came = rmod(col + NCOL - o, NCOL)
        if recv:
            remote(src_of(to), slot_of(came), ssem.at[o], rsem.at[o], (row, to, samp)).wait_recv()
        if send:
            remote(src_of(to), slot_of(came), ssem.at[o], rsem.at[o], (row, to, samp)).wait_send()
        return 0

    lax.fori_loop(1, NCOL, one, 0)


def row_start(src_of, slot_of, ssem, rsem):
    row = lax.axis_index("row")
    for oz, cx in ROW_IDS:
        to = row_dest(oz, cx)
        i = oz * 2 + cx
        remote(src_of(to[0]), slot_of(row), ssem.at[i], rsem.at[i], to).start()


def row_wait(src_of, slot_of, ssem, rsem, recv=True, send=True):
    for oz, cx in ROW_IDS:
        to, came = row_dest(oz, cx), row_source(oz, cx)
        i = oz * 2 + cx
        copy = remote(src_of(to[0]), slot_of(came[0]), ssem.at[i], rsem.at[i], to)
        if recv:
            copy.wait_recv()
        if send:
            copy.wait_send()


def signal(sem, to):
    pl.semaphore_signal(sem, inc=1, device_id=to, device_id_type=MESH)


def own_row_ids():
    return [o for o in range(1, 4)]


def pair_kernel(
    pair_ref, resr_ref, chr_ref, resc_ref, chc_ref, maskp_ref, relpos_ref, tri_ref, triout_ref,
    biasp_ref, kv_ref, dmx_ref,
    pairout_ref, bias_ref, kvall_ref, dmxall_ref,
    pf, gate, lrf, lbuf, recv_a, got, rcat, mtmp, tbuf, got_c, got_d, bias_f, bias_b, bias_got,
    sa, ra, sb, rb, sc, rc, sd, rd, se, re, skv, rkv, skf, rkf, sdm, rdm, loc,
):
    row, col, samp = place()
    core = rmod(row, 2)
    zlo = row // 2
    mate = (row + 1 - 2 * core, col, samp)
    barrier = pltpu.get_barrier_semaphore()
    for oz, cx in ROW_IDS:
        signal(barrier, row_source(oz, cx))

    def greet(o, _):
        signal(barrier, (row, rmod(col + o, NCOL), samp))
        return 0

    lax.fori_loop(1, NCOL, greet, 0)
    for o in own_row_ids():
        signal(barrier, (rmod(zlo + o, 4) * 2 + core, col, samp))
    signal(barrier, mate)
    pl.semaphore_wait(barrier, 7 + 15 + 3 + 1)

    kv_own = pltpu.make_async_copy(kv_ref, kvall_ref.at[row], loc.at[0])
    kv_own.start()
    kv_out = []
    for o in own_row_ids():
        to = (rmod(zlo + o, 4) * 2 + core, col, samp)
        kv_out.append(remote(kv_ref, kvall_ref.at[row], skv.at[o], rkv.at[o], to))
        kv_out[-1].start()
    kv_mate = remote(kv_ref, kvall_ref.at[row], skf.at[0], rkf.at[0], mate)
    kv_mate.start()
    dm_own = pltpu.make_async_copy(dmx_ref, dmxall_ref.at[col], loc.at[1])
    dm_own.start()
    dm_src, dm_slot = (lambda to: dmx_ref), (lambda c: dmxall_ref.at[c])

    def load(i, _):
        pf[pl.ds(i * 32, 32), :] = pair_ref[i].astype(F32)
        return 0

    lax.fori_loop(0, 64, load, 0, unroll=4)
    bins = lax.broadcasted_iota(jnp.int32, (64, 128), 1)
    resr, chr_ = resr_ref[...], chr_ref[...]
    relpos = relpos_ref[...]

    def stage1(lo, _):
        parts = []
        for hi in range(2):
            j = lo + 16 * hi
            off = jnp.clip(resr - resc_ref[pl.ds(j, 1), :] + 32, 0, 64)
            bucket = jnp.where(chr_ == chc_ref[pl.ds(j, 1), :], off, REL_BINS - 1)
            onehot = jnp.where(bucket == bins, 1.0, 0.0).astype(BF16)
            parts.append(
                pf[pl.ds(j, 64, stride=32), :] + jnp.dot(onehot, relpos, preferred_element_type=F32)
            )
        full = jnp.concatenate(parts, 0)
        for hi in range(2):
            pf[pl.ds(lo + 16 * hi, 64, stride=32), :] = parts[hi]
        mean = jnp.mean(full, -1, keepdims=True)
        cent = full - mean
        var = jnp.mean(cent * cent, -1, keepdims=True)
        zl = (cent * lax.rsqrt(var + EPSILON)).astype(BF16)
        pt = dg(tri_ref[:, :512], zl, 0, 1)
        mask = maskp_ref[pl.ds(lo, 1), :]
        left = jax.nn.sigmoid(pt[128:256]) * pt[:128] * mask
        right = jax.nn.sigmoid(pt[384:512]) * pt[256:384] * mask
        lrf[pl.ds(lo, 128, stride=16), :] = left
        lrf[pl.ds(2048 + lo, 128, stride=16), :] = right
        gate[lo] = jax.nn.sigmoid(
            jnp.dot(zl, tri_ref[:, 512:], preferred_element_type=F32)
        )
        return 0

    lax.fori_loop(0, 16, stage1, 0, unroll=2)

    def pack(c, _):
        for half in range(2):
            lbuf[half, c] = (
                lrf[pl.ds(half * 2048 + c * 128, 128), :].astype(BF16).reshape(8, 16, 128)
            )
        return 0

    lax.fori_loop(0, 16, pack, 0)

    a_src = [lambda to, h=h: lbuf.at[h, to] for h in range(2)]
    a_slot = [lambda c, h=h: recv_a.at[h, c] for h in range(2)]
    b_src = [lambda r, h=h: recv_a.at[h, :, r] for h in range(2)]
    b_slot = [lambda r, h=h: got.at[h, r] for h in range(2)]
    for h in range(2):
        pltpu.make_async_copy(lbuf.at[h, col], recv_a.at[h, col], loc.at[2 + h]).start()
        col_start(a_src[h], a_slot[h], sa.at[h], ra.at[h])
    col_start(dm_src, dm_slot, sdm, rdm)
    for h in range(2):
        pltpu.make_async_copy(lbuf.at[h, col], recv_a.at[h, col], loc.at[2 + h]).wait()
        col_wait(a_src[h], a_slot[h], sa.at[h], ra.at[h])
        pltpu.make_async_copy(recv_a.at[h, :, row], got.at[h, row], loc.at[4 + h]).start()
        row_start(b_src[h], b_slot[h], sb.at[h], rb.at[h])
    for o in own_row_ids():
        came = rmod(zlo + 4 - o, 4) * 2 + core
        remote(kv_ref, kvall_ref.at[came], skv.at[o], rkv.at[o], mate).wait_recv()
        remote(kvall_ref.at[came], kvall_ref.at[came], skf.at[o], rkf.at[o], mate).start()
    for h in (1, 0):
        pltpu.make_async_copy(recv_a.at[h, :, row], got.at[h, row], loc.at[4 + h]).wait()
        row_wait(b_src[h], b_slot[h], sb.at[h], rb.at[h])

    def turn(r, _):
        rcat[pl.ds(pl.multiple_of(r * 128, 128), 128), :] = (
            got[1, r].reshape(256, 128).astype(F32).T.astype(BF16)
        )
        return 0

    lax.fori_loop(0, 8, turn, 0)
    low = lax.broadcasted_iota(jnp.int32, (16, 128), 1) < 64

    def tri(rp, _):
        rhs = jnp.concatenate(
            [got[0, 2 * rp].reshape(256, 128), got[0, 2 * rp + 1].reshape(256, 128)], 1
        )
        mtmp[...] = jnp.dot(rcat[...], rhs, preferred_element_type=F32)

        def out(rj, _):
            for half in range(2):
                top = mtmp[pl.ds(rj * 128, 64), half * 128 : half * 128 + 128]
                bot = mtmp[pl.ds(rj * 128 + 64, 64), half * 128 : half * 128 + 128]
                for jh in range(2):
                    a = slice(jh * 32, jh * 32 + 16)
                    b = slice(jh * 32 + 16, jh * 32 + 32)
                    t = jnp.where(
                        low,
                        top[a] + pltpu.roll(bot[a], 64, 1),
                        pltpu.roll(top[b], 64, 1) + bot[b],
                    )
                    tbuf[2 * rp + half, 2 * rj + jh] = t.astype(BF16)
            return 0

        lax.fori_loop(0, 8, out, 0, unroll=2)
        return 0

    lax.fori_loop(0, 4, tri, 0)

    c_src, c_slot = (lambda r: tbuf.at[r]), (lambda r: got_c.at[r])
    d_src, d_slot = (lambda c: got_c.at[:, c]), (lambda c: got_d.at[c])
    own_c = pltpu.make_async_copy(tbuf.at[row], got_c.at[row], loc.at[6])
    own_c.start()
    row_start(c_src, c_slot, sc, rc)
    own_c.wait()
    row_wait(c_src, c_slot, sc, rc)
    own_d = pltpu.make_async_copy(got_c.at[:, col], got_d.at[col], loc.at[7])
    own_d.start()
    col_start(d_src, d_slot, sd, rd)
    own_d.wait()
    col_wait(d_src, d_slot, sd, rd)

    def widen(c, _):
        lrf[pl.ds(c * 128, 128), :] = got_d[c].reshape(128, 128).astype(F32)
        return 0

    lax.fori_loop(0, 16, widen, 0)
    triout = triout_ref[...]
    biasp = biasp_ref[...]

    def stage3(lo, _):
        t = lrf[pl.ds(lo, 128, stride=16), :]
        mean = jnp.mean(t, 0, keepdims=True)
        cent = t - mean
        var = jnp.mean(cent * cent, 0, keepdims=True)
        tn = (cent * lax.rsqrt(var + EPSILON)).astype(BF16)
        upd = dg(tn, triout, 0, 0) * gate[lo]
        outs = []
        for hi in range(2):
            at = pl.ds(lo + 16 * hi, 64, stride=32)
            val = (pf[at, :] + upd[hi * 64 : hi * 64 + 64]).astype(BF16)
            pf[at, :] = val.astype(F32)
            outs.append(val)
        bias_f[pl.ds(lo, 16, stride=16), :] = dg(biasp, jnp.concatenate(outs, 0), 0, 1)
        return 0

    lax.fori_loop(0, 16, stage3, 0, unroll=2)
    bias_b[...] = bias_f[...].astype(BF16).reshape(16, 16, 128)
    e_src, e_slot = (lambda c: bias_b.at[c]), (lambda c: bias_got.at[c])
    own_e = pltpu.make_async_copy(bias_b.at[col], bias_got.at[col], loc.at[8])
    own_e.start()
    col_start(e_src, e_slot, se, re)

    def store(i, _):
        pairout_ref[i] = pf[pl.ds(i * 32, 32), :].astype(BF16)
        return 0

    lax.fori_loop(0, 64, store, 0, unroll=4)
    own_e.wait()
    col_wait(e_src, e_slot, se, re)
    bias_ref[...] = bias_got[...].reshape(256, 128)

    kv_own.wait()
    dm_own.wait()
    for copy in kv_out:
        copy.wait_send()
    kv_mate.wait_send()
    mate_core = 1 - core
    for o in range(4):
        came = rmod(zlo + 4 - o, 4) * 2
        remote(kvall_ref.at[came + core], kvall_ref.at[came + mate_core], skf.at[o], rkf.at[o], mate).wait_recv()
        if o > 0:
            remote(kvall_ref.at[came + core], kvall_ref.at[came + core], skf.at[o], rkf.at[o], mate).wait_send()
    col_wait(dm_src, dm_slot, sdm, rdm)


def pair_stage(pair_in, resr, chr_, resc, chc, maskp, relpos, tri_proj, tri_out, bias_proj, kv, dmx):
    vm = pl.BlockSpec(memory_space=pltpu.VMEM)
    hbm = pl.BlockSpec(memory_space=pl.ANY)
    dma = pltpu.SemaphoreType.DMA
    return pl.pallas_call(
        pair_kernel,
        out_shape=(
            jax.ShapeDtypeStruct((64, 32, 128), BF16),
            jax.ShapeDtypeStruct((256, 128), BF16),
            jax.ShapeDtypeStruct((8, *kv.shape), BF16),
            jax.ShapeDtypeStruct((16, *dmx.shape), BF16),
        ),
        in_specs=[vm] * 12,
        out_specs=(vm, vm, hbm, hbm),
        scratch_shapes=[
            pltpu.VMEM((2048, 128), F32),
            pltpu.VMEM((16, 128, 128), F32),
            pltpu.VMEM((4096, 128), F32),
            pltpu.VMEM((2, 16, 8, 16, 128), BF16),
            pltpu.VMEM((2, 16, 8, 16, 128), BF16),
            pltpu.VMEM((2, 8, 16, 16, 128), BF16),
            pltpu.VMEM((1024, 256), BF16),
            pltpu.VMEM((1024, 256), F32),
            pltpu.VMEM((8, 16, 16, 128), BF16),
            pltpu.VMEM((8, 16, 16, 128), BF16),
            pltpu.VMEM((16, 8, 16, 128), BF16),
            pltpu.VMEM((256, 128), F32),
            pltpu.VMEM((16, 16, 128), BF16),
            pltpu.VMEM((16, 16, 128), BF16),
            dma((2, 16)), dma((2, 16)), dma((2, 8)), dma((2, 8)), dma((8,)), dma((8,)),
            dma((16,)), dma((16,)), dma((16,)), dma((16,)), dma((4,)), dma((4,)),
            dma((4,)), dma((4,)), dma((16,)), dma((16,)), dma((9,)),
        ],
        compiler_params=pltpu.CompilerParams(
            collective_id=1, has_side_effects=True, vmem_limit_bytes=48 * 1024 * 1024
        ),
        name="pair_stage",
    )(pair_in, resr, chr_, resc, chc, maskp, relpos, tri_proj, tri_out, bias_proj, kv, dmx)


def both(x, low, first):
    turned = pltpu.roll(x, 64, 1)
    return jnp.where(low, x, turned) if first else jnp.where(low, turned, x)


def attention_kernel(
    qd_ref, kv_ref, dmx_ref, wout_ref, bias_ref, keyok_ref, biasp_ref,
    mixed_ref, dq_ref, dkv_ref, gpair_ref,
    datt, mix_s, mix_r, dkv_s, dkv_r, dbias, db_s, db_r,
    sm, rm, sk, rk, sb, rb, loc, locm, lock,
):
    row, col, samp = place()
    barrier = pltpu.get_barrier_semaphore()

    def greet(o, _):
        signal(barrier, (row, rmod(col + o, NCOL), samp))
        return 0

    def greet_row(o, _):
        signal(barrier, (rmod(row + o, NROW), col, samp))
        return 0

    def greet_far(o, _):
        signal(barrier, (row, rmod(col + o, NCOL), 1 - samp))
        return 0

    lax.fori_loop(1, NCOL, greet, 0)
    lax.fori_loop(1, NROW, greet_row, 0)
    lax.fori_loop(0, NCOL, greet_far, 0)

    low = lax.broadcasted_iota(jnp.int32, (64, 128), 1) < 64
    diag = (
        (lax.broadcasted_iota(jnp.int32, (128, 128), 0) < 64)
        == (lax.broadcasted_iota(jnp.int32, (128, 128), 1) < 64)
    )

    def blockdiag(x):
        return jnp.where(diag, jnp.concatenate([x, x], 0), 0.0).astype(BF16)

    datt[...] = jnp.zeros_like(datt)

    def d_att(f, _):
        w = blockdiag(wout_ref[f].astype(F32))
        datt[...] += dg(dmx_ref[f], w, 1, 1)
        return 0

    lax.fori_loop(0, NCOL, d_att, 0)
    datt[...] = datt[...].astype(BF16).astype(F32)
    dbias[...] = jnp.zeros_like(dbias)
    scale = 1.0 / HEAD_DIM**0.5

    def mix_src(s4):
        return lambda f: mix_s.at[f, s4]

    def mix_slot(s4):
        return lambda h: mix_r.at[h, s4]

    def row_copy(s4, o):
        to, came = rmod(row + o, NROW), rmod(row + NROW - o, NROW)
        return to, came

    def pair_of_samples(s4, _):
        x = datt[pl.ds(pl.multiple_of(s4 * 64, 64), 64), :]
        folded = []
        for sh in range(2):
            s = s4 + 4 * sh
            kp = jnp.concatenate([kv_ref[r, 0, s] for r in range(8)], 0)
            vp = jnp.concatenate([kv_ref[r, 1, s] for r in range(8)], 0)
            qq = blockdiag(qd_ref[s].astype(F32))
            dd = blockdiag(both(x, low, sh == 0))
            sc = dg(kp, qq, 1, 1) * scale + bias_ref[...].astype(F32)
            sc = jnp.where(keyok_ref[...] > 0, sc, -1000000000.0)
            top = jnp.max(sc, 0, keepdims=True)
            top = jnp.maximum(top, pltpu.roll(top, 64, 1))
            ex = jnp.exp(sc - top)
            tot = jnp.sum(ex, 0, keepdims=True)
            tot = tot + pltpu.roll(tot, 64, 1)
            probs = ex / tot
            pb = probs.astype(BF16)
            m = dg(pb, vp, 0, 0)
            folded.append((m[:64], m[64:]))
            dp = dg(vp, dd, 1, 1)
            dot = jnp.sum(probs * dp, 0, keepdims=True)
            dot = dot + pltpu.roll(dot, 64, 1)
            ds = probs * (dp - dot)
            dbias[...] += ds
            dsb = (ds * scale).astype(BF16)
            mq = dg(dsb, kp, 0, 0)
            a, b = mq[:64], mq[64:]
            dq_ref[s] = (a + pltpu.roll(b, 64, 1)).astype(BF16)
            dk = jnp.dot(dsb, qq, preferred_element_type=F32).astype(BF16)
            dv = jnp.dot(pb, dd, preferred_element_type=F32).astype(BF16)
            for r in range(8):
                dkv_s[r, s4, sh] = dk[r * 32 : r * 32 + 32]
                dkv_s[r, s4, 2 + sh] = dv[r * 32 : r * 32 + 32]
        (a0, b0), (a1, b1) = folded
        att = jnp.where(low, a0 + pltpu.roll(b0, 64, 1), pltpu.roll(a1, 64, 1) + b1).astype(BF16)
        for f in range(NCOL):
            w = blockdiag(wout_ref[f].astype(F32))
            mix_s[f, s4] = jnp.dot(att, w, preferred_element_type=F32).astype(BF16)

        @pl.when(s4 == 0)
        def _():
            pl.semaphore_wait(barrier, 15 + 7 + 16)

        pltpu.make_async_copy(mix_s.at[col, s4], mix_r.at[col, s4], locm.at[s4]).start()
        pltpu.make_async_copy(dkv_s.at[row, s4], dkv_r.at[row, s4], lock.at[s4]).start()
        col_start(mix_src(s4), mix_slot(s4), sm.at[s4], rm.at[s4])

        def one(o, _):
            to, _came = row_copy(s4, o)
            remote(
                dkv_s.at[to, s4], dkv_r.at[row, s4], sk.at[s4, o], rk.at[s4, o], (to, col, samp)
            ).start()
            return 0

        lax.fori_loop(1, NROW, one, 0)
        return 0

    lax.fori_loop(0, 4, pair_of_samples, 0)

    db_s[...] = dbias[...].reshape(16, 16, 128)
    own_b = pltpu.make_async_copy(db_s.at[col], db_r.at[samp, col], loc.at[0])
    own_b.start()

    def db_send(o, _):
        to = rmod(col + o, NCOL)
        remote(db_s.at[to], db_r.at[samp, col], sb.at[1, o], rb.at[1, o], (row, to, 1 - samp)).start()
        return 0

    lax.fori_loop(0, NCOL, db_send, 0)
    near_src, near_slot = (lambda c: db_s.at[c]), (lambda c: db_r.at[samp, c])
    col_start(near_src, near_slot, sb.at[0], rb.at[0])

    for s4 in range(4):
        pltpu.make_async_copy(mix_s.at[col, s4], mix_r.at[col, s4], locm.at[s4]).wait()
        col_wait(mix_src(s4), mix_slot(s4), sm.at[s4], rm.at[s4])
        total = mix_r[0, s4].astype(F32)
        for h in range(1, NCOL):
            total = total + mix_r[h, s4].astype(F32)
        mixed_ref[s4] = total

    own_b.wait()
    col_wait(near_src, near_slot, sb.at[0], rb.at[0])

    def db_wait(o, _):
        to, came = rmod(col + o, NCOL), rmod(col + NCOL - o, NCOL)
        copy = remote(
            db_s.at[to], db_r.at[1 - samp, came], sb.at[1, o], rb.at[1, o], (row, to, 1 - samp)
        )
        copy.wait_recv()
        copy.wait_send()
        return 0

    lax.fori_loop(0, NCOL, db_wait, 0)
    dbias[...] = (db_r[0] + db_r[1]).reshape(256, 128)
    biasp = jnp.concatenate([biasp_ref[...]] * 3, 1)

    def grad(lo, _):
        d = dbias[pl.ds(lo, 16, stride=16), :]
        d1 = d.astype(BF16)
        rest = d - d1.astype(F32)
        d2 = rest.astype(BF16)
        d3 = (rest - d2.astype(F32)).astype(BF16)
        g = dg(jnp.concatenate([d1, d2, d3], 0), biasp, 0, 1)
        for hi in range(2):
            gpair_ref[pl.ds(lo + 16 * hi, 64, stride=32), :] = g[hi * 64 : hi * 64 + 64]
        return 0

    lax.fori_loop(0, 16, grad, 0, unroll=2)

    for s4 in range(4):
        pltpu.make_async_copy(dkv_s.at[row, s4], dkv_r.at[row, s4], lock.at[s4]).wait()

        def done(o, _):
            to, came = row_copy(s4, o)
            copy = remote(
                dkv_s.at[to, s4], dkv_r.at[came, s4], sk.at[s4, o], rk.at[s4, o], (to, col, samp)
            )
            copy.wait_recv()
            copy.wait_send()
            return 0

        lax.fori_loop(1, NROW, done, 0)
        total = dkv_r[0, s4].astype(F32)
        for r in range(1, NROW):
            total = total + dkv_r[r, s4].astype(F32)
        dkv_ref[s4] = total.astype(BF16)


def attention_stage(qd, kv_all, dmx_all, wout, bias, keyok, bias_proj):
    vm = pl.BlockSpec(memory_space=pltpu.VMEM)
    dma = pltpu.SemaphoreType.DMA
    return pl.pallas_call(
        attention_kernel,
        out_shape=(
            jax.ShapeDtypeStruct((4, 64, 128), F32),
            jax.ShapeDtypeStruct((8, 64, 128), BF16),
            jax.ShapeDtypeStruct((4, 4, 32, 128), BF16),
            jax.ShapeDtypeStruct((2048, 128), F32),
        ),
        in_specs=[vm] * 7,
        out_specs=(vm,) * 4,
        scratch_shapes=[
            pltpu.VMEM((256, 128), F32),
            pltpu.VMEM((16, 4, 64, 128), BF16),
            pltpu.VMEM((16, 4, 64, 128), BF16),
            pltpu.VMEM((8, 4, 4, 32, 128), BF16),
            pltpu.VMEM((8, 4, 4, 32, 128), BF16),
            pltpu.VMEM((256, 128), F32),
            pltpu.VMEM((16, 16, 128), F32),
            pltpu.VMEM((2, 16, 16, 128), F32),
            dma((4, 16)), dma((4, 16)), dma((4, 8)), dma((4, 8)), dma((2, 16)), dma((2, 16)),
            dma((1,)), dma((4,)), dma((4,)),
        ],
        compiler_params=pltpu.CompilerParams(
            collective_id=2, has_side_effects=True, vmem_limit_bytes=48 * 1024 * 1024
        ),
        name="attention_stage",
    )(qd, kv_all, dmx_all, wout, bias, keyok, bias_proj)


def total_kernel(x_ref, out_ref, parts, mine, s1, r1, s2, r2, loc):
    row, col, samp = place()
    me = samp * 16 + col
    barrier = pltpu.get_barrier_semaphore()

    def at(i):
        return row, rmod(i, 16), i // 16

    def greet(o, _):
        signal(barrier, at(rmod(me + o, 32)))
        return 0

    lax.fori_loop(1, 32, greet, 0)
    pl.semaphore_wait(barrier, 31)

    def send1(o, _):
        to = rmod(me + o, 32)
        remote(x_ref.at[to], parts.at[me], s1.at[o], r1.at[o], at(to)).start()
        return 0

    own = pltpu.make_async_copy(x_ref.at[me], parts.at[me], loc.at[0])
    own.start()
    lax.fori_loop(1, 32, send1, 0)
    own.wait()

    def wait1(o, _):
        to, came = rmod(me + o, 32), rmod(me + 32 - o, 32)
        copy = remote(x_ref.at[to], parts.at[came], s1.at[o], r1.at[o], at(to))
        copy.wait_recv()
        copy.wait_send()
        return 0

    lax.fori_loop(1, 32, wait1, 0)
    total = parts[0]
    for i in range(1, 32):
        total = total + parts[i]
    mine[...] = total

    def send2(o, _):
        to = rmod(me + o, 32)
        remote(mine, out_ref.at[me], s2.at[o], r2.at[o], at(to)).start()
        return 0

    lax.fori_loop(1, 32, send2, 0)
    own = pltpu.make_async_copy(mine, out_ref.at[me], loc.at[0])
    own.start()
    own.wait()

    def wait2(o, _):
        to, came = rmod(me + o, 32), rmod(me + 32 - o, 32)
        copy = remote(mine, out_ref.at[came], s2.at[o], r2.at[o], at(to))
        copy.wait_recv()
        copy.wait_send()
        return 0

    lax.fori_loop(1, 32, wait2, 0)


def total_stage(x):
    vm = pl.BlockSpec(memory_space=pltpu.VMEM)
    dma = pltpu.SemaphoreType.DMA
    return pl.pallas_call(
        total_kernel,
        out_shape=jax.ShapeDtypeStruct((32, 8, 128), F32),
        in_specs=[vm],
        out_specs=vm,
        scratch_shapes=[
            pltpu.VMEM((32, 8, 128), F32), pltpu.VMEM((8, 128), F32),
            dma((32,)), dma((32,)), dma((32,)), dma((32,)), dma((1,)),
        ],
        compiler_params=pltpu.CompilerParams(collective_id=3, has_side_effects=True),
        name="total_stage",
    )(x)


def normalize(values_in):
    average = jnp.mean(values_in, -1, keepdims=True)
    centered = values_in - average
    variance = jnp.mean(centered * centered, -1, keepdims=True)
    return centered * lax.rsqrt(variance + EPSILON)


def normalize_grad(values_in, upstream):
    average = jnp.mean(values_in, -1, keepdims=True)
    centered = values_in - average
    variance = jnp.mean(centered * centered, -1, keepdims=True)
    inv_std = lax.rsqrt(variance + EPSILON)
    unit_rows = centered * inv_std
    return inv_std * (
        upstream
        - jnp.mean(upstream, -1, keepdims=True)
        - unit_rows * jnp.mean(upstream * unit_rows, -1, keepdims=True)
    )


def pad_last(x, size):
    return jnp.pad(x, [(0, 0)] * (x.ndim - 1) + [(0, size - x.shape[-1])])


def lanes(x):
    x = pad_last(x, 64).reshape(2, 4, 64, 64)
    return jnp.concatenate([x[0], x[1]], -1)


def unlanes(x):
    x = x.reshape(4, 64, 128)
    return jnp.concatenate([x[:, :, :48], x[:, :, 64:112]], 0)


def on_device(
    pair_in, residue_index, chain_index, token_mask, relpos_weight, tri_proj, tri_out, bias_proj,
    single, ada_proj, noisy, qkv_proj, out_proj, cotangent,
):
    row, col = lax.axis_index("row"), lax.axis_index("col")
    row_at, col_at = row * 64, col * 32

    def rows_of(x):
        return lax.dynamic_slice_in_dim(x, row_at, 64)

    def cols_of(x):
        return lax.dynamic_slice_in_dim(x, col_at, 32)

    mask_f = token_mask.astype(F32)
    maskp = (
        jnp.swapaxes(cols_of(mask_f).reshape(2, 16), 0, 1)[:, :, None] * rows_of(mask_f)[None, None]
    ).reshape(16, 128)
    resr = jnp.broadcast_to(rows_of(residue_index)[:, None], (64, 128))
    chr_ = jnp.broadcast_to(rows_of(chain_index)[:, None], (64, 128))
    resc = jnp.broadcast_to(cols_of(residue_index)[:, None], (32, 128))
    chc = jnp.broadcast_to(cols_of(chain_index)[:, None], (32, 128))
    relpos = jnp.pad(relpos_weight, ((0, 128 - REL_BINS), (0, 0)))

    cvec = normalize(single.astype(F32)).astype(BF16)
    conditioning = jnp.dot(cvec, ada_proj, preferred_element_type=F32)
    ada_scale = jax.nn.sigmoid(conditioning[:, :768])
    ada_shift = conditioning[:, 768:1536]
    feat_at = col * 48
    gate_block = jax.nn.sigmoid(
        lax.dynamic_slice_in_dim(conditioning, 1536 + feat_at, 48, 1)
    )
    normed_in = normalize(noisy.astype(F32))
    hidden = (ada_scale * normed_in + ada_shift).astype(BF16).reshape(512, 768)
    wqkv = pad_last(qkv_proj, 64).reshape(768, 192)
    qkv = jnp.dot(hidden, wqkv, preferred_element_type=F32).astype(BF16)
    q = qkv[:, :64].reshape(8, 64, 64)
    qd = jnp.concatenate([q, q], -1)
    kv = (
        qkv[:, 64:].reshape(8, 2, 2, 16, 2, 64).transpose(4, 0, 1, 3, 2, 5).reshape(2, 8, 32, 128)
    )
    grad_in = cotangent.astype(F32)
    dmx = lanes((grad_in * gate_block).astype(BF16)).reshape(256, 128)

    pair_out, bias, kv_all, dmx_all = pair_stage(
        pair_in, resr, chr_, resc, chc, maskp, relpos, tri_proj, tri_out, bias_proj, kv, dmx
    )

    wout = jnp.pad(
        jnp.swapaxes(out_proj.reshape(48, 16, 48), 0, 1), ((0, 0), (0, 16), (0, 16))
    )
    wout = jnp.concatenate([wout, wout], -1)
    keyok = jnp.swapaxes(token_mask.reshape(16, 2, 16), 1, 2).reshape(256, 2)
    keyok = jnp.repeat(keyok, 64, 1)
    mixed_p, dq, dkv, grad_pair = attention_stage(
        qd, kv_all, dmx_all, wout, bias, keyok, bias_proj
    )
    mixed = unlanes(mixed_p)
    noisy_block = lax.dynamic_slice_in_dim(noisy, feat_at, 48, 2)
    block_out = (noisy_block.astype(F32) + gate_block * mixed).astype(BF16)
    d_gate = jnp.sum(grad_in * mixed, 0) * gate_block * (1.0 - gate_block)
    dkv = (
        dkv.reshape(4, 2, 2, 2, 16, 2, 64).transpose(2, 0, 3, 5, 4, 1, 6).reshape(512, 128)
    )
    d_qkv = jnp.concatenate([dq.reshape(512, 128)[:, :64], dkv], 1)
    d_hidden = dg(d_qkv, wqkv, 1, 1).reshape(8, 64, 768)
    d_scale = jnp.sum(d_hidden * normed_in, 0) * ada_scale * (1.0 - ada_scale)
    d_shift = jnp.sum(d_hidden, 0)
    w_gate = lax.dynamic_slice_in_dim(ada_proj, 1536 + feat_at, 48, 1)
    grads = jnp.concatenate([d_scale, d_shift, d_gate], 1)
    weights = jnp.concatenate([ada_proj[:, :1536], w_gate], 1)
    coarse = grads.astype(BF16)
    fine = (grads - coarse.astype(F32)).astype(BF16)
    d_cvec = dg(jnp.concatenate([coarse, fine], 0), weights, 1, 1)
    d_cvec = d_cvec[:64] + d_cvec[64:]
    d_cvec = total_stage(pad_last(d_cvec, 512).reshape(32, 8, 128)).reshape(64, 512)[:, :384]
    grad_single = normalize_grad(single.astype(F32), d_cvec)
    return pair_out, block_out, grad_pair.reshape(64, 32, 128), grad_single


def solution(mesh):
    return jax.shard_map(
        on_device,
        mesh=mesh,
        in_specs=(
            P("row", "col", None), P(), P(), P(), P(), P(), P(), P(), P("row", None), P(),
            P("samp", "row", None), P(None, None, "col"), P("col", None), P("samp", "row", "col"),
        ),
        out_specs=(
            P("row", "col", None), P("samp", "row", "col"), P("row", "col", None), P("row", None),
        ),
        check_vma=False,
    )
```

time: 513 us -> 171 us (0.33); the launches traced: 504 us -> 171 us
  waiting for transfers between devices: 269 us -> 0 us
  Pallas kernels: 0 us -> 138 us
  local copies, waits for them, and re-layouts: 80 us -> 19.6 us
  blocking collectives: 44.5 us -> 0 us
  matrix products: 40.1 us -> 3.5 us
  other arithmetic: 34.2 us -> 8.34 us
  starting transfers between devices: 20.8 us -> 0 us
  between operations: 15.1 us -> 1.27 us
    pallas_call x0 -> x3, Pallas kernels: none -> 138 us  [the longest x1 75.9 us: pair_stage(): pl.pallas_call(pair_kernel, out_shape=(jax.ShapeDtypeStruct((64, 32, 128)...]
    all_gather x2 -> x0, waiting for transfers between devices: 118 us -> none  [the longest x1 62.2 us: gathered_total(): return lax.all_gather(array, axis).sum(0)]
    reduce_scatter x1 -> x0, waiting for transfers between devices: 77.5 us -> none  [on_device(): lax.psum_scatter(jnp.einsum('jkc,ikc->jic', right_all, left_side, preferr...]
    all_to_all x4 -> x0, waiting for transfers between devices: 73.6 us -> none  [the longest x2 48.7 us: sent_and_summed(): blocks = lax.all_to_all(split_up(array, dim, size), axis, 0, 0, tiled=True)]
    all_to_all x3 -> x0, blocking collectives: 44.5 us -> none  [the longest x2 31.6 us: sent_to_all(): return lax.all_to_all(copies, axis, split_axis=0, concat_axis=0, tiled=True)]
    dot_general x18 -> x4, matrix products: 38.7 us -> 3.5 us  [the longest x1 2.06 us: on_device(): conditioning = jnp.dot(cvec, ada_proj, preferred_element_type=F32)]
    transpose x6 -> x4, local copies, waits for them, and re-layouts: 24.9 us -> 0.62 us  [the longest x1 0.27 us: on_device(): dkv.reshape(4, 2, 2, 2, 16, 2, 64).transpose(2, 0, 3, 5, 4, 1, 6)]
    all_to_all x4 -> x0, starting transfers between devices: 20.4 us -> none  [the longest x2 10.3 us: sent_and_summed(): blocks = lax.all_to_all(split_up(array, dim, size), axis, 0, 0, tiled=True)]
  transfers between devices with their start and end apart: 7 -> 0, of which waited for: 7 -> 0; matrix products, arithmetic and copies ran while one was open for 6% -> 0% of each run, Pallas kernels for 0% -> 0%
where the time goes in v1:
time: 171 us
  Pallas kernels  138 us (81%)
  local copies, waits for them, and re-layouts  19.6 us (11%)
  other arithmetic  8.34 us (5%)
  matrix products  3.5 us (2%)
    pallas_call x1, Pallas kernels, pair_stage(): pl.pallas_call(pair_kernel, out_shape=(jax.ShapeDtypeStruct((64, 32, 128)...  75.9 us
    pallas_call x1, Pallas kernels, attention_stage(): pl.pallas_call(attention_kernel, out_shape=(jax.ShapeDtypeStruct((4, 64,...  37.8 us
    pallas_call x1, Pallas kernels, total_stage(): pl.pallas_call(total_kernel, out_shape=jax.ShapeDtypeStruct((32, 8, 128),...  24.2 us
    unnamed x57, local copies, waits for them, and re-layouts  9.42 us

profile of v1, /device:TPU:8, one launch (start us, length us, event | category | flops | bytes accessed | tf_op | source)
XLA Modules:
  0.0 170.6 jit_solution(65356861810767664)
XLA Ops:
  0.6 0.8 dynamic_slice.27
  1.5 0.8 dynamic_slice.28
  2.3 0.8 dynamic_slice.29
  3.1 0.8 dynamic_slice.30
  6.0 0.8 copy.41.biasp_ref
  6.8 0.9 convert_reduce_fusion.1
  7.7 1.0 fusion.33
  8.7 2.1 %fusion.34 = f32[64,2304]{1,0:T(8,128)S(1)} fusion(bf16[384,2304]{1,0:T(8,128)(2,1)} %param.23, bf16[64,384]{1,0:T(8,128)(2,1)} %param.22, f32[64]{0:T(128)S(1)} %add_rsqrt_fusion.1, f32[64]{0:T(128)S(1)} %broadcast_multiply_fusion.4), kind=kOutput, calls=%fused_computation.55 | convolution fusion | flops 113344512 | bytes 2408960 | tf_op jit(solution)/shard_map/dot_general | solution.py:719
  14.9 75.9 %pair_stage.1 = (bf16[64,32,128]{2,1,0:T(8,128)(2,1)S(1)}, bf16[256,128]{1,0:T(8,128)(2,1)S(1)}, bf16[8,2,8,32,128]{4,3,2,1,0:T(8,128)(2,1)S(1)}, bf16[16,256,128]{2,1,0:T(8,128)(2,1)S(1)}) custom-call(bf16[64,32,128]{2,1,0:T(8,128)(2,1)S(1)} %copy-done, s32[64,128]{1,0:T(8,128)S(1)} %broadcast_in_dim.10.resr_ref, s32[64,128]{1,0:T(8,128)S(1)} %broadcast_in_dim.11.chr_ref, ...), custom_call_target="tpu_custom_call" | custom-call | tf_op jit(solution)/shard_map/pair_stage/pallas_call | solution.py:328
  90.9 0.8 copy-done.1
  94.0 0.9 copy-done.3
  94.9 0.8 copy-done.5
  95.7 0.8 copy-done.10
  96.5 37.8 %attention_stage.1 = (f32[4,64,128]{2,1,0:T(8,128)S(1)}, bf16[8,64,128]{2,1,0:T(8,128)(2,1)S(1)}, bf16[4,4,32,128]{3,2,1,0:T(8,128)(2,1)S(1)}, f32[2048,128]{1,0:T(8,128)S(1)}) custom-call(bf16[8,64,128]{2,1,0:T(8,128)(2,1)S(1)} %pad_maximum_fusion.3.qd_ref, bf16[8,2,8,32,128]{4,3,2,1,0:T(8,128)(2,1)S(1)} %get-tuple-element.13.kv_ref, ...), custom_call_target="tpu_custom_call" | custom-call | tf_op jit(solution)/shard_map/attention_stage/pallas_call | solution.py:557
  135.0 1.1 fusion.17
  136.2 0.8 copy.48
  136.9 1.0 constant_dynamic-slice_fusion
  138.0 1.0 subtract_multiply_fusion.1
  140.2 1.1 subtract_multiply_fusion
  142.7 24.2 %total_stage.1 = f32[32,8,128]{2,1,0:T(8,128)} custom-call(f32[32,8,128]{2,1,0:T(8,128)} %reshape.124.x_ref), custom_call_target="tpu_custom_call" | custom-call | tf_op jit(solution)/shard_map/total_stage/pallas_call | solution.py:647
  166.9 0.9 reshape.125
  168.1 0.8 fusion.32
  168.8 0.8 copy.53
  169.6 1.0 copy.54
  (110 shorter events, 11.9 us)
Async XLA Ops:
  6.8 8.1 %copy-start.4 = (bf16[128,16]{1,0:T(8,128)(2,1)}, bf16[128,16]{1,0:T(8,128)(2,1)S(1)}, u32[]{:S(2)}) copy-start(bf16[128,16]{1,0:T(8,128)(2,1)S(1)} %copy.41.biasp_ref) | copy-start | bytes 12292
  8.7 2.2 %copy-start.14 = (bf16[8,64,768]{2,1,0:T(8,128)(2,1)S(1)}, bf16[8,64,768]{2,1,0:T(8,128)(2,1)}, u32[]{:S(2)}) copy-start(bf16[8,64,768]{2,1,0:T(8,128)(2,1)} %param.24) | copy-start | bytes 2359300
  10.8 3.3 %copy-start.16 = (f32[64,2304]{1,0:T(8,128)}, f32[64,2304]{1,0:T(8,128)S(1)}, u32[]{:S(2)}) copy-start(f32[64,2304]{1,0:T(8,128)S(1)} %fusion.34) | copy-start | bytes 1769476
  11.1 0.9 copy-start.22
  12.0 0.7 copy-start.18
  12.0 1.9 %copy-start.23 = (bf16[8,64,48]{1,2,0:T(8,128)(2,1)S(1)}, bf16[8,64,48]{1,2,0:T(8,128)(2,1)}, u32[]{:S(2)}) copy-start(bf16[8,64,48]{1,2,0:T(8,128)(2,1)} %param.27) | copy-start | bytes 147460
  13.2 1.8 %copy-start = (bf16[64,32,128]{2,1,0:T(8,128)(2,1)S(1)}, bf16[64,32,128]{2,1,0:T(8,128)(2,1)}, u32[]{:S(2)}) copy-start(bf16[64,32,128]{2,1,0:T(8,128)(2,1)} %pair_ref.1) | copy-start | bytes 1572868
  13.2 1.7 %copy-start.6 = (bf16[128,640]{1,0:T(8,128)(2,1)S(1)}, bf16[128,640]{1,0:T(8,128)(2,1)}, u32[]{:S(2)}) copy-start(bf16[128,640]{1,0:T(8,128)(2,1)} %tri_ref.1) | copy-start | bytes 491524
  13.2 1.7 %copy-start.11 = (bf16[128,128]{1,0:T(8,128)(2,1)S(1)}, bf16[128,128]{1,0:T(8,128)(2,1)}, u32[]{:S(2)}) copy-start(bf16[128,128]{1,0:T(8,128)(2,1)} %triout_ref.1) | copy-start | bytes 98308
  13.7 78.8 %copy-start.24 = (bf16[48,768]{1,0:T(8,128)(2,1)S(1)}, bf16[48,768]{1,0:T(8,128)(2,1)}, u32[]{:S(2)}) copy-start(bf16[48,768]{1,0:T(8,128)(2,1)} %param.26) | copy-start | bytes 221188
  14.1 0.7 copy-start.20
  14.9 78.1 %copy-start.25 = (s32[512]{0:T(512)S(1)}, s32[512]{0:T(512)}, u32[]{:S(2)}) copy-start(s32[512]{0:T(512)} %param.17) | copy-start | bytes 6148
  90.9 0.8 copy-start.1
  94.0 0.9 copy-start.3
  94.9 0.8 copy-start.5
  95.7 0.8 copy-start.10
  134.3 0.7 copy-start.12
  136.1 2.9 %copy-start.8 = (bf16[4,4,32,128]{3,2,1,0:T(8,128)(2,1)S(1)}, bf16[4,4,32,128]{3,2,1,0:T(8,128)(2,1)}, u32[]{:S(2)}) copy-start(bf16[4,4,32,128]{3,2,1,0:T(8,128)(2,1)} %copy-done.7) | copy-start | bytes 393220
  137.9 1.7 copy-start.13
  137.9 1.7 copy-start.15
  138.0 1.7 copy-start.19
  140.1 1.4 slice-start
  141.5 26.4 %copy-start.17 = (bf16[64,384]{1,0:T(8,128)(2,1)S(1)}, bf16[64,384]{1,0:T(8,128)(2,1)}, u32[]{:S(2)}) copy-start(bf16[64,384]{1,0:T(8,128)(2,1)} %param.22) | copy-start | bytes 147460
  142.0 26.8 %copy-start.2 = (bf16[64,32,128]{2,1,0:T(8,128)(2,1)S(1)}, bf16[64,32,128]{2,1,0:T(8,128)(2,1)}, u32[]{:S(2)}) copy-start(bf16[64,32,128]{2,1,0:T(8,128)(2,1)} %copy-done.1) | copy-start | bytes 1572868
  (3 other events, 1.9 us)

commit v2 on v0

v2 whole, which is shorter than its diff:
```python
import jax
import jax.numpy as jnp
from jax import lax
from jax.experimental import pallas as pl
from jax.experimental.pallas import tpu as pltpu
from jax.sharding import PartitionSpec as P

HEAD_DIM = 48
REL_BINS = 66
EPSILON = 1e-05
MESH = pl.DeviceIdType.MESH
F32 = jnp.float32
BF16 = jnp.bfloat16
NCOL = 16
NROW = 8


def dg(a, b, ca, cb, **kw):
    return lax.dot_general(a, b, (((ca,), (cb,)), ((), ())), preferred_element_type=F32, **kw)


def place():
    return lax.axis_index("row"), lax.axis_index("col"), lax.axis_index("samp")


def rmod(a, n):
    return lax.rem(a, n)


def ring_shift(oz, dest_core):
    if oz == 2:
        return 2 + 4 * dest_core
    return (0, 1, None, 7)[oz]


def row_dest(oz, cx):
    row, col, samp = place()
    z, core = samp * 4 + row // 2, rmod(row, 2)
    to_core = rmod(core + cx, 2)
    to_z = rmod(z + ring_shift(oz, to_core), 8)
    return rmod(to_z, 4) * 2 + to_core, col, to_z // 4


def row_source(oz, cx):
    row, col, samp = place()
    z, core = samp * 4 + row // 2, rmod(row, 2)
    from_core = rmod(core + cx, 2)
    from_z = rmod(z + 8 - ring_shift(oz, core), 8)
    return rmod(from_z, 4) * 2 + from_core, col, from_z // 4


ROW_IDS = [(oz, cx) for oz in range(4) for cx in range(2) if (oz, cx) != (0, 0)]


def remote(src, dst, ssem, rsem, to):
    return pltpu.make_async_remote_copy(
        src_ref=src, dst_ref=dst, send_sem=ssem, recv_sem=rsem, device_id=to, device_id_type=MESH
    )


def col_start(src_of, slot_of, ssem, rsem):
    row, col, samp = place()

    def one(o, _):
        to = rmod(col + o, NCOL)
        remote(src_of(to), slot_of(col), ssem.at[o], rsem.at[o], (row, to, samp)).start()
        return 0

    lax.fori_loop(1, NCOL, one, 0)


def col_wait(src_of, slot_of, ssem, rsem, recv=True, send=True):
    row, col, samp = place()

    def one(o, _):
        to = rmod(col + o, NCOL)
        came = rmod(col + NCOL - o, NCOL)
        if recv:
            remote(src_of(to), slot_of(came), ssem.at[o], rsem.at[o], (row, to, samp)).wait_recv()
        if send:
            remote(src_of(to), slot_of(came), ssem.at[o], rsem.at[o], (row, to, samp)).wait_send()
        return 0

    lax.fori_loop(1, NCOL, one, 0)


def row_start(src_of, slot_of, ssem, rsem):
    row = lax.axis_index("row")
    for oz, cx in ROW_IDS:
        to = row_dest(oz, cx)
        i = oz * 2 + cx
        remote(src_of(to[0]), slot_of(row), ssem.at[i], rsem.at[i], to).start()


def row_wait(src_of, slot_of, ssem, rsem, recv=True, send=True):
    for oz, cx in ROW_IDS:
        to, came = row_dest(oz, cx), row_source(oz, cx)
        i = oz * 2 + cx
        copy = remote(src_of(to[0]), slot_of(came[0]), ssem.at[i], rsem.at[i], to)
        if recv:
            copy.wait_recv()
        if send:
            copy.wait_send()


def signal(sem, to):
    pl.semaphore_signal(sem, inc=1, device_id=to, device_id_type=MESH)


def both(x, low, first):
    turned = pltpu.roll(x, 64, 1)
    return jnp.where(low, x, turned) if first else jnp.where(low, turned, x)


def layer_norm(x, axis):
    mean = jnp.mean(x, axis, keepdims=True)
    cent = x - mean
    var = jnp.mean(cent * cent, axis, keepdims=True)
    return cent * lax.rsqrt(var + EPSILON)


def two_parts(x):
    coarse = x.astype(BF16)
    return jnp.concatenate([coarse, (x - coarse.astype(F32)).astype(BF16)], 0)


def step_kernel(
    res_ref, chain_ref, mask_ref,
    pair_hbm, relpos_ref, tri_hbm, triout_ref, biasp_ref, single_ref, ada_hbm, noisy_hbm,
    qkvw_ref, outp_ref, cot_ref,
    pairout_ref, block_ref, gpair_ref, gsingle_ref,
    pair_in, tri_w, ada_w, noisy, idx_r, mrow, relpos_w,
    pf, gate, lrf, lbuf, recv_a, got, rcat, mtmp, tbuf, got_c, got_d, bias_f, bias_b, bias_got,
    cvec_s, scale_s, shift_s, wg_s, gate_t, g_t, noisy_t, normed, hidden, wqkv, q_t, kv_f,
    kv_own, kv_all, dmx_own, dmx_all, da_t, keyok, sraw, draw,
    mix_s, mix_r, dkv_s, dkv_m, dkv_o, dkv_r, dq_t, dkv_tok, dbias, db_s, db_r,
    dsc, dsh, dga, dc_s, dc_r, dc_p, gs_own, gs_all,
    sa, ra, sb, rb, sc, rc, sd, rd, se, re, skv, rkv, skf, rkf, sdm, rdm,
    sm, rm, sk, rk, sko, rko, sbb, rbb, st, rt, sp, rp_, sg, rg, loc, locm,
):
    row, col, samp = place()
    core = rmod(row, 2)
    zlo = row // 2
    mate = (row + 1 - 2 * core, col, samp)
    far = (row, col, 1 - samp)
    barrier = pltpu.get_barrier_semaphore()

    loads = [
        pltpu.make_async_copy(s, d, loc.at[10 + i])
        for i, (s, d) in enumerate(
            [(pair_hbm, pair_in), (tri_hbm, tri_w), (ada_hbm, ada_w), (noisy_hbm, noisy)]
        )
    ]
    for copy in loads:
        copy.start()
    for oz, cx in ROW_IDS:
        signal(barrier, row_source(oz, cx))

    def greet(o, _):
        signal(barrier, (row, rmod(col + o, NCOL), samp))
        return 0

    def greet_row(o, _):
        signal(barrier, (rmod(row + o, NROW), col, samp))
        return 0

    def greet_far(o, _):
        signal(barrier, (row, rmod(col + o, NCOL), 1 - samp))
        return 0

    lax.fori_loop(1, NCOL, greet, 0)
    lax.fori_loop(1, NROW, greet_row, 0)
    lax.fori_loop(0, NCOL, greet_far, 0)

    low = lax.broadcasted_iota(jnp.int32, (64, 128), 1) < 64
    low16 = lax.broadcasted_iota(jnp.int32, (16, 128), 1) < 64
    low1 = lax.broadcasted_iota(jnp.int32, (1, 128), 1) < 64
    diag = (lax.broadcasted_iota(jnp.int32, (128, 128), 0) < 64) == (
        lax.broadcasted_iota(jnp.int32, (128, 128), 1) < 64
    )

    def blockdiag(x):
        return jnp.where(diag, jnp.concatenate([x, x], 0), 0.0).astype(BF16)

    def indices(i, _):
        at = pl.ds(i, 1)
        idx_r[0, at, :] = jnp.full((1, 128), res_ref[row * 64 + i], jnp.int32)
        idx_r[1, at, :] = jnp.full((1, 128), chain_ref[row * 64 + i], jnp.int32)
        m = jnp.full((1, 128), mask_ref[row * 64 + i].astype(F32), F32)
        mrow[at, :] = m
        mrow[pl.ds(64 + i, 1), :] = m
        return 0

    lax.fori_loop(0, 64, indices, 0, unroll=4)
    mrow[...] = mrow[...].T
    relpos_w[...] = jnp.zeros_like(relpos_w)
    relpos_w[0:REL_BINS, :] = relpos_ref[...]
    loads[0].wait()

    def load(i, _):
        pf[pl.ds(i * 32, 32), :] = pair_in[i].astype(F32)
        return 0

    lax.fori_loop(0, 64, load, 0, unroll=4)
    loads[1].wait()
    bins = lax.broadcasted_iota(jnp.int32, (64, 128), 1)

    def stage1(lo, _):
        parts = []
        for hi in range(2):
            j = lo + 16 * hi
            off = jnp.clip(idx_r[0] - res_ref[col * 32 + j] + 32, 0, 64)
            bucket = jnp.where(idx_r[1] == chain_ref[col * 32 + j], off, REL_BINS - 1)
            onehot = jnp.where(bucket == bins, 1.0, 0.0).astype(BF16)
            parts.append(
                pf[pl.ds(j, 64, stride=32), :]
                + jnp.dot(onehot, relpos_w[...], preferred_element_type=F32)
            )
            pf[pl.ds(j, 64, stride=32), :] = parts[hi]
        zl = layer_norm(jnp.concatenate(parts, 0), -1).astype(BF16)
        pt = dg(tri_w[:, :512], zl, 0, 1)
        mask = mrow[0:1, :] * jnp.where(
            low1, mask_ref[col * 32 + lo].astype(F32), mask_ref[col * 32 + 16 + lo].astype(F32)
        )
        lrf[pl.ds(lo, 128, stride=16), :] = jax.nn.sigmoid(pt[128:256]) * pt[:128] * mask
        lrf[pl.ds(2048 + lo, 128, stride=16), :] = (
            jax.nn.sigmoid(pt[384:512]) * pt[256:384] * mask
        )
        gate[lo] = jax.nn.sigmoid(jnp.dot(zl, tri_w[:, 512:], preferred_element_type=F32))
        return 0

    lax.fori_loop(0, 16, stage1, 0, unroll=2)

    a_src = [lambda to, h=h: lbuf.at[h, to] for h in range(2)]
    a_slot = [lambda c, h=h: recv_a.at[h, c] for h in range(2)]
    b_src = [lambda r, h=h: recv_a.at[h, :, r] for h in range(2)]
    b_slot = [lambda r, h=h: got.at[h, r] for h in range(2)]
    own_a = [pltpu.make_async_copy(lbuf.at[h, col], recv_a.at[h, col], loc.at[h]) for h in range(2)]
    own_b = [
        pltpu.make_async_copy(recv_a.at[h, :, row], got.at[h, row], loc.at[2 + h])
        for h in range(2)
    ]
    for h in range(2):

        def pack(c, _):
            lbuf[h, c] = lrf[pl.ds(h * 2048 + c * 128, 128), :].astype(BF16).reshape(8, 16, 128)
            return 0

        lax.fori_loop(0, 16, pack, 0)
        if h == 0:
            pl.semaphore_wait(barrier, 7 + 15 + 7 + 16)
        own_a[h].start()
        col_start(a_src[h], a_slot[h], sa.at[h], ra.at[h])

    cvec = layer_norm(single_ref[...].astype(F32), -1).astype(BF16)
    cvec_s[...] = cvec
    wqkv[...] = jnp.zeros_like(wqkv)
    for p in range(3):
        wqkv[p * 64 : p * 64 + 48, :] = qkvw_ref[p]
    loads[2].wait()
    scale_s[...] = jax.nn.sigmoid(jnp.dot(cvec, ada_w[:, :768], preferred_element_type=F32))
    shift_s[...] = jnp.dot(cvec, ada_w[:, 768:1536], preferred_element_type=F32)
    loads[3].wait()

    def sample(s, _):
        at = pl.ds(pl.multiple_of(s * 64, 64), 64)
        n = layer_norm(noisy[at, :].astype(F32), -1)
        normed[at, :] = n
        hidden[at, :] = (scale_s[...] * n + shift_s[...]).astype(BF16)
        return 0

    lax.fori_loop(0, 8, sample, 0)
    kv_f[...] = dg(hidden[...], wqkv[64:, :], 1, 1)

    def kv_pack(t, _):
        r0 = kv_f[pl.ds(t * 32, 16), :]
        r1 = kv_f[pl.ds(t * 32 + 16, 16), :]
        to = pl.ds(pl.multiple_of(rmod(t, 2) * 16, 16), 16)
        kv_own[0, t // 2, to, :] = jnp.where(low16, r0, pltpu.roll(r1, 64, 1)).astype(BF16)
        kv_own[1, t // 2, to, :] = jnp.where(low16, pltpu.roll(r0, 64, 1), r1).astype(BF16)
        return 0

    lax.fori_loop(0, 16, kv_pack, 0, unroll=2)
    kv_keep = pltpu.make_async_copy(kv_own, kv_all.at[row], loc.at[4])
    kv_keep.start()
    kv_out = []
    for o in range(1, 4):
        to = (rmod(zlo + o, 4) * 2 + core, col, samp)
        kv_out.append(remote(kv_own, kv_all.at[row], skv.at[o], rkv.at[o], to))
    kv_mate = remote(kv_own, kv_all.at[row], skf.at[0], rkf.at[0], mate)

    own_a[0].wait()
    col_wait(a_src[0], a_slot[0], sa.at[0], ra.at[0])
    own_b[0].start()
    row_start(b_src[0], b_slot[0], sb.at[0], rb.at[0])
    kv_mate.start()
    for copy in kv_out:
        copy.start()

    feat = lax.broadcasted_iota(jnp.int32, (768, 64), 1)
    sel = jnp.where(
        (lax.broadcasted_iota(jnp.int32, (768, 64), 0) == col * 48 + feat) & (feat < 48), 1.0, 0.0
    ).astype(BF16)
    wg_s[...] = jnp.dot(ada_w[:, 1536:], sel, preferred_element_type=F32).astype(BF16)
    gate_t[...] = jax.nn.sigmoid(
        dg(wg_s[...], jnp.concatenate([cvec_s[...], cvec_s[...]], 0), 0, 1)
    )
    lane = lax.broadcasted_iota(jnp.int32, (64, 128), 1)
    tok = lax.broadcasted_iota(jnp.int32, (64, 128), 0)
    put = [jnp.where(lane == tok + 64 * h, 1.0, 0.0).astype(BF16) for h in range(2)]
    for u in range(4):
        g = jnp.dot(cot_ref[2 * u], put[0], preferred_element_type=F32) + jnp.dot(
            cot_ref[2 * u + 1], put[1], preferred_element_type=F32
        )
        g_t[u] = g
        dmx_own[:, u * 128 : u * 128 + 128] = (g * gate_t[:48, :]).astype(BF16)
    dm_src, dm_slot = (lambda to: dmx_own), (lambda c: dmx_all.at[c])
    dm_keep = pltpu.make_async_copy(dmx_own, dmx_all.at[col], loc.at[5])
    own_a[1].wait()
    col_wait(a_src[1], a_slot[1], sa.at[1], ra.at[1])
    own_b[1].start()
    row_start(b_src[1], b_slot[1], sb.at[1], rb.at[1])
    dm_keep.start()
    col_start(dm_src, dm_slot, sdm, rdm)
    q_t[...] = dg(wqkv[:64, :], hidden[...], 1, 1)
    noisy_t[...] = dg(sel, noisy[...], 0, 1)

    def key_mask(t, _):
        jb, lo = t // 16, rmod(t, 16)
        keyok[pl.ds(t, 1), :] = jnp.where(
            low1,
            mask_ref[jb * 32 + lo].astype(F32),
            mask_ref[jb * 32 + 16 + lo].astype(F32),
        )
        return 0

    lax.fori_loop(0, 256, key_mask, 0, unroll=4)

    for h in (1, 0):
        own_b[h].wait()
        row_wait(b_src[h], b_slot[h], sb.at[h], rb.at[h])

    def turn(r, _):
        rcat[pl.ds(pl.multiple_of(r * 128, 128), 128), :] = (
            got[1, r].reshape(256, 128).astype(F32).T.astype(BF16)
        )
        return 0

    lax.fori_loop(0, 8, turn, 0)

    def tri(rp, _):
        rhs = jnp.concatenate(
            [got[0, 2 * rp].reshape(256, 128), got[0, 2 * rp + 1].reshape(256, 128)], 1
        )
        mtmp[...] = jnp.dot(rcat[...], rhs, preferred_element_type=F32)

        def out(rj, _):
            for half in range(2):
                top = mtmp[pl.ds(rj * 128, 64), half * 128 : half * 128 + 128]
                bot = mtmp[pl.ds(rj * 128 + 64, 64), half * 128 : half * 128 + 128]
                for jh in range(2):
                    a = slice(jh * 32, jh * 32 + 16)
                    b = slice(jh * 32 + 16, jh * 32 + 32)
                    t = jnp.where(
                        low16,
                        top[a] + pltpu.roll(bot[a], 64, 1),
                        pltpu.roll(top[b], 64, 1) + bot[b],
                    )
                    tbuf[2 * rp + half, 2 * rj + jh] = t.astype(BF16)
            return 0

        lax.fori_loop(0, 8, out, 0, unroll=2)
        return 0

    lax.fori_loop(0, 4, tri, 0)

    c_src, c_slot = (lambda r: tbuf.at[r]), (lambda r: got_c.at[r])
    d_src, d_slot = (lambda c: got_c.at[:, c]), (lambda c: got_d.at[c])
    own_c = pltpu.make_async_copy(tbuf.at[row], got_c.at[row], loc.at[6])
    own_c.start()
    row_start(c_src, c_slot, sc, rc)

    for o in range(1, 4):
        came = rmod(zlo + 4 - o, 4) * 2 + core
        remote(kv_own, kv_all.at[came], skv.at[o], rkv.at[o], mate).wait_recv()
        remote(kv_all.at[came], kv_all.at[came], skf.at[o], rkf.at[o], mate).start()

    dm_keep.wait()
    col_wait(dm_src, dm_slot, sdm, rdm)
    da_t[...] = jnp.zeros_like(da_t)
    da_t[:48, :] = (
        jnp.dot(outp_ref[...], dmx_all[...].reshape(768, 512), preferred_element_type=F32)
        .astype(BF16)
        .astype(F32)
    )
    own_c.wait()
    row_wait(c_src, c_slot, sc, rc)
    own_d = pltpu.make_async_copy(got_c.at[:, col], got_d.at[col], loc.at[7])
    own_d.start()
    col_start(d_src, d_slot, sd, rd)

    kv_keep.wait()
    for copy in kv_out:
        copy.wait_send()
    kv_mate.wait_send()
    for o in range(4):
        came = rmod(zlo + 4 - o, 4) * 2
        remote(
            kv_all.at[came + core], kv_all.at[came + 1 - core], skf.at[o], rkf.at[o], mate
        ).wait_recv()
        if o > 0:
            remote(
                kv_all.at[came + core], kv_all.at[came + core], skf.at[o], rkf.at[o], mate
            ).wait_send()

    def half_of(ref, u, sh):
        tile = ref[:, pl.ds(pl.multiple_of(u * 128, 128), 128)].astype(F32)
        return blockdiag(both(tile, low, sh == 0))

    def keys(which, s):
        return jnp.concatenate([kv_all[r, which, s] for r in range(NROW)], 0)

    def raw(u, _):
        for sh in range(2):
            s = 2 * u + sh
            sraw[s] = jnp.dot(keys(0, s), half_of(q_t, u, sh), preferred_element_type=F32)
            draw[s] = jnp.dot(keys(1, s), half_of(da_t, u, sh), preferred_element_type=F32)
        return 0

    lax.fori_loop(0, 4, raw, 0)
    own_d.wait()
    col_wait(d_src, d_slot, sd, rd)

    def widen(c, _):
        lrf[pl.ds(c * 128, 128), :] = got_d[c].reshape(128, 128).astype(F32)
        return 0

    lax.fori_loop(0, 16, widen, 0)

    def stage3(lo, _):
        tn = layer_norm(lrf[pl.ds(lo, 128, stride=16), :], 0).astype(BF16)
        upd = dg(tn, triout_ref[...], 0, 0) * gate[lo]
        outs = []
        for hi in range(2):
            at = pl.ds(lo + 16 * hi, 64, stride=32)
            val = (pf[at, :] + upd[hi * 64 : hi * 64 + 64]).astype(BF16)
            pf[at, :] = val.astype(F32)
            outs.append(val)
        bias_f[pl.ds(lo, 16, stride=16), :] = dg(biasp_ref[...], jnp.concatenate(outs, 0), 1, 1)
        return 0

    lax.fori_loop(0, 16, stage3, 0, unroll=2)
    bias_b[...] = bias_f[...].astype(BF16).reshape(16, 16, 128)
    e_src, e_slot = (lambda c: bias_b.at[c]), (lambda c: bias_got.at[c])
    own_e = pltpu.make_async_copy(bias_b.at[col], bias_got.at[col], loc.at[8])
    own_e.start()
    col_start(e_src, e_slot, se, re)

    def store(i, _):
        pairout_ref[i] = pf[pl.ds(i * 32, 32), :].astype(BF16)
        return 0

    lax.fori_loop(0, 64, store, 0, unroll=4)
    dbias[...] = jnp.zeros_like(dbias)
    own_e.wait()
    col_wait(e_src, e_slot, se, re)

    scale = 1.0 / HEAD_DIM**0.5

    def mix_src(u):
        return lambda f: mix_s.at[u, f]

    def mix_slot(u):
        return lambda h: mix_r.at[u, h]

    def to_mate(u):
        return remote(dkv_s.at[:, 1 - core, u], dkv_m.at[u], sk.at[u], rk.at[u], mate)

    def to_chip(u, o):
        z = rmod(zlo + o, 4)
        return remote(
            dkv_o.at[u, z], dkv_r.at[u, zlo], sko.at[u, o], rko.at[u, o], (z * 2 + core, col, samp)
        )

    def pass_on(u):
        to_mate(u).wait_recv()
        for z in range(4):
            dkv_o[u, z] = (
                dkv_s[z, core, u].astype(F32) + dkv_m[u, z].astype(F32)
            ).astype(BF16)
        for o in range(1, 4):
            to_chip(u, o).start()

    def pair_of_samples(u, _):
        folded, dqs = [], []
        for sh in range(2):
            s = 2 * u + sh
            kp, vp = keys(0, s), keys(1, s)
            qq, dd = half_of(q_t, u, sh), half_of(da_t, u, sh)
            sco = sraw[s] * scale + bias_got[...].reshape(256, 128).astype(F32)
            sco = jnp.where(keyok[...] > 0, sco, -1000000000.0)
            top = jnp.max(sco, 0, keepdims=True)
            top = jnp.maximum(top, pltpu.roll(top, 64, 1))
            ex = jnp.exp(sco - top)
            tot = jnp.sum(ex, 0, keepdims=True)
            probs = ex * (1.0 / (tot + pltpu.roll(tot, 64, 1)))
            pb = probs.astype(BF16)
            folded.append(dg(vp, pb, 0, 0))
            dp = draw[s]
            dot = jnp.sum(probs * dp, 0, keepdims=True)
            ds = probs * (dp - (dot + pltpu.roll(dot, 64, 1)))
            dbias[...] += ds
            dsb = (ds * scale).astype(BF16)
            dqs.append(dg(kp, dsb, 0, 0))
            dk = dg(dsb, qq, 1, 1).astype(BF16)
            dv = dg(pb, dd, 1, 1).astype(BF16)
            for r in range(NROW):
                dkv_s[r // 2, r % 2, u, sh] = dk[r * 32 : r * 32 + 32]
                dkv_s[r // 2, r % 2, u, 2 + sh] = dv[r * 32 : r * 32 + 32]

        def fold(m0, m1):
            return jnp.where(
                low,
                m0[:64] + pltpu.roll(m0[64:], 64, 1),
                pltpu.roll(m1[:64], 64, 1) + m1[64:],
            ).astype(BF16)

        att = fold(*folded)
        dq_t[u] = fold(*dqs)
        mix_s[u] = dg(outp_ref[...], att[:48], 0, 0).astype(BF16).reshape(16, 48, 128)
        pltpu.make_async_copy(mix_s.at[u, col], mix_r.at[u, col], locm.at[u]).start()
        to_mate(u).start()
        col_start(mix_src(u), mix_slot(u), sm.at[u], rm.at[u])

        @pl.when(u > 0)
        def _():
            pass_on(u - 1)

        return 0

    lax.fori_loop(0, 4, pair_of_samples, 0)

    db_s[...] = dbias[...].reshape(16, 16, 128)
    own_db = pltpu.make_async_copy(db_s.at[col], db_r.at[samp, col], loc.at[9])
    own_db.start()

    def db_copy(o):
        to = rmod(col + o, NCOL)
        return remote(
            db_s.at[to], db_r.at[samp, col], sbb.at[1, o], rbb.at[1, o], (row, to, 1 - samp)
        )

    def db_send(o, _):
        db_copy(o).start()
        return 0

    pass_on(3)
    lax.fori_loop(0, NCOL, db_send, 0)
    near_src, near_slot = (lambda c: db_s.at[c]), (lambda c: db_r.at[samp, c])
    col_start(near_src, near_slot, sbb.at[0], rbb.at[0])

    dga[...] = jnp.zeros_like(dga)

    def mixed_of(u, _):
        pltpu.make_async_copy(mix_s.at[u, col], mix_r.at[u, col], locm.at[u]).wait()
        col_wait(mix_src(u), mix_slot(u), sm.at[u], rm.at[u])
        total = mix_r[u, 0].astype(F32)
        for h in range(1, NCOL):
            total = total + mix_r[u, h].astype(F32)
        lanes = pl.ds(pl.multiple_of(u * 128, 128), 128)
        out = noisy_t[:48, lanes] + gate_t[:48, :] * total
        block_ref[2 * u] = out[:, :64].astype(BF16)
        block_ref[2 * u + 1] = pltpu.roll(out, 64, 1)[:, :64].astype(BF16)
        dga[:48, :] += g_t[u] * total
        return 0

    lax.fori_loop(0, 4, mixed_of, 0)

    dsc[...] = jnp.zeros_like(dsc)
    dsh[...] = jnp.zeros_like(dsh)

    def hidden_grad(u, _):
        to_mate(u).wait_send()
        for o in range(1, 4):
            came = rmod(zlo + 4 - o, 4)
            remote(
                dkv_o.at[u, came], dkv_r.at[u, came], sko.at[u, o], rko.at[u, o], mate
            ).wait_recv()
            to_chip(u, o).wait_send()
        dkv_r[u, zlo] = dkv_o[u, zlo]
        tot = dkv_r[u, 0].astype(F32)
        for z in range(1, 4):
            tot = tot + dkv_r[u, z].astype(F32)
        for sh in range(2):
            for jb in range(2):
                a = tot[sh, jb * 16 : jb * 16 + 16]
                b = tot[2 + sh, jb * 16 : jb * 16 + 16]
                base = sh * 64 + jb * 32
                dkv_tok[base : base + 16, :] = jnp.where(low16, a, pltpu.roll(b, 64, 1)).astype(BF16)
                dkv_tok[base + 16 : base + 32, :] = jnp.where(
                    low16, pltpu.roll(a, 64, 1), b
                ).astype(BF16)
        dh = dg(dq_t[u], wqkv[:64, :], 0, 0) + jnp.dot(
            dkv_tok[...], wqkv[64:, :], preferred_element_type=F32
        )
        n = normed[pl.ds(pl.multiple_of(u * 128, 128), 128), :]
        w = dh * n
        dsc[...] += w[:64] + w[64:]
        dsh[...] += dh[:64] + dh[64:]
        return 0

    lax.fori_loop(0, 4, hidden_grad, 0)
    sg_ = scale_s[...]
    part = dg(two_parts(dsc[...] * sg_ * (1.0 - sg_)), ada_w[:, :768], 1, 1)
    part = part + dg(two_parts(dsh[...]), ada_w[:, 768:1536], 1, 1)
    part = part[:64] + part[64:]
    acc = dga[...]
    acc = (acc + pltpu.roll(acc, 64, 1)) * gate_t[...] * (1.0 - gate_t[...])
    coarse = acc.astype(BF16)
    fine = (acc - coarse.astype(F32)).astype(BF16)
    part = part + (dg(coarse, wg_s[...], 0, 1) + dg(fine, wg_s[...], 0, 1))[:64]
    dc_s[...] = part.reshape(8, 8, 384)

    half_col = col // 2
    even = rmod(col, 2) == 0

    def part_copy(o):
        g = rmod(half_col + o, 8)
        return remote(dc_s.at[g], dc_r.at[col], st.at[o], rt.at[col], (row, 2 * g, samp))

    @pl.when(jnp.logical_not(even))
    def _():
        part_copy(0).start()

    def part_send(o, _):
        part_copy(o).start()
        return 0

    lax.fori_loop(1, 8, part_send, 0)

    def own_copy(o):
        return remote(
            gs_own, gs_all.at[half_col], sg.at[o], rg.at[half_col], (row, rmod(col + o, NCOL), samp)
        )

    @pl.when(even)
    def _():
        dc_r[col] = dc_s[half_col]

        def arrived(o, _):
            came = rmod(col + o, NCOL)
            remote(dc_s.at[0], dc_r.at[came], st.at[0], rt.at[came], far).wait_recv()
            return 0

        lax.fori_loop(1, NCOL, arrived, 0)
        tot = dc_r[0]
        for c in range(1, NCOL):
            tot = tot + dc_r[c]
        dc_p[samp] = tot
        other = remote(dc_p.at[samp], dc_p.at[samp], sp.at[0], rp_.at[0], far)
        other.start()
        own = single_ref[...].astype(F32).reshape(8, 8, 384)
        mine = jnp.zeros((8, 384), F32)
        for g in range(8):
            mine = mine + jnp.where(half_col == g, own[g], 0.0)
        mean = jnp.mean(mine, -1, keepdims=True)
        cent = mine - mean
        inv = lax.rsqrt(jnp.mean(cent * cent, -1, keepdims=True) + EPSILON)
        unit = cent * inv
        remote(dc_p.at[samp], dc_p.at[1 - samp], sp.at[0], rp_.at[0], far).wait_recv()
        other.wait_send()
        up = dc_p[0] + dc_p[1]
        gs_own[...] = inv * (
            up - jnp.mean(up, -1, keepdims=True) - unit * jnp.mean(up * unit, -1, keepdims=True)
        )

        def tell(o, _):
            own_copy(o).start()
            return 0

        lax.fori_loop(1, NCOL, tell, 0)
        gs_all[half_col] = gs_own[...]

    own_db.wait()
    col_wait(near_src, near_slot, sbb.at[0], rbb.at[0])

    def db_wait(o, _):
        came = rmod(col + NCOL - o, NCOL)
        remote(db_s.at[came], db_r.at[1 - samp, came], sbb.at[1, o], rbb.at[1, o], far).wait_recv()
        db_copy(o).wait_send()
        return 0

    lax.fori_loop(0, NCOL, db_wait, 0)
    dbias[...] = (db_r[0] + db_r[1]).reshape(256, 128)
    biasp3 = jnp.concatenate([biasp_ref[...]] * 3, 0)

    def grad(lo, _):
        d = dbias[pl.ds(lo, 16, stride=16), :]
        d1 = d.astype(BF16)
        rest = d - d1.astype(F32)
        d2 = rest.astype(BF16)
        d3 = (rest - d2.astype(F32)).astype(BF16)
        g = dg(jnp.concatenate([d1, d2, d3], 0), biasp3, 0, 0)
        for hi in range(2):
            gpair_ref[pl.ds(lo + 16 * hi, 64, stride=32), :] = g[hi * 64 : hi * 64 + 64]
        return 0

    lax.fori_loop(0, 16, grad, 0, unroll=2)

    @pl.when(jnp.logical_not(even))
    def _():
        part_copy(0).wait_send()

    def part_sent(o, _):
        part_copy(o).wait_send()
        return 0

    lax.fori_loop(1, 8, part_sent, 0)

    @pl.when(even)
    def _():
        def told(o, _):
            own_copy(o).wait_send()
            return 0

        lax.fori_loop(1, NCOL, told, 0)

    def total_came(g):
        remote(gs_own, gs_all.at[g], sg.at[0], rg.at[g], far).wait_recv()

    @pl.when(jnp.logical_not(even))
    def _():
        total_came(half_col)

    def came_from(o, _):
        total_came(rmod(half_col + o, 8))
        return 0

    lax.fori_loop(1, 8, came_from, 0)
    gsingle_ref[...] = gs_all[...].reshape(64, 384)


def on_device(
    pair_in, residue_index, chain_index, token_mask, relpos_weight, tri_proj, tri_out, bias_proj,
    single, ada_proj, noisy, qkv_proj, out_proj, cotangent,
):
    vm = pl.BlockSpec(memory_space=pltpu.VMEM)
    sm = pl.BlockSpec(memory_space=pltpu.SMEM)
    hbm = pl.BlockSpec(memory_space=pl.ANY)
    dma = pltpu.SemaphoreType.DMA
    v = pltpu.VMEM
    pair_out, block_t, grad_pair, grad_single = pl.pallas_call(
        step_kernel,
        out_shape=(
            jax.ShapeDtypeStruct((64, 32, 128), BF16),
            jax.ShapeDtypeStruct((8, 48, 64), BF16),
            jax.ShapeDtypeStruct((2048, 128), F32),
            jax.ShapeDtypeStruct((64, 384), F32),
        ),
        in_specs=[sm, sm, sm, hbm, vm, hbm, vm, vm, vm, hbm, hbm, vm, vm, vm],
        out_specs=(vm,) * 4,
        scratch_shapes=[
            v((64, 32, 128), BF16), v((128, 640), BF16), v((384, 2304), BF16), v((512, 768), BF16),
            v((2, 64, 128), jnp.int32), v((128, 128), F32), v((128, 128), BF16),
            v((2048, 128), F32), v((16, 128, 128), F32), v((4096, 128), F32),
            v((2, 16, 8, 16, 128), BF16), v((2, 16, 8, 16, 128), BF16),
            v((2, 8, 16, 16, 128), BF16), v((1024, 256), BF16), v((1024, 256), F32),
            v((8, 16, 16, 128), BF16), v((8, 16, 16, 128), BF16), v((16, 8, 16, 128), BF16),
            v((256, 128), F32), v((16, 16, 128), BF16), v((16, 16, 128), BF16),
            v((64, 384), BF16), v((64, 768), F32), v((64, 768), F32), v((384, 64), BF16),
            v((64, 128), F32), v((4, 48, 128), F32), v((64, 512), F32), v((512, 768), F32),
            v((512, 768), BF16), v((192, 768), BF16), v((64, 512), F32), v((512, 128), F32),
            v((2, 8, 32, 128), BF16), v((8, 2, 8, 32, 128), BF16), v((48, 512), BF16),
            v((16, 48, 512), BF16), v((64, 512), F32), v((256, 128), F32), v((8, 256, 128), F32),
            v((8, 256, 128), F32),
            v((4, 16, 48, 128), BF16), v((4, 16, 48, 128), BF16), v((4, 2, 4, 4, 32, 128), BF16),
            v((4, 4, 4, 32, 128), BF16), v((4, 4, 4, 32, 128), BF16), v((4, 4, 4, 32, 128), BF16),
            v((4, 64, 128), BF16), v((128, 128), BF16), v((256, 128), F32), v((16, 16, 128), F32),
            v((2, 16, 16, 128), F32),
            v((64, 768), F32), v((64, 768), F32), v((64, 128), F32), v((8, 8, 384), F32),
            v((16, 8, 384), F32), v((2, 8, 384), F32), v((8, 384), F32), v((8, 8, 384), F32),
            dma((2, 16)), dma((2, 16)), dma((2, 8)), dma((2, 8)), dma((8,)), dma((8,)),
            dma((16,)), dma((16,)), dma((16,)), dma((16,)), dma((4,)), dma((4,)),
            dma((4,)), dma((4,)), dma((16,)), dma((16,)),
            dma((4, 16)), dma((4, 16)), dma((4,)), dma((4,)), dma((4, 4)), dma((4, 4)),
            dma((2, 16)), dma((2, 16)), dma((8,)), dma((16,)), dma((1,)), dma((1,)),
            dma((16,)), dma((8,)), dma((14,)), dma((4,)),
        ],
        compiler_params=pltpu.CompilerParams(
            collective_id=1, has_side_effects=True, vmem_limit_bytes=60 * 1024 * 1024
        ),
        name="step",
    )(
        residue_index, chain_index, token_mask, pair_in, relpos_weight, tri_proj, tri_out,
        bias_proj.T, single, ada_proj, noisy.reshape(512, 768), qkv_proj.transpose(1, 2, 0),
        out_proj, cotangent.transpose(0, 2, 1),
    )
    return pair_out, block_t.transpose(0, 2, 1), grad_pair.reshape(64, 32, 128), grad_single


def solution(mesh):
    return jax.shard_map(
        on_device,
        mesh=mesh,
        in_specs=(
            P("row", "col", None), P(), P(), P(), P(), P(), P(), P(), P("row", None), P(),
            P("samp", "row", None), P(None, None, "col"), P("col", None), P("samp", "row", "col"),
        ),
        out_specs=(
            P("row", "col", None), P("samp", "row", "col"), P("row", "col", None), P("row", None),
        ),
        check_vma=False,
    )
```

time: 513 us -> 125 us (0.24); the launches traced: 504 us -> 125 us
  waiting for transfers between devices: 269 us -> 0 us
  Pallas kernels: 0 us -> 119 us
  local copies, waits for them, and re-layouts: 80 us -> 5.12 us
  blocking collectives: 44.5 us -> 0 us
  matrix products: 40.1 us -> 0 us
  other arithmetic: 34.2 us -> 0 us
  starting transfers between devices: 20.8 us -> 0 us
  between operations: 15.1 us -> 0.66 us
    pallas_call x0 -> x1, Pallas kernels: none -> 119 us  [on_device(): pl.pallas_call(step_kernel, out_shape=(jax.ShapeDtypeStruct((64, 32, 128)...]
    all_gather x2 -> x0, waiting for transfers between devices: 118 us -> none  [the longest x1 62.2 us: gathered_total(): return lax.all_gather(array, axis).sum(0)]
    reduce_scatter x1 -> x0, waiting for transfers between devices: 77.5 us -> none  [on_device(): lax.psum_scatter(jnp.einsum('jkc,ikc->jic', right_all, left_side, preferr...]
    all_to_all x4 -> x0, waiting for transfers between devices: 73.6 us -> none  [the longest x2 48.7 us: sent_and_summed(): blocks = lax.all_to_all(split_up(array, dim, size), axis, 0, 0, tiled=True)]
    all_to_all x3 -> x0, blocking collectives: 44.5 us -> none  [the longest x2 31.6 us: sent_to_all(): return lax.all_to_all(copies, axis, split_axis=0, concat_axis=0, tiled=True)]
    dot_general x18 -> x0, matrix products: 38.7 us -> none  [the longest x1 10.3 us: on_device(): jnp.einsum('jkc,ikc->jic', right_all, left_side, preferred_element_type=j...]
    transpose x6 -> x0, local copies, waits for them, and re-layouts: 24.9 us -> none  [the longest x1 16.8 us: on_device(): jnp.einsum('jkc,ikc->jic', right_all, left_side, preferred_element_type=j...]
    unnamed x87 -> x8, local copies, waits for them, and re-layouts: 29.6 us -> 5.12 us
  transfers between devices with their start and end apart: 7 -> 0, of which waited for: 7 -> 0; matrix products, arithmetic and copies ran while one was open for 6% -> 0% of each run, Pallas kernels for 0% -> 0%
where the time goes in v2:
time: 125 us
  Pallas kernels  119 us (95%)
  local copies, waits for them, and re-layouts  5.12 us (4%)
    pallas_call x1, Pallas kernels, on_device(): pl.pallas_call(step_kernel, out_shape=(jax.ShapeDtypeStruct((64, 32, 128)...  119 us
    unnamed x8, local copies, waits for them, and re-layouts  5.12 us

profile of v2, /device:TPU:8, one launch (start us, length us, event | category | flops | bytes accessed | tf_op | source)
XLA Modules:
  0.0 124.7 jit_solution(6912574284181748352)
XLA Ops:
  0.6 118.9 %step.1 = (bf16[64,32,128]{2,1,0:T(8,128)(2,1)}, bf16[8,48,64]{2,1,0:T(8,128)(2,1)}, f32[2048,128]{1,0:T(8,128)}, f32[64,384]{1,0:T(8,128)}) custom-call(s32[512]{0:T(512)} %res_ref.1, s32[512]{0:T(512)} %chain_ref.1, s32[512]{0:T(512)} %mask_ref.1, bf16[64,32,128]{2,1,0:T(8,128)(2,1)} %pair_hbm.1, bf16[66,128]{1,0:T(8,128)(2,1)} %relpos_ref.1, ...), custom_call_target="tpu_custom_call" | custom-call | tf_op jit(solution)/shard_map/step/pallas_call | solution.py:752
  119.6 0.0 copy-start
  119.6 0.0 copy-start.1
  119.6 2.0 %copy.22 = bf16[64,32,128]{2,1,0:T(8,128)(2,1)} copy(bf16[64,32,128]{2,1,0:T(8,128)(2,1)} %get-tuple-element.16) | data formatting | bytes 1048576
  121.5 1.5 %copy.23 = bf16[8,64,48]{1,2,0:T(8,128)(2,1)} copy(bf16[8,64,48]{1,2,0:T(8,128)(2,1)} %bitcast.9) | data formatting | bytes 98304
  123.1 0.0 copy-done
  123.1 1.0 copy.24
  124.1 0.0 copy-done.1
  124.1 0.6 copy.25
Async XLA Ops:
  119.6 3.5 %copy-start = (f32[2048,128]{1,0:T(8,128)S(1)}, f32[2048,128]{1,0:T(8,128)}, u32[]{:S(2)}) copy-start(f32[2048,128]{1,0:T(8,128)} %get-tuple-element.10) | copy-start | bytes 3145732
  119.6 4.5 %copy-start.1 = (f32[64,384]{1,0:T(8,128)S(1)}, f32[64,384]{1,0:T(8,128)}, u32[]{:S(2)}) copy-start(f32[64,384]{1,0:T(8,128)} %get-tuple-element.19) | copy-start | bytes 294916

commit v3 on v2

--- a/solution.py
+++ b/solution.py
@@ -128,9 +128,10 @@
     res_ref, chain_ref, mask_ref,
     pair_hbm, relpos_ref, tri_hbm, triout_ref, biasp_ref, single_ref, ada_hbm, noisy_hbm,
     qkvw_ref, outp_ref, cot_ref,
-    pairout_ref, block_ref, gpair_ref, gsingle_ref,
+    pairout_hbm, block_hbm, gpair_hbm, gsingle_hbm,
+    pairout_ref, block_ref, gpair_ref,
     pair_in, tri_w, ada_w, noisy, idx_r, mrow, relpos_w,
-    pf, gate, lrf, lbuf, recv_a, got, rcat, mtmp, tbuf, got_c, got_d, bias_f, bias_b, bias_got,
+    zl_s, tri_t, pf, gate, lrf, lbuf, recv_a, got, rcat, mtmp, tbuf, got_c, got_d, bias_f, bias_b, bias_got,
     cvec_s, scale_s, shift_s, wg_s, gate_t, g_t, noisy_t, normed, hidden, wqkv, q_t, kv_f,
     kv_own, kv_all, dmx_own, dmx_all, da_t, keyok, sraw, draw,
     mix_s, mix_r, dkv_s, dkv_m, dkv_o, dkv_r, dq_t, dkv_tok, dbias, db_s, db_r,
@@ -202,34 +203,41 @@
         return 0
 
     lax.fori_loop(0, 64, load, 0, unroll=4)
+    bins = lax.broadcasted_iota(jnp.int32, (64, 128), 1)
+
+    def normed_rows(t, _):
+        parts = []
+        for q in range(2):
+            for hi in range(2):
+                j = 2 * t + q + 16 * hi
+                off = jnp.clip(idx_r[0] - res_ref[col * 32 + j] + 32, 0, 64)
+                bucket = jnp.where(idx_r[1] == chain_ref[col * 32 + j], off, REL_BINS - 1)
+                onehot = jnp.where(bucket == bins, 1.0, 0.0).astype(BF16)
+                parts.append(
+                    pf[pl.ds(j, 64, stride=32), :]
+                    + jnp.dot(onehot, relpos_w[...], preferred_element_type=F32)
+                )
+        for q in range(2):
+            for hi in range(2):
+                pf[pl.ds(2 * t + q + 16 * hi, 64, stride=32), :] = parts[2 * q + hi]
+        at = pl.ds(pl.multiple_of(t * 256, 256), 256)
+        zl_s[at, :] = layer_norm(jnp.concatenate(parts, 0), -1).astype(BF16)
+        return 0
+
+    lax.fori_loop(0, 8, normed_rows, 0)
     loads[1].wait()
-    bins = lax.broadcasted_iota(jnp.int32, (64, 128), 1)
-
-    def stage1(lo, _):
-        parts = []
-        for hi in range(2):
-            j = lo + 16 * hi
-            off = jnp.clip(idx_r[0] - res_ref[col * 32 + j] + 32, 0, 64)
-            bucket = jnp.where(idx_r[1] == chain_ref[col * 32 + j], off, REL_BINS - 1)
-            onehot = jnp.where(bucket == bins, 1.0, 0.0).astype(BF16)
-            parts.append(
-                pf[pl.ds(j, 64, stride=32), :]
-                + jnp.dot(onehot, relpos_w[...], preferred_element_type=F32)
+    tri_t[...] = tri_w[:, :512].astype(F32).T.astype(BF16)
+
+    def project(h, t):
+        at = pl.ds(pl.multiple_of(t * 256, 256), 256)
+        pt = dg(tri_t[h * 256 : h * 256 + 256, :], zl_s[at, :], 1, 1)
+        val = jax.nn.sigmoid(pt[128:]) * pt[:128]
+        for q in range(2):
+            lo = 2 * t + q
+            mask = mrow[0:1, :] * jnp.where(
+                low1, mask_ref[col * 32 + lo].astype(F32), mask_ref[col * 32 + 16 + lo].astype(F32)
             )
-            pf[pl.ds(j, 64, stride=32), :] = parts[hi]
-        zl = layer_norm(jnp.concatenate(parts, 0), -1).astype(BF16)
-        pt = dg(tri_w[:, :512], zl, 0, 1)
-        mask = mrow[0:1, :] * jnp.where(
-            low1, mask_ref[col * 32 + lo].astype(F32), mask_ref[col * 32 + 16 + lo].astype(F32)
-        )
-        lrf[pl.ds(lo, 128, stride=16), :] = jax.nn.sigmoid(pt[128:256]) * pt[:128] * mask
-        lrf[pl.ds(2048 + lo, 128, stride=16), :] = (
-            jax.nn.sigmoid(pt[384:512]) * pt[256:384] * mask
-        )
-        gate[lo] = jax.nn.sigmoid(jnp.dot(zl, tri_w[:, 512:], preferred_element_type=F32))
-        return 0
-
-    lax.fori_loop(0, 16, stage1, 0, unroll=2)
+            lrf[pl.ds(h * 2048 + lo, 128, stride=16), :] = val[:, q * 128 : q * 128 + 128] * mask
 
     a_src = [lambda to, h=h: lbuf.at[h, to] for h in range(2)]
     a_slot = [lambda c, h=h: recv_a.at[h, c] for h in range(2)]
@@ -242,6 +250,12 @@
     ]
     for h in range(2):
 
+        def one_side(t, _):
+            project(h, t)
+            return 0
+
+        lax.fori_loop(0, 8, one_side, 0)
+
         def pack(c, _):
             lbuf[h, c] = lrf[pl.ds(h * 2048 + c * 128, 128), :].astype(BF16).reshape(8, 16, 128)
             return 0
@@ -270,32 +284,10 @@
         return 0
 
     lax.fori_loop(0, 8, sample, 0)
-    kv_f[...] = dg(hidden[...], wqkv[64:, :], 1, 1)
-
-    def kv_pack(t, _):
-        r0 = kv_f[pl.ds(t * 32, 16), :]
-        r1 = kv_f[pl.ds(t * 32 + 16, 16), :]
-        to = pl.ds(pl.multiple_of(rmod(t, 2) * 16, 16), 16)
-        kv_own[0, t // 2, to, :] = jnp.where(low16, r0, pltpu.roll(r1, 64, 1)).astype(BF16)
-        kv_own[1, t // 2, to, :] = jnp.where(low16, pltpu.roll(r0, 64, 1), r1).astype(BF16)
-        return 0
-
-    lax.fori_loop(0, 16, kv_pack, 0, unroll=2)
-    kv_keep = pltpu.make_async_copy(kv_own, kv_all.at[row], loc.at[4])
-    kv_keep.start()
-    kv_out = []
-    for o in range(1, 4):
-        to = (rmod(zlo + o, 4) * 2 + core, col, samp)
-        kv_out.append(remote(kv_own, kv_all.at[row], skv.at[o], rkv.at[o], to))
-    kv_mate = remote(kv_own, kv_all.at[row], skf.at[0], rkf.at[0], mate)
-
     own_a[0].wait()
     col_wait(a_src[0], a_slot[0], sa.at[0], ra.at[0])
     own_b[0].start()
     row_start(b_src[0], b_slot[0], sb.at[0], rb.at[0])
-    kv_mate.start()
-    for copy in kv_out:
-        copy.start()
 
     feat = lax.broadcasted_iota(jnp.int32, (768, 64), 1)
     sel = jnp.where(
@@ -316,12 +308,42 @@
         dmx_own[:, u * 128 : u * 128 + 128] = (g * gate_t[:48, :]).astype(BF16)
     dm_src, dm_slot = (lambda to: dmx_own), (lambda c: dmx_all.at[c])
     dm_keep = pltpu.make_async_copy(dmx_own, dmx_all.at[col], loc.at[5])
+    dm_keep.start()
+    col_start(dm_src, dm_slot, sdm, rdm)
+    kv_f[...] = dg(hidden[...], wqkv[64:, :], 1, 1)
+
+    def kv_pack(t, _):
+        r0 = kv_f[pl.ds(t * 32, 16), :]
+        r1 = kv_f[pl.ds(t * 32 + 16, 16), :]
+        to = pl.ds(pl.multiple_of(rmod(t, 2) * 16, 16), 16)
+        kv_own[0, t // 2, to, :] = jnp.where(low16, r0, pltpu.roll(r1, 64, 1)).astype(BF16)
+        kv_own[1, t // 2, to, :] = jnp.where(low16, pltpu.roll(r0, 64, 1), r1).astype(BF16)
+        return 0
+
+    lax.fori_loop(0, 16, kv_pack, 0, unroll=2)
+    kv_keep = pltpu.make_async_copy(kv_own, kv_all.at[row], loc.at[4])
+    kv_keep.start()
+    kv_out = []
+    for o in range(1, 4):
+        to = (rmod(zlo + o, 4) * 2 + core, col, samp)
+        kv_out.append(remote(kv_own, kv_all.at[row], skv.at[o], rkv.at[o], to))
+    kv_mate = remote(kv_own, kv_all.at[row], skf.at[0], rkf.at[0], mate)
     own_a[1].wait()
     col_wait(a_src[1], a_slot[1], sa.at[1], ra.at[1])
     own_b[1].start()
     row_start(b_src[1], b_slot[1], sb.at[1], rb.at[1])
-    dm_keep.start()
-    col_start(dm_src, dm_slot, sdm, rdm)
+    kv_mate.start()
+    for copy in kv_out:
+        copy.start()
+
+    def gates(t, _):
+        at = pl.ds(pl.multiple_of(t * 256, 256), 256)
+        gate[at, :] = jax.nn.sigmoid(
+            jnp.dot(zl_s[at, :], tri_w[:, 512:], preferred_element_type=F32)
+        )
+        return 0
+
+    lax.fori_loop(0, 8, gates, 0)
     q_t[...] = dg(wqkv[:64, :], hidden[...], 1, 1)
     noisy_t[...] = dg(sel, noisy[...], 0, 1)
 
@@ -348,7 +370,9 @@
 
     lax.fori_loop(0, 8, turn, 0)
 
-    def tri(rp, _):
+    c_src, c_slot = (lambda r: tbuf.at[r]), (lambda r: got_c.at[r])
+
+    def tri(rp):
         rhs = jnp.concatenate(
             [got[0, 2 * rp].reshape(256, 128), got[0, 2 * rp + 1].reshape(256, 128)], 1
         )
@@ -370,15 +394,17 @@
             return 0
 
         lax.fori_loop(0, 8, out, 0, unroll=2)
-        return 0
-
-    lax.fori_loop(0, 4, tri, 0)
-
-    c_src, c_slot = (lambda r: tbuf.at[r]), (lambda r: got_c.at[r])
+
+    own_c = pltpu.make_async_copy(tbuf.at[row], got_c.at[row], loc.at[6])
+    for oz in (2, 1, 3, 0):
+        tri(rmod(zlo + oz, 4))
+        for cx in range(2):
+            if (oz, cx) != (0, 0):
+                to = row_dest(oz, cx)
+                i = oz * 2 + cx
+                remote(c_src(to[0]), c_slot(row), sc.at[i], rc.at[i], to).start()
+    own_c.start()
     d_src, d_slot = (lambda c: got_c.at[:, c]), (lambda c: got_d.at[c])
-    own_c = pltpu.make_async_copy(tbuf.at[row], got_c.at[row], loc.at[6])
-    own_c.start()
-    row_start(c_src, c_slot, sc, rc)
 
     for o in range(1, 4):
         came = rmod(zlo + 4 - o, 4) * 2 + core
@@ -439,7 +465,7 @@
 
     def stage3(lo, _):
         tn = layer_norm(lrf[pl.ds(lo, 128, stride=16), :], 0).astype(BF16)
-        upd = dg(tn, triout_ref[...], 0, 0) * gate[lo]
+        upd = dg(tn, triout_ref[...], 0, 0) * gate[pl.ds(pl.multiple_of(lo * 128, 128), 128), :]
         outs = []
         for hi in range(2):
             at = pl.ds(lo + 16 * hi, 64, stride=32)
@@ -461,6 +487,8 @@
         return 0
 
     lax.fori_loop(0, 64, store, 0, unroll=4)
+    out_pair = pltpu.make_async_copy(pairout_ref, pairout_hbm, loc.at[14])
+    out_pair.start()
     dbias[...] = jnp.zeros_like(dbias)
     own_e.wait()
     col_wait(e_src, e_slot, se, re)
@@ -575,6 +603,8 @@
         return 0
 
     lax.fori_loop(0, 4, mixed_of, 0)
+    out_block = pltpu.make_async_copy(block_ref, block_hbm, loc.at[15])
+    out_block.start()
 
     dsc[...] = jnp.zeros_like(dsc)
     dsh[...] = jnp.zeros_like(dsh)
@@ -638,6 +668,34 @@
 
     lax.fori_loop(1, 8, part_send, 0)
 
+    own_db.wait()
+    col_wait(near_src, near_slot, sbb.at[0], rbb.at[0])
+
+    def db_wait(o, _):
+        came = rmod(col + NCOL - o, NCOL)
+        remote(db_s.at[came], db_r.at[1 - samp, came], sbb.at[1, o], rbb.at[1, o], far).wait_recv()
+        db_copy(o).wait_send()
+        return 0
+
+    lax.fori_loop(0, NCOL, db_wait, 0)
+    dbias[...] = (db_r[0] + db_r[1]).reshape(256, 128)
+    biasp3 = jnp.concatenate([biasp_ref[...]] * 3, 0)
+
+    def grad(lo, _):
+        d = dbias[pl.ds(lo, 16, stride=16), :]
+        d1 = d.astype(BF16)
+        rest = d - d1.astype(F32)
+        d2 = rest.astype(BF16)
+        d3 = (rest - d2.astype(F32)).astype(BF16)
+        g = dg(jnp.concatenate([d1, d2, d3], 0), biasp3, 0, 0)
+        for hi in range(2):
+            gpair_ref[pl.ds(lo + 16 * hi, 64, stride=32), :] = g[hi * 64 : hi * 64 + 64]
+        return 0
+
+    lax.fori_loop(0, 16, grad, 0, unroll=2)
+    out_grad = pltpu.make_async_copy(gpair_ref, gpair_hbm, loc.at[16])
+    out_grad.start()
+
     def own_copy(o):
         return remote(
             gs_own, gs_all.at[half_col], sg.at[o], rg.at[half_col], (row, rmod(col + o, NCOL), samp)
@@ -681,32 +739,6 @@
         lax.fori_loop(1, NCOL, tell, 0)
         gs_all[half_col] = gs_own[...]
 
-    own_db.wait()
-    col_wait(near_src, near_slot, sbb.at[0], rbb.at[0])
-
-    def db_wait(o, _):
-        came = rmod(col + NCOL - o, NCOL)
-        remote(db_s.at[came], db_r.at[1 - samp, came], sbb.at[1, o], rbb.at[1, o], far).wait_recv()
-        db_copy(o).wait_send()
-        return 0
-
-    lax.fori_loop(0, NCOL, db_wait, 0)
-    dbias[...] = (db_r[0] + db_r[1]).reshape(256, 128)
-    biasp3 = jnp.concatenate([biasp_ref[...]] * 3, 0)
-
-    def grad(lo, _):
-        d = dbias[pl.ds(lo, 16, stride=16), :]
-        d1 = d.astype(BF16)
-        rest = d - d1.astype(F32)
-        d2 = rest.astype(BF16)
-        d3 = (rest - d2.astype(F32)).astype(BF16)
-        g = dg(jnp.concatenate([d1, d2, d3], 0), biasp3, 0, 0)
-        for hi in range(2):
-            gpair_ref[pl.ds(lo + 16 * hi, 64, stride=32), :] = g[hi * 64 : hi * 64 + 64]
-        return 0
-
-    lax.fori_loop(0, 16, grad, 0, unroll=2)
-
     @pl.when(jnp.logical_not(even))
     def _():
         part_copy(0).wait_send()
@@ -737,7 +769,39 @@
         return 0
 
     lax.fori_loop(1, 8, came_from, 0)
-    gsingle_ref[...] = gs_all[...].reshape(64, 384)
+    out_single = pltpu.make_async_copy(gs_all, gsingle_hbm, loc.at[17])
+    out_single.start()
+    for copy in (out_pair, out_block, out_grad, out_single):
+        copy.wait()
+
+
+def finish_kernel(*refs):
+    n = 4
+    ins, outs, bufs = refs[:n], refs[n : 2 * n], refs[2 * n : 3 * n]
+    got, put = refs[3 * n], refs[3 * n + 1]
+    reads = [pltpu.make_async_copy(ins[i], bufs[i], got.at[i]) for i in range(n)]
+    writes = [pltpu.make_async_copy(bufs[i], outs[i], put.at[i]) for i in range(n)]
+    for copy in reads:
+        copy.start()
+    for i in (3, 1, 0, 2):
+        reads[i].wait()
+        writes[i].start()
+    for copy in writes:
+        copy.wait()
+
+
+def finished(arrays):
+    hbm = pl.BlockSpec(memory_space=pl.ANY)
+    return pl.pallas_call(
+        finish_kernel,
+        out_shape=[jax.ShapeDtypeStruct(x.shape, x.dtype) for x in arrays],
+        in_specs=[hbm] * 4,
+        out_specs=[hbm] * 4,
+        scratch_shapes=[pltpu.VMEM(x.shape, x.dtype) for x in arrays]
+        + [pltpu.SemaphoreType.DMA((4,)), pltpu.SemaphoreType.DMA((4,))],
+        compiler_params=pltpu.CompilerParams(vmem_limit_bytes=60 * 1024 * 1024),
+        name="finish",
+    )(*arrays)
 
 
 def on_device(
@@ -755,14 +819,16 @@
             jax.ShapeDtypeStruct((64, 32, 128), BF16),
             jax.ShapeDtypeStruct((8, 48, 64), BF16),
             jax.ShapeDtypeStruct((2048, 128), F32),
-            jax.ShapeDtypeStruct((64, 384), F32),
+            jax.ShapeDtypeStruct((8, 8, 384), F32),
         ),
         in_specs=[sm, sm, sm, hbm, vm, hbm, vm, vm, vm, hbm, hbm, vm, vm, vm],
-        out_specs=(vm,) * 4,
+        out_specs=(hbm,) * 4,
         scratch_shapes=[
+            v((64, 32, 128), BF16), v((8, 48, 64), BF16), v((2048, 128), F32),
             v((64, 32, 128), BF16), v((128, 640), BF16), v((384, 2304), BF16), v((512, 768), BF16),
             v((2, 64, 128), jnp.int32), v((128, 128), F32), v((128, 128), BF16),
-            v((2048, 128), F32), v((16, 128, 128), F32), v((4096, 128), F32),
+            v((2048, 128), BF16), v((512, 128), BF16), v((2048, 128), F32), v((2048, 128), F32),
+            v((4096, 128), F32),
             v((2, 16, 8, 16, 128), BF16), v((2, 16, 8, 16, 128), BF16),
             v((2, 8, 16, 16, 128), BF16), v((1024, 256), BF16), v((1024, 256), F32),
             v((8, 16, 16, 128), BF16), v((8, 16, 16, 128), BF16), v((16, 8, 16, 128), BF16),
@@ -784,7 +850,7 @@
             dma((4,)), dma((4,)), dma((16,)), dma((16,)),
             dma((4, 16)), dma((4, 16)), dma((4,)), dma((4,)), dma((4, 4)), dma((4, 4)),
             dma((2, 16)), dma((2, 16)), dma((8,)), dma((16,)), dma((1,)), dma((1,)),
-            dma((16,)), dma((8,)), dma((14,)), dma((4,)),
+            dma((16,)), dma((8,)), dma((18,)), dma((4,)),
         ],
         compiler_params=pltpu.CompilerParams(
             collective_id=1, has_side_effects=True, vmem_limit_bytes=60 * 1024 * 1024
@@ -795,7 +861,15 @@
         bias_proj.T, single, ada_proj, noisy.reshape(512, 768), qkv_proj.transpose(1, 2, 0),
         out_proj, cotangent.transpose(0, 2, 1),
     )
-    return pair_out, block_t.transpose(0, 2, 1), grad_pair.reshape(64, 32, 128), grad_single
+    pair_out, block_t, grad_pair, grad_single = finished(
+        (pair_out, block_t, grad_pair, grad_single)
+    )
+    return (
+        pair_out,
+        block_t.transpose(0, 2, 1),
+        grad_pair.reshape(64, 32, 128),
+        grad_single.reshape(64, 384),
+    )
 
 
 def solution(mesh):

time: 125 us -> 117 us (0.936)
  local copies, waits for them, and re-layouts: 5.12 us -> 0 us
  Pallas kernels: 119 us -> 116 us
    pallas_call x1, Pallas kernels: 119 us -> 113 us  [on_device(): pl.pallas_call(step_kernel, out_shape=(jax.ShapeDtypeStruct((64, 32, 128)...]
    unnamed x8 -> x0, local copies, waits for them, and re-layouts: 5.12 us -> none
    pallas_call x0 -> x1, Pallas kernels: none -> 2.67 us  [finished(): pl.pallas_call(finish_kernel, out_shape=[jax.ShapeDtypeStruct(x.shape, x....]
where the time goes in v3:
time: 117 us
  Pallas kernels  116 us (99%)
    pallas_call x1, Pallas kernels, on_device(): pl.pallas_call(step_kernel, out_shape=(jax.ShapeDtypeStruct((64, 32, 128)...  113 us
    pallas_call x1, Pallas kernels, finished(): pl.pallas_call(finish_kernel, out_shape=[jax.ShapeDtypeStruct(x.shape, x....  2.67 us

profile of v3, /device:TPU:8, one launch (start us, length us, event | category | flops | bytes accessed | tf_op | source)
XLA Modules:
  0.0 116.7 jit_solution(6368584569256801275)
XLA Ops:
  0.6 113.4 %step.1 = (bf16[64,32,128]{2,1,0:T(8,128)(2,1)}, bf16[8,48,64]{2,1,0:T(8,128)(2,1)}, f32[2048,128]{1,0:T(8,128)}, f32[8,8,384]{2,1,0:T(8,128)}) custom-call(s32[512]{0:T(512)} %res_ref.1, s32[512]{0:T(512)} %chain_ref.1, s32[512]{0:T(512)} %mask_ref.1, bf16[64,32,128]{2,1,0:T(8,128)(2,1)} %pair_hbm.1, bf16[66,128]{1,0:T(8,128)(2,1)} %relpos_ref.1, ...), custom_call_target="tpu_custom_call" | custom-call | tf_op jit(solution)/shard_map/step/pallas_call | solution.py:816
  114.0 2.7 %finish.1 = (bf16[64,32,128]{2,1,0:T(8,128)(2,1)}, bf16[8,48,64]{2,1,0:T(8,128)(2,1)}, f32[2048,128]{1,0:T(8,128)}, f32[8,8,384]{2,1,0:T(8,128)}) custom-call(bf16[64,32,128]{2,1,0:T(8,128)(2,1)} %get-tuple-element.12.refs_0_, bf16[8,48,64]{2,1,0:T(8,128)(2,1)} %get-tuple-element.13.refs_1_, f32[2048,128]{1,0:T(8,128)} %get-tuple-element.14.refs_2_, ...), custom_call_target="tpu_custom_call" | custom-call | tf_op jit(solution)/shard_map/finish/pallas_call | solution.py:795

commit v4 on v3

--- a/solution.py
+++ b/solution.py
@@ -126,11 +126,12 @@
 
 def step_kernel(
     res_ref, chain_ref, mask_ref,
-    pair_hbm, relpos_ref, tri_hbm, triout_ref, biasp_ref, single_ref, ada_hbm, noisy_hbm,
-    qkvw_ref, outp_ref, cot_ref,
+    pair_hbm, relpos_hbm, tri_hbm, triout_hbm, biasp_hbm, single_hbm, ada_hbm, noisy_hbm,
+    qkvw_hbm, outp_hbm, cot_hbm,
     pairout_hbm, block_hbm, gpair_hbm, gsingle_hbm,
     pairout_ref, block_ref, gpair_ref,
-    pair_in, tri_w, ada_w, noisy, idx_r, mrow, relpos_w,
+    pair_in, tri_w, ada_w, noisy, relpos_ref, triout_ref, biasp_ref, single_ref, qkvw_ref, outp_ref,
+    cot_ref, idx_r, mrow, relpos_w,
     zl_s, tri_t, pf, gate, lrf, lbuf, recv_a, got, rcat, mtmp, tbuf, got_c, got_d, bias_f, bias_b, bias_got,
     cvec_s, scale_s, shift_s, wg_s, gate_t, g_t, noisy_t, normed, hidden, wqkv, q_t, kv_f,
     kv_own, kv_all, dmx_own, dmx_all, da_t, keyok, sraw, draw,
@@ -147,9 +148,14 @@
     barrier = pltpu.get_barrier_semaphore()
 
     loads = [
-        pltpu.make_async_copy(s, d, loc.at[10 + i])
+        pltpu.make_async_copy(s, d, loc.at[18 + i])
         for i, (s, d) in enumerate(
-            [(pair_hbm, pair_in), (tri_hbm, tri_w), (ada_hbm, ada_w), (noisy_hbm, noisy)]
+            [
+                (pair_hbm, pair_in), (relpos_hbm, relpos_ref), (tri_hbm, tri_w),
+                (single_hbm, single_ref), (qkvw_hbm, qkvw_ref), (ada_hbm, ada_w),
+                (noisy_hbm, noisy), (cot_hbm, cot_ref), (triout_hbm, triout_ref),
+                (biasp_hbm, biasp_ref), (outp_hbm, outp_ref),
+            ]
         )
     ]
     for copy in loads:
@@ -195,6 +201,7 @@
     lax.fori_loop(0, 64, indices, 0, unroll=4)
     mrow[...] = mrow[...].T
     relpos_w[...] = jnp.zeros_like(relpos_w)
+    loads[1].wait()
     relpos_w[0:REL_BINS, :] = relpos_ref[...]
     loads[0].wait()
 
@@ -224,8 +231,8 @@
         zl_s[at, :] = layer_norm(jnp.concatenate(parts, 0), -1).astype(BF16)
         return 0
 
-    lax.fori_loop(0, 8, normed_rows, 0)
-    loads[1].wait()
+    lax.fori_loop(0, 8, normed_rows, 0, unroll=2)
+    loads[2].wait()
     tri_t[...] = tri_w[:, :512].astype(F32).T.astype(BF16)
 
     def project(h, t):
@@ -266,15 +273,17 @@
         own_a[h].start()
         col_start(a_src[h], a_slot[h], sa.at[h], ra.at[h])
 
+    for copy in loads[3:6]:
+        copy.wait()
     cvec = layer_norm(single_ref[...].astype(F32), -1).astype(BF16)
     cvec_s[...] = cvec
     wqkv[...] = jnp.zeros_like(wqkv)
     for p in range(3):
         wqkv[p * 64 : p * 64 + 48, :] = qkvw_ref[p]
-    loads[2].wait()
     scale_s[...] = jax.nn.sigmoid(jnp.dot(cvec, ada_w[:, :768], preferred_element_type=F32))
     shift_s[...] = jnp.dot(cvec, ada_w[:, 768:1536], preferred_element_type=F32)
-    loads[3].wait()
+    for copy in loads[6:]:
+        copy.wait()
 
     def sample(s, _):
         at = pl.ds(pl.multiple_of(s * 64, 64), 64)
@@ -332,9 +341,6 @@
     col_wait(a_src[1], a_slot[1], sa.at[1], ra.at[1])
     own_b[1].start()
     row_start(b_src[1], b_slot[1], sb.at[1], rb.at[1])
-    kv_mate.start()
-    for copy in kv_out:
-        copy.start()
 
     def gates(t, _):
         at = pl.ds(pl.multiple_of(t * 256, 256), 256)
@@ -344,20 +350,6 @@
         return 0
 
     lax.fori_loop(0, 8, gates, 0)
-    q_t[...] = dg(wqkv[:64, :], hidden[...], 1, 1)
-    noisy_t[...] = dg(sel, noisy[...], 0, 1)
-
-    def key_mask(t, _):
-        jb, lo = t // 16, rmod(t, 16)
-        keyok[pl.ds(t, 1), :] = jnp.where(
-            low1,
-            mask_ref[jb * 32 + lo].astype(F32),
-            mask_ref[jb * 32 + 16 + lo].astype(F32),
-        )
-        return 0
-
-    lax.fori_loop(0, 256, key_mask, 0, unroll=4)
-
     for h in (1, 0):
         own_b[h].wait()
         row_wait(b_src[h], b_slot[h], sb.at[h], rb.at[h])
@@ -404,12 +396,10 @@
                 i = oz * 2 + cx
                 remote(c_src(to[0]), c_slot(row), sc.at[i], rc.at[i], to).start()
     own_c.start()
+    kv_mate.start()
+    for copy in kv_out:
+        copy.start()
     d_src, d_slot = (lambda c: got_c.at[:, c]), (lambda c: got_d.at[c])
-
-    for o in range(1, 4):
-        came = rmod(zlo + 4 - o, 4) * 2 + core
-        remote(kv_own, kv_all.at[came], skv.at[o], rkv.at[o], mate).wait_recv()
-        remote(kv_all.at[came], kv_all.at[came], skf.at[o], rkf.at[o], mate).start()
 
     dm_keep.wait()
     col_wait(dm_src, dm_slot, sdm, rdm)
@@ -425,6 +415,72 @@
     own_d.start()
     col_start(d_src, d_slot, sd, rd)
 
+    q_t[...] = dg(wqkv[:64, :], hidden[...], 1, 1)
+    noisy_t[...] = dg(sel, noisy[...], 0, 1)
+
+    def key_mask(t, _):
+        jb, lo = t // 16, rmod(t, 16)
+        keyok[pl.ds(t, 1), :] = jnp.where(
+            low1,
+            mask_ref[jb * 32 + lo].astype(F32),
+            mask_ref[jb * 32 + 16 + lo].astype(F32),
+        )
+        return 0
+
+    lax.fori_loop(0, 256, key_mask, 0, unroll=4)
+
+    for o in range(1, 4):
+        came = rmod(zlo + 4 - o, 4) * 2 + core
+        remote(kv_own, kv_all.at[came], skv.at[o], rkv.at[o], mate).wait_recv()
+        remote(kv_all.at[came], kv_all.at[came], skf.at[o], rkf.at[o], mate).start()
+
+
+    def half_of(ref, u, sh):
+        tile = ref[:, pl.ds(pl.multiple_of(u * 128, 128), 128)].astype(F32)
+        return blockdiag(both(tile, low, sh == 0))
+
+    def keys(which, s):
+        return jnp.concatenate([kv_all[r, which, s] for r in range(NROW)], 0)
+
+    def raw(u, _):
+        for sh in range(2):
+            s = 2 * u + sh
+            sraw[s] = jnp.dot(keys(0, s), half_of(q_t, u, sh), preferred_element_type=F32)
+            draw[s] = jnp.dot(keys(1, s), half_of(da_t, u, sh), preferred_element_type=F32)
+        return 0
+
+    own_d.wait()
+    col_wait(d_src, d_slot, sd, rd)
+
+    def widen(c, _):
+        lrf[pl.ds(c * 128, 128), :] = got_d[c].reshape(128, 128).astype(F32)
+        return 0
+
+    lax.fori_loop(0, 16, widen, 0)
+
+    def stage3(t, _):
+        tn = layer_norm(
+            jnp.concatenate([lrf[pl.ds(2 * t + q, 128, stride=16), :] for q in range(2)], 1), 0
+        ).astype(BF16)
+        upd = dg(tn, triout_ref[...], 0, 0) * gate[pl.ds(pl.multiple_of(t * 256, 256), 256), :]
+        spots = [pl.ds(2 * t + q + 16 * hi, 64, stride=32) for q in range(2) for hi in range(2)]
+        outs = [
+            (pf[at, :] + upd[i * 64 : i * 64 + 64]).astype(BF16) for i, at in enumerate(spots)
+        ]
+        for at, val in zip(spots, outs):
+            pf[at, :] = val.astype(F32)
+        tile = dg(biasp_ref[...], jnp.concatenate(outs, 0), 1, 1)
+        for q in range(2):
+            bias_f[pl.ds(2 * t + q, 16, stride=16), :] = tile[:, q * 128 : q * 128 + 128]
+        return 0
+
+    lax.fori_loop(0, 8, stage3, 0, unroll=2)
+    bias_b[...] = bias_f[...].astype(BF16).reshape(16, 16, 128)
+    e_src, e_slot = (lambda c: bias_b.at[c]), (lambda c: bias_got.at[c])
+    own_e = pltpu.make_async_copy(bias_b.at[col], bias_got.at[col], loc.at[8])
+    own_e.start()
+    col_start(e_src, e_slot, se, re)
+
     kv_keep.wait()
     for copy in kv_out:
         copy.wait_send()
@@ -438,50 +494,7 @@
             remote(
                 kv_all.at[came + core], kv_all.at[came + core], skf.at[o], rkf.at[o], mate
             ).wait_send()
-
-    def half_of(ref, u, sh):
-        tile = ref[:, pl.ds(pl.multiple_of(u * 128, 128), 128)].astype(F32)
-        return blockdiag(both(tile, low, sh == 0))
-
-    def keys(which, s):
-        return jnp.concatenate([kv_all[r, which, s] for r in range(NROW)], 0)
-
-    def raw(u, _):
-        for sh in range(2):
-            s = 2 * u + sh
-            sraw[s] = jnp.dot(keys(0, s), half_of(q_t, u, sh), preferred_element_type=F32)
-            draw[s] = jnp.dot(keys(1, s), half_of(da_t, u, sh), preferred_element_type=F32)
-        return 0
-
     lax.fori_loop(0, 4, raw, 0)
-    own_d.wait()
-    col_wait(d_src, d_slot, sd, rd)
-
-    def widen(c, _):
-        lrf[pl.ds(c * 128, 128), :] = got_d[c].reshape(128, 128).astype(F32)
-        return 0
-
-    lax.fori_loop(0, 16, widen, 0)
-
-    def stage3(lo, _):
-        tn = layer_norm(lrf[pl.ds(lo, 128, stride=16), :], 0).astype(BF16)
-        upd = dg(tn, triout_ref[...], 0, 0) * gate[pl.ds(pl.multiple_of(lo * 128, 128), 128), :]
-        outs = []
-        for hi in range(2):
-            at = pl.ds(lo + 16 * hi, 64, stride=32)
-            val = (pf[at, :] + upd[hi * 64 : hi * 64 + 64]).astype(BF16)
-            pf[at, :] = val.astype(F32)
-            outs.append(val)
-        bias_f[pl.ds(lo, 16, stride=16), :] = dg(biasp_ref[...], jnp.concatenate(outs, 0), 1, 1)
-        return 0
-
-    lax.fori_loop(0, 16, stage3, 0, unroll=2)
-    bias_b[...] = bias_f[...].astype(BF16).reshape(16, 16, 128)
-    e_src, e_slot = (lambda c: bias_b.at[c]), (lambda c: bias_got.at[c])
-    own_e = pltpu.make_async_copy(bias_b.at[col], bias_got.at[col], loc.at[8])
-    own_e.start()
-    col_start(e_src, e_slot, se, re)
-
     def store(i, _):
         pairout_ref[i] = pf[pl.ds(i * 32, 32), :].astype(BF16)
         return 0
@@ -568,7 +581,7 @@
 
     lax.fori_loop(0, 4, pair_of_samples, 0)
 
-    db_s[...] = dbias[...].reshape(16, 16, 128)
+    db_s[...] = dbias[...].astype(BF16).reshape(16, 16, 128)
     own_db = pltpu.make_async_copy(db_s.at[col], db_r.at[samp, col], loc.at[9])
     own_db.start()
 
@@ -602,9 +615,7 @@
         dga[:48, :] += g_t[u] * total
         return 0
 
-    lax.fori_loop(0, 4, mixed_of, 0)
-    out_block = pltpu.make_async_copy(block_ref, block_hbm, loc.at[15])
-    out_block.start()
+    lax.fori_loop(0, 3, mixed_of, 0)
 
     dsc[...] = jnp.zeros_like(dsc)
     dsh[...] = jnp.zeros_like(dsh)
@@ -639,7 +650,11 @@
         dsh[...] += dh[:64] + dh[64:]
         return 0
 
-    lax.fori_loop(0, 4, hidden_grad, 0)
+    lax.fori_loop(0, 3, hidden_grad, 0)
+    mixed_of(3, 0)
+    out_block = pltpu.make_async_copy(block_ref, block_hbm, loc.at[15])
+    out_block.start()
+    hidden_grad(3, 0)
     sg_ = scale_s[...]
     part = dg(two_parts(dsc[...] * sg_ * (1.0 - sg_)), ada_w[:, :768], 1, 1)
     part = part + dg(two_parts(dsh[...]), ada_w[:, 768:1536], 1, 1)
@@ -678,7 +693,7 @@
         return 0
 
     lax.fori_loop(0, NCOL, db_wait, 0)
-    dbias[...] = (db_r[0] + db_r[1]).reshape(256, 128)
+    dbias[...] = (db_r[0].astype(F32) + db_r[1].astype(F32)).reshape(256, 128)
     biasp3 = jnp.concatenate([biasp_ref[...]] * 3, 0)
 
     def grad(lo, _):
@@ -808,7 +823,6 @@
     pair_in, residue_index, chain_index, token_mask, relpos_weight, tri_proj, tri_out, bias_proj,
     single, ada_proj, noisy, qkv_proj, out_proj, cotangent,
 ):
-    vm = pl.BlockSpec(memory_space=pltpu.VMEM)
     sm = pl.BlockSpec(memory_space=pltpu.SMEM)
     hbm = pl.BlockSpec(memory_space=pl.ANY)
     dma = pltpu.SemaphoreType.DMA
@@ -821,11 +835,13 @@
             jax.ShapeDtypeStruct((2048, 128), F32),
             jax.ShapeDtypeStruct((8, 8, 384), F32),
         ),
-        in_specs=[sm, sm, sm, hbm, vm, hbm, vm, vm, vm, hbm, hbm, vm, vm, vm],
+        in_specs=[sm] * 3 + [hbm] * 11,
         out_specs=(hbm,) * 4,
         scratch_shapes=[
             v((64, 32, 128), BF16), v((8, 48, 64), BF16), v((2048, 128), F32),
             v((64, 32, 128), BF16), v((128, 640), BF16), v((384, 2304), BF16), v((512, 768), BF16),
+            v((REL_BINS, 128), BF16), v((128, 128), BF16), v((16, 128), BF16), v((64, 384), BF16),
+            v((3, 48, 768), BF16), v((48, 768), BF16), v((8, 48, 64), BF16),
             v((2, 64, 128), jnp.int32), v((128, 128), F32), v((128, 128), BF16),
             v((2048, 128), BF16), v((512, 128), BF16), v((2048, 128), F32), v((2048, 128), F32),
             v((4096, 128), F32),
@@ -841,8 +857,8 @@
             v((8, 256, 128), F32),
             v((4, 16, 48, 128), BF16), v((4, 16, 48, 128), BF16), v((4, 2, 4, 4, 32, 128), BF16),
             v((4, 4, 4, 32, 128), BF16), v((4, 4, 4, 32, 128), BF16), v((4, 4, 4, 32, 128), BF16),
-            v((4, 64, 128), BF16), v((128, 128), BF16), v((256, 128), F32), v((16, 16, 128), F32),
-            v((2, 16, 16, 128), F32),
+            v((4, 64, 128), BF16), v((128, 128), BF16), v((256, 128), F32), v((16, 16, 128), BF16),
+            v((2, 16, 16, 128), BF16),
             v((64, 768), F32), v((64, 768), F32), v((64, 128), F32), v((8, 8, 384), F32),
             v((16, 8, 384), F32), v((2, 8, 384), F32), v((8, 384), F32), v((8, 8, 384), F32),
             dma((2, 16)), dma((2, 16)), dma((2, 8)), dma((2, 8)), dma((8,)), dma((8,)),
@@ -850,7 +866,7 @@
             dma((4,)), dma((4,)), dma((16,)), dma((16,)),
             dma((4, 16)), dma((4, 16)), dma((4,)), dma((4,)), dma((4, 4)), dma((4, 4)),
             dma((2, 16)), dma((2, 16)), dma((8,)), dma((16,)), dma((1,)), dma((1,)),
-            dma((16,)), dma((8,)), dma((18,)), dma((4,)),
+            dma((16,)), dma((8,)), dma((29,)), dma((4,)),
         ],
         compiler_params=pltpu.CompilerParams(
             collective_id=1, has_side_effects=True, vmem_limit_bytes=60 * 1024 * 1024

time: 117 us -> 108 us (0.923)
  Pallas kernels: 116 us -> 107 us
    pallas_call x1, Pallas kernels: 113 us -> 105 us  [on_device(): pl.pallas_call(step_kernel, out_shape=(jax.ShapeDtypeStruct((64, 32, 128)...]
where the time goes in v4:
time: 108 us
  Pallas kernels  107 us (99%)
    pallas_call x1, Pallas kernels, on_device(): pl.pallas_call(step_kernel, out_shape=(jax.ShapeDtypeStruct((64, 32, 128)...  105 us
    pallas_call x1, Pallas kernels, finished(): pl.pallas_call(finish_kernel, out_shape=[jax.ShapeDtypeStruct(x.shape, x....  2.67 us

profile of v4, /device:TPU:8, one launch (start us, length us, event | category | flops | bytes accessed | tf_op | source)
XLA Modules:
  0.0 107.9 jit_solution(2209640788239258880)
XLA Ops:
  0.6 104.6 %step.1 = (bf16[64,32,128]{2,1,0:T(8,128)(2,1)}, bf16[8,48,64]{2,1,0:T(8,128)(2,1)}, f32[2048,128]{1,0:T(8,128)}, f32[8,8,384]{2,1,0:T(8,128)}) custom-call(s32[512]{0:T(512)} %res_ref.1, s32[512]{0:T(512)} %chain_ref.1, s32[512]{0:T(512)} %mask_ref.1, bf16[64,32,128]{2,1,0:T(8,128)(2,1)} %pair_hbm.1, bf16[66,128]{1,0:T(8,128)(2,1)} %relpos_hbm.1, ...), custom_call_target="tpu_custom_call" | custom-call | tf_op jit(solution)/shard_map/step/pallas_call | solution.py:830
  105.2 2.7 %finish.1 = (bf16[64,32,128]{2,1,0:T(8,128)(2,1)}, bf16[8,48,64]{2,1,0:T(8,128)(2,1)}, f32[2048,128]{1,0:T(8,128)}, f32[8,8,384]{2,1,0:T(8,128)}) custom-call(bf16[64,32,128]{2,1,0:T(8,128)(2,1)} %get-tuple-element.12.refs_0_, bf16[8,48,64]{2,1,0:T(8,128)(2,1)} %get-tuple-element.13.refs_1_, f32[2048,128]{1,0:T(8,128)} %get-tuple-element.14.refs_2_, ...), custom_call_target="tpu_custom_call" | custom-call | tf_op jit(solution)/shard_map/finish/pallas_call | solution.py:810

commit v5 on v4

--- a/solution.py
+++ b/solution.py
@@ -27,9 +27,9 @@
     return lax.rem(a, n)
 
 
-def ring_shift(oz, dest_core):
+def ring_shift(oz, from_core):
     if oz == 2:
-        return 2 + 4 * dest_core
+        return 2 + 4 * from_core
     return (0, 1, None, 7)[oz]
 
 
@@ -37,7 +37,7 @@
     row, col, samp = place()
     z, core = samp * 4 + row // 2, rmod(row, 2)
     to_core = rmod(core + cx, 2)
-    to_z = rmod(z + ring_shift(oz, to_core), 8)
+    to_z = rmod(z + ring_shift(oz, core), 8)
     return rmod(to_z, 4) * 2 + to_core, col, to_z // 4
 
 
@@ -45,8 +45,12 @@
     row, col, samp = place()
     z, core = samp * 4 + row // 2, rmod(row, 2)
     from_core = rmod(core + cx, 2)
-    from_z = rmod(z + 8 - ring_shift(oz, core), 8)
+    from_z = rmod(z + 8 - ring_shift(oz, from_core), 8)
     return rmod(from_z, 4) * 2 + from_core, col, from_z // 4
+
+
+def spot(row):
+    return rmod(row, 2) * 4 + row // 2
 
 
 ROW_IDS = [(oz, cx) for oz in range(4) for cx in range(2) if (oz, cx) != (0, 0)]
@@ -110,6 +114,10 @@
 def both(x, low, first):
     turned = pltpu.roll(x, 64, 1)
     return jnp.where(low, x, turned) if first else jnp.where(low, turned, x)
+
+
+def sigmoid(x):
+    return 0.5 * jnp.tanh(0.5 * x) + 0.5
 
 
 def layer_norm(x, axis):
@@ -138,7 +146,7 @@
     mix_s, mix_r, dkv_s, dkv_m, dkv_o, dkv_r, dq_t, dkv_tok, dbias, db_s, db_r,
     dsc, dsh, dga, dc_s, dc_r, dc_p, gs_own, gs_all,
     sa, ra, sb, rb, sc, rc, sd, rd, se, re, skv, rkv, skf, rkf, sdm, rdm,
-    sm, rm, sk, rk, sko, rko, sbb, rbb, st, rt, sp, rp_, sg, rg, loc, locm,
+    sm, rm, sk, rk, sko, rko, sbb, rbb, st, rt, sp, rp_, sg, rg, loc, locm, ready,
 ):
     row, col, samp = place()
     core = rmod(row, 2)
@@ -171,13 +179,9 @@
         signal(barrier, (rmod(row + o, NROW), col, samp))
         return 0
 
-    def greet_far(o, _):
-        signal(barrier, (row, rmod(col + o, NCOL), 1 - samp))
-        return 0
-
     lax.fori_loop(1, NCOL, greet, 0)
     lax.fori_loop(1, NROW, greet_row, 0)
-    lax.fori_loop(0, NCOL, greet_far, 0)
+    signal(barrier, far)
 
     low = lax.broadcasted_iota(jnp.int32, (64, 128), 1) < 64
     low16 = lax.broadcasted_iota(jnp.int32, (16, 128), 1) < 64
@@ -238,7 +242,7 @@
     def project(h, t):
         at = pl.ds(pl.multiple_of(t * 256, 256), 256)
         pt = dg(tri_t[h * 256 : h * 256 + 256, :], zl_s[at, :], 1, 1)
-        val = jax.nn.sigmoid(pt[128:]) * pt[:128]
+        val = sigmoid(pt[128:]) * pt[:128]
         for q in range(2):
             lo = 2 * t + q
             mask = mrow[0:1, :] * jnp.where(
@@ -246,13 +250,14 @@
             )
             lrf[pl.ds(h * 2048 + lo, 128, stride=16), :] = val[:, q * 128 : q * 128 + 128] * mask
 
-    a_src = [lambda to, h=h: lbuf.at[h, to] for h in range(2)]
-    a_slot = [lambda c, h=h: recv_a.at[h, c] for h in range(2)]
-    b_src = [lambda r, h=h: recv_a.at[h, :, r] for h in range(2)]
+    pieces = [(0, slice(0, 8)), (1, slice(0, 4)), (1, slice(4, 8))]
+    a_src = [lambda to, h=h, p=p: lbuf.at[h, to, p] for h, p in pieces]
+    a_slot = [lambda c, h=h, p=p: recv_a.at[h, c, p] for h, p in pieces]
+    b_src = [lambda r, h=h: recv_a.at[h, :, spot(r)] for h in range(2)]
     b_slot = [lambda r, h=h: got.at[h, r] for h in range(2)]
     own_a = [pltpu.make_async_copy(lbuf.at[h, col], recv_a.at[h, col], loc.at[h]) for h in range(2)]
     own_b = [
-        pltpu.make_async_copy(recv_a.at[h, :, row], got.at[h, row], loc.at[2 + h])
+        pltpu.make_async_copy(recv_a.at[h, :, spot(row)], got.at[h, row], loc.at[2 + h])
         for h in range(2)
     ]
     for h in range(2):
@@ -261,17 +266,19 @@
             project(h, t)
             return 0
 
-        lax.fori_loop(0, 8, one_side, 0)
+        lax.fori_loop(0, 8, one_side, 0, unroll=2)
 
         def pack(c, _):
             lbuf[h, c] = lrf[pl.ds(h * 2048 + c * 128, 128), :].astype(BF16).reshape(8, 16, 128)
             return 0
 
-        lax.fori_loop(0, 16, pack, 0)
+        lax.fori_loop(0, 16, pack, 0, unroll=2)
         if h == 0:
-            pl.semaphore_wait(barrier, 7 + 15 + 7 + 16)
+            pl.semaphore_wait(barrier, 7 + 15 + 7 + 1)
+            signal(ready, far)
         own_a[h].start()
-        col_start(a_src[h], a_slot[h], sa.at[h], ra.at[h])
+        for i in ((0,), (1, 2))[h]:
+            col_start(a_src[i], a_slot[i], sa.at[i], ra.at[i])
 
     for copy in loads[3:6]:
         copy.wait()
@@ -280,7 +287,7 @@
     wqkv[...] = jnp.zeros_like(wqkv)
     for p in range(3):
         wqkv[p * 64 : p * 64 + 48, :] = qkvw_ref[p]
-    scale_s[...] = jax.nn.sigmoid(jnp.dot(cvec, ada_w[:, :768], preferred_element_type=F32))
+    scale_s[...] = sigmoid(jnp.dot(cvec, ada_w[:, :768], preferred_element_type=F32))
     shift_s[...] = jnp.dot(cvec, ada_w[:, 768:1536], preferred_element_type=F32)
     for copy in loads[6:]:
         copy.wait()
@@ -303,7 +310,7 @@
         (lax.broadcasted_iota(jnp.int32, (768, 64), 0) == col * 48 + feat) & (feat < 48), 1.0, 0.0
     ).astype(BF16)
     wg_s[...] = jnp.dot(ada_w[:, 1536:], sel, preferred_element_type=F32).astype(BF16)
-    gate_t[...] = jax.nn.sigmoid(
+    gate_t[...] = sigmoid(
         dg(wg_s[...], jnp.concatenate([cvec_s[...], cvec_s[...]], 0), 0, 1)
     )
     lane = lax.broadcasted_iota(jnp.int32, (64, 128), 1)
@@ -338,13 +345,23 @@
         kv_out.append(remote(kv_own, kv_all.at[row], skv.at[o], rkv.at[o], to))
     kv_mate = remote(kv_own, kv_all.at[row], skf.at[0], rkf.at[0], mate)
     own_a[1].wait()
-    col_wait(a_src[1], a_slot[1], sa.at[1], ra.at[1])
+    for k in range(2):
+        col_wait(a_src[1 + k], a_slot[1 + k], sa.at[1 + k], ra.at[1 + k])
+        cx = rmod(core + k, 2)
+        for oz in (2, 1, 3):
+            to = row_dest(oz, cx)
+            i = oz * 2 + cx
+            remote(b_src[1](to[0]), b_slot[1](row), sb.at[1, i], rb.at[1, i], to).start()
+
+        @pl.when(cx == 1)
+        def _():
+            remote(b_src[1](mate[0]), b_slot[1](row), sb.at[1, 1], rb.at[1, 1], mate).start()
+
     own_b[1].start()
-    row_start(b_src[1], b_slot[1], sb.at[1], rb.at[1])
 
     def gates(t, _):
         at = pl.ds(pl.multiple_of(t * 256, 256), 256)
-        gate[at, :] = jax.nn.sigmoid(
+        gate[at, :] = sigmoid(
             jnp.dot(zl_s[at, :], tri_w[:, 512:], preferred_element_type=F32)
         )
         return 0
@@ -362,13 +379,19 @@
 
     lax.fori_loop(0, 8, turn, 0)
 
-    c_src, c_slot = (lambda r: tbuf.at[r]), (lambda r: got_c.at[r])
-
-    def tri(rp):
+    c_src = [lambda r, p=p: tbuf.at[r, p] for p in (slice(0, 8), slice(8, 16))]
+    c_slot = [lambda r, p=p: got_c.at[spot(r), p] for p in (slice(0, 8), slice(8, 16))]
+    own_c = [
+        pltpu.make_async_copy(c_src[h](row), c_slot[h](row), loc.at[6 + 3 * h]) for h in range(2)
+    ]
+
+    def tri(rp, part):
         rhs = jnp.concatenate(
             [got[0, 2 * rp].reshape(256, 128), got[0, 2 * rp + 1].reshape(256, 128)], 1
         )
-        mtmp[...] = jnp.dot(rcat[...], rhs, preferred_element_type=F32)
+        mtmp[...] = jnp.dot(
+            rcat[part * 512 : part * 512 + 512, :], rhs, preferred_element_type=F32
+        )
 
         def out(rj, _):
             for half in range(2):
@@ -382,24 +405,64 @@
                         top[a] + pltpu.roll(bot[a], 64, 1),
                         pltpu.roll(top[b], 64, 1) + bot[b],
                     )
-                    tbuf[2 * rp + half, 2 * rj + jh] = t.astype(BF16)
+                    tbuf[2 * rp + half, part * 8 + 2 * rj + jh] = t.astype(BF16)
             return 0
 
-        lax.fori_loop(0, 8, out, 0, unroll=2)
-
-    own_c = pltpu.make_async_copy(tbuf.at[row], got_c.at[row], loc.at[6])
-    for oz in (2, 1, 3, 0):
-        tri(rmod(zlo + oz, 4))
-        for cx in range(2):
-            if (oz, cx) != (0, 0):
-                to = row_dest(oz, cx)
-                i = oz * 2 + cx
-                remote(c_src(to[0]), c_slot(row), sc.at[i], rc.at[i], to).start()
-    own_c.start()
+        lax.fori_loop(0, 4, out, 0, unroll=2)
+
+    for part in range(2):
+        for oz in (2, 1, 3, 0):
+            tri(rmod(zlo + oz, 4), part)
+            for cx in range(2):
+                if (oz, cx) != (0, 0):
+                    to = row_dest(oz, cx)
+                    i = oz * 2 + cx
+                    remote(
+                        c_src[part](to[0]), c_slot[part](row), sc.at[part, i], rc.at[part, i], to
+                    ).start()
+        own_c[part].start()
     kv_mate.start()
     for copy in kv_out:
         copy.start()
-    d_src, d_slot = (lambda c: got_c.at[:, c]), (lambda c: got_d.at[c])
+    d_own = pltpu.make_async_copy(got_c.at[:, col], got_d.at[col], loc.at[7])
+
+    def d_copy(part, o):
+        to = part * 8 + rmod(col + o, 8)
+        return to, remote(
+            got_c.at[:, to], got_d.at[col], sd.at[part, o], rd.at[col], (row, to, samp)
+        )
+
+    def d_start(part):
+        def one(o, _):
+            to, copy = d_copy(part, o)
+
+            @pl.when(to != col)
+            def _():
+                copy.start()
+
+            return 0
+
+        lax.fori_loop(0, 8, one, 0)
+
+    def d_wait():
+        def came(o, _):
+            c = rmod(col + o, NCOL)
+            remote(got_c.at[:, c], got_d.at[c], sd.at[0, 0], rd.at[c], mate).wait_recv()
+            return 0
+
+        lax.fori_loop(1, NCOL, came, 0)
+        for part in range(2):
+
+            def sent(o, _):
+                to, copy = d_copy(part, o)
+
+                @pl.when(to != col)
+                def _():
+                    copy.wait_send()
+
+                return 0
+
+            lax.fori_loop(0, 8, sent, 0)
 
     dm_keep.wait()
     col_wait(dm_src, dm_slot, sdm, rdm)
@@ -409,11 +472,11 @@
         .astype(BF16)
         .astype(F32)
     )
-    own_c.wait()
-    row_wait(c_src, c_slot, sc, rc)
-    own_d = pltpu.make_async_copy(got_c.at[:, col], got_d.at[col], loc.at[7])
-    own_d.start()
-    col_start(d_src, d_slot, sd, rd)
+    for part in range(2):
+        own_c[part].wait()
+        row_wait(c_src[part], c_slot[part], sc.at[part], rc.at[part])
+        d_start(part)
+    d_own.start()
 
     q_t[...] = dg(wqkv[:64, :], hidden[...], 1, 1)
     noisy_t[...] = dg(sel, noisy[...], 0, 1)
@@ -449,8 +512,8 @@
             draw[s] = jnp.dot(keys(1, s), half_of(da_t, u, sh), preferred_element_type=F32)
         return 0
 
-    own_d.wait()
-    col_wait(d_src, d_slot, sd, rd)
+    d_own.wait()
+    d_wait()
 
     def widen(c, _):
         lrf[pl.ds(c * 128, 128), :] = got_d[c].reshape(128, 128).astype(F32)
@@ -582,7 +645,7 @@
     lax.fori_loop(0, 4, pair_of_samples, 0)
 
     db_s[...] = dbias[...].astype(BF16).reshape(16, 16, 128)
-    own_db = pltpu.make_async_copy(db_s.at[col], db_r.at[samp, col], loc.at[9])
+    own_db = pltpu.make_async_copy(db_s.at[col], db_r.at[samp, col], loc.at[29])
     own_db.start()
 
     def db_copy(o):
@@ -596,6 +659,7 @@
         return 0
 
     pass_on(3)
+    pl.semaphore_wait(ready, 1)
     lax.fori_loop(0, NCOL, db_send, 0)
     near_src, near_slot = (lambda c: db_s.at[c]), (lambda c: db_r.at[samp, c])
     col_start(near_src, near_slot, sbb.at[0], rbb.at[0])
@@ -846,7 +910,7 @@
             v((2048, 128), BF16), v((512, 128), BF16), v((2048, 128), F32), v((2048, 128), F32),
             v((4096, 128), F32),
             v((2, 16, 8, 16, 128), BF16), v((2, 16, 8, 16, 128), BF16),
-            v((2, 8, 16, 16, 128), BF16), v((1024, 256), BF16), v((1024, 256), F32),
+            v((2, 8, 16, 16, 128), BF16), v((1024, 256), BF16), v((512, 256), F32),
             v((8, 16, 16, 128), BF16), v((8, 16, 16, 128), BF16), v((16, 8, 16, 128), BF16),
             v((256, 128), F32), v((16, 16, 128), BF16), v((16, 16, 128), BF16),
             v((64, 384), BF16), v((64, 768), F32), v((64, 768), F32), v((384, 64), BF16),
@@ -861,12 +925,12 @@
             v((2, 16, 16, 128), BF16),
             v((64, 768), F32), v((64, 768), F32), v((64, 128), F32), v((8, 8, 384), F32),
             v((16, 8, 384), F32), v((2, 8, 384), F32), v((8, 384), F32), v((8, 8, 384), F32),
-            dma((2, 16)), dma((2, 16)), dma((2, 8)), dma((2, 8)), dma((8,)), dma((8,)),
-            dma((16,)), dma((16,)), dma((16,)), dma((16,)), dma((4,)), dma((4,)),
+            dma((3, 16)), dma((3, 16)), dma((2, 8)), dma((2, 8)), dma((2, 8)), dma((2, 8)),
+            dma((2, 8)), dma((16,)), dma((16,)), dma((16,)), dma((4,)), dma((4,)),
             dma((4,)), dma((4,)), dma((16,)), dma((16,)),
             dma((4, 16)), dma((4, 16)), dma((4,)), dma((4,)), dma((4, 4)), dma((4, 4)),
             dma((2, 16)), dma((2, 16)), dma((8,)), dma((16,)), dma((1,)), dma((1,)),
-            dma((16,)), dma((8,)), dma((29,)), dma((4,)),
+            dma((16,)), dma((8,)), dma((30,)), dma((4,)), pltpu.SemaphoreType.REGULAR,
         ],
         compiler_params=pltpu.CompilerParams(
             collective_id=1, has_side_effects=True, vmem_limit_bytes=60 * 1024 * 1024

time: 108 us -> 106 us (0.981); the launches traced: 108 us -> 105 us
  Pallas kernels: 107 us -> 104 us
    pallas_call x1, Pallas kernels: 105 us -> 101 us  [on_device(): pl.pallas_call(step_kernel, out_shape=(jax.ShapeDtypeStruct((64, 32, 128)...]
where the time goes in v5:
time: 106 us; the launch traced here: 105 us
  Pallas kernels  104 us (98%)
    pallas_call x1, Pallas kernels, on_device(): pl.pallas_call(step_kernel, out_shape=(jax.ShapeDtypeStruct((64, 32, 128)...  101 us
    pallas_call x1, Pallas kernels, finished(): pl.pallas_call(finish_kernel, out_shape=[jax.ShapeDtypeStruct(x.shape, x....  2.67 us

profile of v5, /device:TPU:8, one launch (start us, length us, event | category | flops | bytes accessed | tf_op | source)
XLA Modules:
  0.0 104.6 jit_solution(9093834202510029974)
XLA Ops:
  0.6 101.3 %step.1 = (bf16[64,32,128]{2,1,0:T(8,128)(2,1)}, bf16[8,48,64]{2,1,0:T(8,128)(2,1)}, f32[2048,128]{1,0:T(8,128)}, f32[8,8,384]{2,1,0:T(8,128)}) custom-call(s32[512]{0:T(512)} %res_ref.1, s32[512]{0:T(512)} %chain_ref.1, s32[512]{0:T(512)} %mask_ref.1, bf16[64,32,128]{2,1,0:T(8,128)(2,1)} %pair_hbm.1, bf16[66,128]{1,0:T(8,128)(2,1)} %relpos_hbm.1, ...), custom_call_target="tpu_custom_call" | custom-call | tf_op jit(solution)/shard_map/step/pallas_call | solution.py:894
  101.9 2.7 %finish.1 = (bf16[64,32,128]{2,1,0:T(8,128)(2,1)}, bf16[8,48,64]{2,1,0:T(8,128)(2,1)}, f32[2048,128]{1,0:T(8,128)}, f32[8,8,384]{2,1,0:T(8,128)}) custom-call(bf16[64,32,128]{2,1,0:T(8,128)(2,1)} %get-tuple-element.12.refs_0_, bf16[8,48,64]{2,1,0:T(8,128)(2,1)} %get-tuple-element.13.refs_1_, f32[2048,128]{1,0:T(8,128)} %get-tuple-element.14.refs_2_, ...), custom_call_target="tpu_custom_call" | custom-call | tf_op jit(solution)/shard_map/finish/pallas_call | solution.py:874

commit v6 on v5

--- a/solution.py
+++ b/solution.py
@@ -67,44 +67,22 @@
 
     def one(o, _):
         to = rmod(col + o, NCOL)
-        remote(src_of(to), slot_of(col), ssem.at[o], rsem.at[o], (row, to, samp)).start()
+        remote(src_of(to), slot_of(col), ssem, rsem, (row, to, samp)).start()
         return 0
 
     lax.fori_loop(1, NCOL, one, 0)
 
 
-def col_wait(src_of, slot_of, ssem, rsem, recv=True, send=True):
-    row, col, samp = place()
-
-    def one(o, _):
-        to = rmod(col + o, NCOL)
-        came = rmod(col + NCOL - o, NCOL)
-        if recv:
-            remote(src_of(to), slot_of(came), ssem.at[o], rsem.at[o], (row, to, samp)).wait_recv()
-        if send:
-            remote(src_of(to), slot_of(came), ssem.at[o], rsem.at[o], (row, to, samp)).wait_send()
-        return 0
-
-    lax.fori_loop(1, NCOL, one, 0)
+def take(region, *sems):
+    for sem in sems:
+        pltpu.make_async_copy(region, region, sem).wait()
 
 
 def row_start(src_of, slot_of, ssem, rsem):
     row = lax.axis_index("row")
     for oz, cx in ROW_IDS:
         to = row_dest(oz, cx)
-        i = oz * 2 + cx
-        remote(src_of(to[0]), slot_of(row), ssem.at[i], rsem.at[i], to).start()
-
-
-def row_wait(src_of, slot_of, ssem, rsem, recv=True, send=True):
-    for oz, cx in ROW_IDS:
-        to, came = row_dest(oz, cx), row_source(oz, cx)
-        i = oz * 2 + cx
-        copy = remote(src_of(to[0]), slot_of(came[0]), ssem.at[i], rsem.at[i], to)
-        if recv:
-            copy.wait_recv()
-        if send:
-            copy.wait_send()
+        remote(src_of(to[0]), slot_of(row), ssem, rsem, to).start()
 
 
 def signal(sem, to):
@@ -140,7 +118,7 @@
     pairout_ref, block_ref, gpair_ref,
     pair_in, tri_w, ada_w, noisy, relpos_ref, triout_ref, biasp_ref, single_ref, qkvw_ref, outp_ref,
     cot_ref, idx_r, mrow, relpos_w,
-    zl_s, tri_t, pf, gate, lrf, lbuf, recv_a, got, rcat, mtmp, tbuf, got_c, got_d, bias_f, bias_b, bias_got,
+    zl_s, tri_t, pf, gate, lrf, lbuf, recv_a, got, rcat, lcat, mtmp, tbuf, got_c, got_d, bias_f, bias_b, bias_got,
     cvec_s, scale_s, shift_s, wg_s, gate_t, g_t, noisy_t, normed, hidden, wqkv, q_t, kv_f,
     kv_own, kv_all, dmx_own, dmx_all, da_t, keyok, sraw, draw,
     mix_s, mix_r, dkv_s, dkv_m, dkv_o, dkv_r, dq_t, dkv_tok, dbias, db_s, db_r,
@@ -301,7 +279,7 @@
 
     lax.fori_loop(0, 8, sample, 0)
     own_a[0].wait()
-    col_wait(a_src[0], a_slot[0], sa.at[0], ra.at[0])
+    take(recv_a.at[0, 0:15], sa.at[0], ra.at[0])
     own_b[0].start()
     row_start(b_src[0], b_slot[0], sb.at[0], rb.at[0])
 
@@ -325,7 +303,7 @@
     dm_src, dm_slot = (lambda to: dmx_own), (lambda c: dmx_all.at[c])
     dm_keep = pltpu.make_async_copy(dmx_own, dmx_all.at[col], loc.at[5])
     dm_keep.start()
-    col_start(dm_src, dm_slot, sdm, rdm)
+    col_start(dm_src, dm_slot, sdm.at[0], rdm.at[0])
     kv_f[...] = dg(hidden[...], wqkv[64:, :], 1, 1)
 
     def kv_pack(t, _):
@@ -346,16 +324,15 @@
     kv_mate = remote(kv_own, kv_all.at[row], skf.at[0], rkf.at[0], mate)
     own_a[1].wait()
     for k in range(2):
-        col_wait(a_src[1 + k], a_slot[1 + k], sa.at[1 + k], ra.at[1 + k])
+        take(recv_a.at[1, 0:15, 0:4], sa.at[1 + k], ra.at[1 + k])
         cx = rmod(core + k, 2)
         for oz in (2, 1, 3):
             to = row_dest(oz, cx)
-            i = oz * 2 + cx
-            remote(b_src[1](to[0]), b_slot[1](row), sb.at[1, i], rb.at[1, i], to).start()
+            remote(b_src[1](to[0]), b_slot[1](row), sb.at[1], rb.at[1], to).start()
 
         @pl.when(cx == 1)
         def _():
-            remote(b_src[1](mate[0]), b_slot[1](row), sb.at[1, 1], rb.at[1, 1], mate).start()
+            remote(b_src[1](mate[0]), b_slot[1](row), sb.at[1], rb.at[1], mate).start()
 
     own_b[1].start()
 
@@ -369,103 +346,82 @@
     lax.fori_loop(0, 8, gates, 0)
     for h in (1, 0):
         own_b[h].wait()
-        row_wait(b_src[h], b_slot[h], sb.at[h], rb.at[h])
+        take(got.at[h, 0:7], sb.at[h], rb.at[h])
 
     def turn(r, _):
-        rcat[pl.ds(pl.multiple_of(r * 128, 128), 128), :] = (
-            got[1, r].reshape(256, 128).astype(F32).T.astype(BF16)
-        )
-        return 0
-
-    lax.fori_loop(0, 8, turn, 0)
-
+        x = got[1, r].reshape(256, 128).astype(F32).T.astype(BF16)
+        at = pl.ds(pl.multiple_of(r * 64, 64), 64)
+        rcat[at, 0:256] = x[:64]
+        rcat[at, 256:512] = x[64:]
+        return 0
+
+    lax.fori_loop(0, 8, turn, 0, unroll=2)
+    low256 = lax.broadcasted_iota(jnp.int32, (256, 128), 1) < 64
+    turns = ((2, 1), (3, 0))
+    for i, pair in enumerate(turns):
+        for k, oz in enumerate(pair):
+            z = rmod(zlo + oz, 4)
+            la = got[0, 2 * z].reshape(256, 128).astype(F32)
+            lb = got[0, 2 * z + 1].reshape(256, 128).astype(F32)
+            lanes = slice(k * 128, k * 128 + 128)
+            lcat[i, 0:256, lanes] = jnp.where(low256, la, pltpu.roll(lb, 64, 1)).astype(BF16)
+            lcat[i, 256:512, lanes] = jnp.where(low256, pltpu.roll(la, 64, 1), lb).astype(BF16)
     c_src = [lambda r, p=p: tbuf.at[r, p] for p in (slice(0, 8), slice(8, 16))]
     c_slot = [lambda r, p=p: got_c.at[spot(r), p] for p in (slice(0, 8), slice(8, 16))]
     own_c = [
         pltpu.make_async_copy(c_src[h](row), c_slot[h](row), loc.at[6 + 3 * h]) for h in range(2)
     ]
 
-    def tri(rp, part):
-        rhs = jnp.concatenate(
-            [got[0, 2 * rp].reshape(256, 128), got[0, 2 * rp + 1].reshape(256, 128)], 1
-        )
+    def tri(i, part):
         mtmp[...] = jnp.dot(
-            rcat[part * 512 : part * 512 + 512, :], rhs, preferred_element_type=F32
+            rcat[part * 256 : part * 256 + 256, :], lcat[i], preferred_element_type=F32
         )
 
         def out(rj, _):
-            for half in range(2):
-                top = mtmp[pl.ds(rj * 128, 64), half * 128 : half * 128 + 128]
-                bot = mtmp[pl.ds(rj * 128 + 64, 64), half * 128 : half * 128 + 128]
+            for k, oz in enumerate(turns[i]):
+                z = rmod(zlo + oz, 4)
                 for jh in range(2):
-                    a = slice(jh * 32, jh * 32 + 16)
-                    b = slice(jh * 32 + 16, jh * 32 + 32)
-                    t = jnp.where(
-                        low16,
-                        top[a] + pltpu.roll(bot[a], 64, 1),
-                        pltpu.roll(top[b], 64, 1) + bot[b],
-                    )
-                    tbuf[2 * rp + half, part * 8 + 2 * rj + jh] = t.astype(BF16)
+                    at = rj * 64 + jh * 32
+                    a = mtmp[pl.ds(at, 16), k * 128 : k * 128 + 128]
+                    b = mtmp[pl.ds(at + 16, 16), k * 128 : k * 128 + 128]
+                    even_row = jnp.where(low16, a, pltpu.roll(b, 64, 1))
+                    odd_row = jnp.where(low16, pltpu.roll(a, 64, 1), b)
+                    tbuf[2 * z, part * 8 + 2 * rj + jh] = even_row.astype(BF16)
+                    tbuf[2 * z + 1, part * 8 + 2 * rj + jh] = odd_row.astype(BF16)
             return 0
 
         lax.fori_loop(0, 4, out, 0, unroll=2)
 
     for part in range(2):
-        for oz in (2, 1, 3, 0):
-            tri(rmod(zlo + oz, 4), part)
-            for cx in range(2):
-                if (oz, cx) != (0, 0):
-                    to = row_dest(oz, cx)
-                    i = oz * 2 + cx
-                    remote(
-                        c_src[part](to[0]), c_slot[part](row), sc.at[part, i], rc.at[part, i], to
-                    ).start()
+        for i, pair in enumerate(turns):
+            tri(i, part)
+            for oz in pair:
+                for cx in range(2):
+                    if (oz, cx) != (0, 0):
+                        to = row_dest(oz, cx)
+                        remote(
+                            c_src[part](to[0]), c_slot[part](row), sc.at[part], rc.at[part], to
+                        ).start()
         own_c[part].start()
     kv_mate.start()
     for copy in kv_out:
         copy.start()
     d_own = pltpu.make_async_copy(got_c.at[:, col], got_d.at[col], loc.at[7])
 
-    def d_copy(part, o):
-        to = part * 8 + rmod(col + o, 8)
-        return to, remote(
-            got_c.at[:, to], got_d.at[col], sd.at[part, o], rd.at[col], (row, to, samp)
-        )
-
     def d_start(part):
         def one(o, _):
-            to, copy = d_copy(part, o)
+            to = part * 8 + rmod(col + o, 8)
 
             @pl.when(to != col)
             def _():
-                copy.start()
+                remote(got_c.at[:, to], got_d.at[col], sd.at[0], rd.at[0], (row, to, samp)).start()
 
             return 0
 
         lax.fori_loop(0, 8, one, 0)
 
-    def d_wait():
-        def came(o, _):
-            c = rmod(col + o, NCOL)
-            remote(got_c.at[:, c], got_d.at[c], sd.at[0, 0], rd.at[c], mate).wait_recv()
-            return 0
-
-        lax.fori_loop(1, NCOL, came, 0)
-        for part in range(2):
-
-            def sent(o, _):
-                to, copy = d_copy(part, o)
-
-                @pl.when(to != col)
-                def _():
-                    copy.wait_send()
-
-                return 0
-
-            lax.fori_loop(0, 8, sent, 0)
-
     dm_keep.wait()
-    col_wait(dm_src, dm_slot, sdm, rdm)
+    take(dmx_all.at[0:15], sdm.at[0], rdm.at[0])
     da_t[...] = jnp.zeros_like(da_t)
     da_t[:48, :] = (
         jnp.dot(outp_ref[...], dmx_all[...].reshape(768, 512), preferred_element_type=F32)
@@ -474,7 +430,7 @@
     )
     for part in range(2):
         own_c[part].wait()
-        row_wait(c_src[part], c_slot[part], sc.at[part], rc.at[part])
+        take(got_c.at[0:7, 0:8], sc.at[part], rc.at[part])
         d_start(part)
     d_own.start()
 
@@ -513,7 +469,7 @@
         return 0
 
     d_own.wait()
-    d_wait()
+    take(got_d.at[0:15], sd.at[0], rd.at[0])
 
     def widen(c, _):
         lrf[pl.ds(c * 128, 128), :] = got_d[c].reshape(128, 128).astype(F32)
@@ -537,12 +493,12 @@
             bias_f[pl.ds(2 * t + q, 16, stride=16), :] = tile[:, q * 128 : q * 128 + 128]
         return 0
 
-    lax.fori_loop(0, 8, stage3, 0, unroll=2)
+    lax.fori_loop(0, 8, stage3, 0, unroll=4)
     bias_b[...] = bias_f[...].astype(BF16).reshape(16, 16, 128)
     e_src, e_slot = (lambda c: bias_b.at[c]), (lambda c: bias_got.at[c])
     own_e = pltpu.make_async_copy(bias_b.at[col], bias_got.at[col], loc.at[8])
     own_e.start()
-    col_start(e_src, e_slot, se, re)
+    col_start(e_src, e_slot, se.at[0], re.at[0])
 
     kv_keep.wait()
     for copy in kv_out:
@@ -567,7 +523,7 @@
     out_pair.start()
     dbias[...] = jnp.zeros_like(dbias)
     own_e.wait()
-    col_wait(e_src, e_slot, se, re)
+    take(bias_got.at[0:15], se.at[0], re.at[0])
 
     scale = 1.0 / HEAD_DIM**0.5
 
@@ -651,7 +607,7 @@
     def db_copy(o):
         to = rmod(col + o, NCOL)
         return remote(
-            db_s.at[to], db_r.at[samp, col], sbb.at[1, o], rbb.at[1, o], (row, to, 1 - samp)
+            db_s.at[to], db_r.at[samp, col], sbb.at[1], rbb.at[1], (row, to, 1 - samp)
         )
 
     def db_send(o, _):
@@ -668,7 +624,7 @@
 
     def mixed_of(u, _):
         pltpu.make_async_copy(mix_s.at[u, col], mix_r.at[u, col], locm.at[u]).wait()
-        col_wait(mix_src(u), mix_slot(u), sm.at[u], rm.at[u])
+        take(mix_r.at[u, 0:15], sm.at[u], rm.at[u])
         total = mix_r[u, 0].astype(F32)
         for h in range(1, NCOL):
             total = total + mix_r[u, h].astype(F32)
@@ -735,7 +691,7 @@
 
     def part_copy(o):
         g = rmod(half_col + o, 8)
-        return remote(dc_s.at[g], dc_r.at[col], st.at[o], rt.at[col], (row, 2 * g, samp))
+        return remote(dc_s.at[g], dc_r.at[col], st.at[0], rt.at[0], (row, 2 * g, samp))
 
     @pl.when(jnp.logical_not(even))
     def _():
@@ -748,15 +704,8 @@
     lax.fori_loop(1, 8, part_send, 0)
 
     own_db.wait()
-    col_wait(near_src, near_slot, sbb.at[0], rbb.at[0])
-
-    def db_wait(o, _):
-        came = rmod(col + NCOL - o, NCOL)
-        remote(db_s.at[came], db_r.at[1 - samp, came], sbb.at[1, o], rbb.at[1, o], far).wait_recv()
-        db_copy(o).wait_send()
-        return 0
-
-    lax.fori_loop(0, NCOL, db_wait, 0)
+    take(db_r.at[0, 0:15], sbb.at[0], rbb.at[0])
+    take(db_r.at[0], sbb.at[1], rbb.at[1])
     dbias[...] = (db_r[0].astype(F32) + db_r[1].astype(F32)).reshape(256, 128)
     biasp3 = jnp.concatenate([biasp_ref[...]] * 3, 0)
 
@@ -777,19 +726,14 @@
 
     def own_copy(o):
         return remote(
-            gs_own, gs_all.at[half_col], sg.at[o], rg.at[half_col], (row, rmod(col + o, NCOL), samp)
+            gs_own, gs_all.at[half_col], sg.at[0], rg.at[0], (row, rmod(col + o, NCOL), samp)
         )
 
     @pl.when(even)
     def _():
         dc_r[col] = dc_s[half_col]
 
-        def arrived(o, _):
-            came = rmod(col + o, NCOL)
-            remote(dc_s.at[0], dc_r.at[came], st.at[0], rt.at[came], far).wait_recv()
-            return 0
-
-        lax.fori_loop(1, NCOL, arrived, 0)
+        take(dc_r.at[0:15], rt.at[0])
         tot = dc_r[0]
         for c in range(1, NCOL):
             tot = tot + dc_r[c]
@@ -818,36 +762,17 @@
         lax.fori_loop(1, NCOL, tell, 0)
         gs_all[half_col] = gs_own[...]
 
+    @pl.when(even)
+    def _():
+        take(dc_s.at[0:7], st.at[0])
+        take(dc_r.at[0:15], sg.at[0])
+        take(gs_all.at[0:7], rg.at[0])
+
     @pl.when(jnp.logical_not(even))
     def _():
-        part_copy(0).wait_send()
-
-    def part_sent(o, _):
-        part_copy(o).wait_send()
-        return 0
-
-    lax.fori_loop(1, 8, part_sent, 0)
-
-    @pl.when(even)
-    def _():
-        def told(o, _):
-            own_copy(o).wait_send()
-            return 0
-
-        lax.fori_loop(1, NCOL, told, 0)
-
-    def total_came(g):
-        remote(gs_own, gs_all.at[g], sg.at[0], rg.at[g], far).wait_recv()
-
-    @pl.when(jnp.logical_not(even))
-    def _():
-        total_came(half_col)
-
-    def came_from(o, _):
-        total_came(rmod(half_col + o, 8))
-        return 0
-
-    lax.fori_loop(1, 8, came_from, 0)
+        take(dc_s, st.at[0])
+        take(gs_all, rg.at[0])
+
     out_single = pltpu.make_async_copy(gs_all, gsingle_hbm, loc.at[17])
     out_single.start()
     for copy in (out_pair, out_block, out_grad, out_single):
@@ -910,7 +835,8 @@
             v((2048, 128), BF16), v((512, 128), BF16), v((2048, 128), F32), v((2048, 128), F32),
             v((4096, 128), F32),
             v((2, 16, 8, 16, 128), BF16), v((2, 16, 8, 16, 128), BF16),
-            v((2, 8, 16, 16, 128), BF16), v((1024, 256), BF16), v((512, 256), F32),
+            v((2, 8, 16, 16, 128), BF16), v((512, 512), BF16), v((2, 512, 256), BF16),
+            v((256, 256), F32),
             v((8, 16, 16, 128), BF16), v((8, 16, 16, 128), BF16), v((16, 8, 16, 128), BF16),
             v((256, 128), F32), v((16, 16, 128), BF16), v((16, 16, 128), BF16),
             v((64, 384), BF16), v((64, 768), F32), v((64, 768), F32), v((384, 64), BF16),
@@ -925,12 +851,12 @@
             v((2, 16, 16, 128), BF16),
             v((64, 768), F32), v((64, 768), F32), v((64, 128), F32), v((8, 8, 384), F32),
             v((16, 8, 384), F32), v((2, 8, 384), F32), v((8, 384), F32), v((8, 8, 384), F32),
-            dma((3, 16)), dma((3, 16)), dma((2, 8)), dma((2, 8)), dma((2, 8)), dma((2, 8)),
-            dma((2, 8)), dma((16,)), dma((16,)), dma((16,)), dma((4,)), dma((4,)),
-            dma((4,)), dma((4,)), dma((16,)), dma((16,)),
-            dma((4, 16)), dma((4, 16)), dma((4,)), dma((4,)), dma((4, 4)), dma((4, 4)),
-            dma((2, 16)), dma((2, 16)), dma((8,)), dma((16,)), dma((1,)), dma((1,)),
-            dma((16,)), dma((8,)), dma((30,)), dma((4,)), pltpu.SemaphoreType.REGULAR,
+            dma((3,)), dma((3,)), dma((2,)), dma((2,)), dma((2,)), dma((2,)),
+            dma((1,)), dma((1,)), dma((1,)), dma((1,)), dma((4,)), dma((4,)),
+            dma((4,)), dma((4,)), dma((1,)), dma((1,)),
+            dma((4,)), dma((4,)), dma((4,)), dma((4,)), dma((4, 4)), dma((4, 4)),
+            dma((2,)), dma((2,)), dma((1,)), dma((1,)), dma((1,)), dma((1,)),
+            dma((1,)), dma((1,)), dma((30,)), dma((4,)), pltpu.SemaphoreType.REGULAR,
         ],
         compiler_params=pltpu.CompilerParams(
             collective_id=1, has_side_effects=True, vmem_limit_bytes=60 * 1024 * 1024

time: 106 us -> 101 us (0.953)
  Pallas kernels: 104 us -> 98.8 us
    pallas_call x1, Pallas kernels: 101 us -> 96.1 us  [on_device(): pl.pallas_call(step_kernel, out_shape=(jax.ShapeDtypeStruct((64, 32, 128)...]
where the time goes in v6:
time: 101 us; the launch traced here: 99.5 us
  Pallas kernels  98.8 us (98%)
    pallas_call x1, Pallas kernels, on_device(): pl.pallas_call(step_kernel, out_shape=(jax.ShapeDtypeStruct((64, 32, 128)...  96.1 us
    pallas_call x1, Pallas kernels, finished(): pl.pallas_call(finish_kernel, out_shape=[jax.ShapeDtypeStruct(x.shape, x....  2.67 us

profile of v6, /device:TPU:8, one launch (start us, length us, event | category | flops | bytes accessed | tf_op | source)
XLA Modules:
  0.0 99.5 jit_solution(7144002972017050462)
XLA Ops:
  0.6 96.1 %step.1 = (bf16[64,32,128]{2,1,0:T(8,128)(2,1)}, bf16[8,48,64]{2,1,0:T(8,128)(2,1)}, f32[2048,128]{1,0:T(8,128)}, f32[8,8,384]{2,1,0:T(8,128)}) custom-call(s32[512]{0:T(512)} %res_ref.1, s32[512]{0:T(512)} %chain_ref.1, s32[512]{0:T(512)} %mask_ref.1, bf16[64,32,128]{2,1,0:T(8,128)(2,1)} %pair_hbm.1, bf16[66,128]{1,0:T(8,128)(2,1)} %relpos_hbm.1, ...), custom_call_target="tpu_custom_call" | custom-call | tf_op jit(solution)/shard_map/step/pallas_call | solution.py:819
  96.8 2.7 %finish.1 = (bf16[64,32,128]{2,1,0:T(8,128)(2,1)}, bf16[8,48,64]{2,1,0:T(8,128)(2,1)}, f32[2048,128]{1,0:T(8,128)}, f32[8,8,384]{2,1,0:T(8,128)}) custom-call(bf16[64,32,128]{2,1,0:T(8,128)(2,1)} %get-tuple-element.12.refs_0_, bf16[8,48,64]{2,1,0:T(8,128)(2,1)} %get-tuple-element.13.refs_1_, f32[2048,128]{1,0:T(8,128)} %get-tuple-element.14.refs_2_, ...), custom_call_target="tpu_custom_call" | custom-call | tf_op jit(solution)/shard_map/finish/pallas_call | solution.py:799

commit v7 on v6

--- a/solution.py
+++ b/solution.py
@@ -70,7 +70,7 @@
         remote(src_of(to), slot_of(col), ssem, rsem, (row, to, samp)).start()
         return 0
 
-    lax.fori_loop(1, NCOL, one, 0)
+    lax.fori_loop(1, NCOL, one, 0, unroll=5)
 
 
 def take(region, *sems):
@@ -120,7 +120,7 @@
     cot_ref, idx_r, mrow, relpos_w,
     zl_s, tri_t, pf, gate, lrf, lbuf, recv_a, got, rcat, lcat, mtmp, tbuf, got_c, got_d, bias_f, bias_b, bias_got,
     cvec_s, scale_s, shift_s, wg_s, gate_t, g_t, noisy_t, normed, hidden, wqkv, q_t, kv_f,
-    kv_own, kv_all, dmx_own, dmx_all, da_t, keyok, sraw, draw,
+    kv_own, kv_all, dmx_own, dmx_all, da_t, keyok, sraw, draw, qq_s, dd_s,
     mix_s, mix_r, dkv_s, dkv_m, dkv_o, dkv_r, dq_t, dkv_tok, dbias, db_s, db_r,
     dsc, dsh, dga, dc_s, dc_r, dc_p, gs_own, gs_all,
     sa, ra, sb, rb, sc, rc, sd, rd, se, re, skv, rkv, skf, rkf, sdm, rdm,
@@ -157,8 +157,8 @@
         signal(barrier, (rmod(row + o, NROW), col, samp))
         return 0
 
-    lax.fori_loop(1, NCOL, greet, 0)
-    lax.fori_loop(1, NROW, greet_row, 0)
+    lax.fori_loop(1, NCOL, greet, 0, unroll=5)
+    lax.fori_loop(1, NROW, greet_row, 0, unroll=7)
     signal(barrier, far)
 
     low = lax.broadcasted_iota(jnp.int32, (64, 128), 1) < 64
@@ -418,7 +418,7 @@
 
             return 0
 
-        lax.fori_loop(0, 8, one, 0)
+        lax.fori_loop(0, 8, one, 0, unroll=4)
 
     dm_keep.wait()
     take(dmx_all.at[0:15], sdm.at[0], rdm.at[0])
@@ -461,11 +461,16 @@
     def keys(which, s):
         return jnp.concatenate([kv_all[r, which, s] for r in range(NROW)], 0)
 
+    scale = 1.0 / HEAD_DIM**0.5
+
     def raw(u, _):
         for sh in range(2):
             s = 2 * u + sh
-            sraw[s] = jnp.dot(keys(0, s), half_of(q_t, u, sh), preferred_element_type=F32)
-            draw[s] = jnp.dot(keys(1, s), half_of(da_t, u, sh), preferred_element_type=F32)
+            qq, dd = half_of(q_t, u, sh), half_of(da_t, u, sh)
+            qq_s[s] = qq
+            dd_s[s] = dd
+            sraw[s] = jnp.dot(keys(0, s), qq, preferred_element_type=F32) * scale
+            draw[s] = jnp.dot(keys(1, s), dd, preferred_element_type=F32)
         return 0
 
     d_own.wait()
@@ -525,7 +530,7 @@
     own_e.wait()
     take(bias_got.at[0:15], se.at[0], re.at[0])
 
-    scale = 1.0 / HEAD_DIM**0.5
+    bias_f[...] = bias_got[...].reshape(256, 128).astype(F32)
 
     def mix_src(u):
         return lambda f: mix_s.at[u, f]
@@ -552,13 +557,11 @@
             to_chip(u, o).start()
 
     def pair_of_samples(u, _):
-        folded, dqs = [], []
+        folded, dqs, grads = [], [], []
         for sh in range(2):
             s = 2 * u + sh
             kp, vp = keys(0, s), keys(1, s)
-            qq, dd = half_of(q_t, u, sh), half_of(da_t, u, sh)
-            sco = sraw[s] * scale + bias_got[...].reshape(256, 128).astype(F32)
-            sco = jnp.where(keyok[...] > 0, sco, -1000000000.0)
+            sco = jnp.where(keyok[...] > 0, sraw[s] + bias_f[...], -1000000000.0)
             top = jnp.max(sco, 0, keepdims=True)
             top = jnp.maximum(top, pltpu.roll(top, 64, 1))
             ex = jnp.exp(sco - top)
@@ -569,11 +572,11 @@
             dp = draw[s]
             dot = jnp.sum(probs * dp, 0, keepdims=True)
             ds = probs * (dp - (dot + pltpu.roll(dot, 64, 1)))
-            dbias[...] += ds
+            grads.append(ds)
             dsb = (ds * scale).astype(BF16)
             dqs.append(dg(kp, dsb, 0, 0))
-            dk = dg(dsb, qq, 1, 1).astype(BF16)
-            dv = dg(pb, dd, 1, 1).astype(BF16)
+            dk = dg(dsb, qq_s[s], 1, 1).astype(BF16)
+            dv = dg(pb, dd_s[s], 1, 1).astype(BF16)
             for r in range(NROW):
                 dkv_s[r // 2, r % 2, u, sh] = dk[r * 32 : r * 32 + 32]
                 dkv_s[r // 2, r % 2, u, 2 + sh] = dv[r * 32 : r * 32 + 32]
@@ -585,6 +588,7 @@
                 pltpu.roll(m1[:64], 64, 1) + m1[64:],
             ).astype(BF16)
 
+        dbias[...] += grads[0] + grads[1]
         att = fold(*folded)
         dq_t[u] = fold(*dqs)
         mix_s[u] = dg(outp_ref[...], att[:48], 0, 0).astype(BF16).reshape(16, 48, 128)
@@ -616,7 +620,7 @@
 
     pass_on(3)
     pl.semaphore_wait(ready, 1)
-    lax.fori_loop(0, NCOL, db_send, 0)
+    lax.fori_loop(0, NCOL, db_send, 0, unroll=4)
     near_src, near_slot = (lambda c: db_s.at[c]), (lambda c: db_r.at[samp, c])
     col_start(near_src, near_slot, sbb.at[0], rbb.at[0])
 
@@ -701,7 +705,7 @@
         part_copy(o).start()
         return 0
 
-    lax.fori_loop(1, 8, part_send, 0)
+    lax.fori_loop(1, 8, part_send, 0, unroll=7)
 
     own_db.wait()
     take(db_r.at[0, 0:15], sbb.at[0], rbb.at[0])
@@ -709,20 +713,20 @@
     dbias[...] = (db_r[0].astype(F32) + db_r[1].astype(F32)).reshape(256, 128)
     biasp3 = jnp.concatenate([biasp_ref[...]] * 3, 0)
 
-    def grad(lo, _):
-        d = dbias[pl.ds(lo, 16, stride=16), :]
+    def grad(t, _):
+        d = jnp.concatenate([dbias[pl.ds(2 * t + q, 16, stride=16), :] for q in range(2)], 1)
         d1 = d.astype(BF16)
         rest = d - d1.astype(F32)
         d2 = rest.astype(BF16)
         d3 = (rest - d2.astype(F32)).astype(BF16)
         g = dg(jnp.concatenate([d1, d2, d3], 0), biasp3, 0, 0)
-        for hi in range(2):
-            gpair_ref[pl.ds(lo + 16 * hi, 64, stride=32), :] = g[hi * 64 : hi * 64 + 64]
-        return 0
-
-    lax.fori_loop(0, 16, grad, 0, unroll=2)
-    out_grad = pltpu.make_async_copy(gpair_ref, gpair_hbm, loc.at[16])
-    out_grad.start()
+        for q in range(2):
+            for hi in range(2):
+                base = q * 128 + hi * 64
+                gpair_ref[pl.ds(2 * t + q + 16 * hi, 64, stride=32), :] = g[base : base + 64]
+        return 0
+
+    lax.fori_loop(0, 4, grad, 0, unroll=2)
 
     def own_copy(o):
         return remote(
@@ -738,8 +742,14 @@
         for c in range(1, NCOL):
             tot = tot + dc_r[c]
         dc_p[samp] = tot
-        other = remote(dc_p.at[samp], dc_p.at[samp], sp.at[0], rp_.at[0], far)
-        other.start()
+        remote(dc_p.at[samp], dc_p.at[samp], sp.at[0], rp_.at[0], far).start()
+
+    lax.fori_loop(4, 8, grad, 0, unroll=2)
+    out_grad = pltpu.make_async_copy(gpair_ref, gpair_hbm, loc.at[16])
+    out_grad.start()
+
+    @pl.when(even)
+    def _():
         own = single_ref[...].astype(F32).reshape(8, 8, 384)
         mine = jnp.zeros((8, 384), F32)
         for g in range(8):
@@ -749,7 +759,7 @@
         inv = lax.rsqrt(jnp.mean(cent * cent, -1, keepdims=True) + EPSILON)
         unit = cent * inv
         remote(dc_p.at[samp], dc_p.at[1 - samp], sp.at[0], rp_.at[0], far).wait_recv()
-        other.wait_send()
+        remote(dc_p.at[samp], dc_p.at[samp], sp.at[0], rp_.at[0], far).wait_send()
         up = dc_p[0] + dc_p[1]
         gs_own[...] = inv * (
             up - jnp.mean(up, -1, keepdims=True) - unit * jnp.mean(up * unit, -1, keepdims=True)
@@ -759,7 +769,7 @@
             own_copy(o).start()
             return 0
 
-        lax.fori_loop(1, NCOL, tell, 0)
+        lax.fori_loop(1, NCOL, tell, 0, unroll=5)
         gs_all[half_col] = gs_own[...]
 
     @pl.when(even)
@@ -844,7 +854,7 @@
             v((512, 768), BF16), v((192, 768), BF16), v((64, 512), F32), v((512, 128), F32),
             v((2, 8, 32, 128), BF16), v((8, 2, 8, 32, 128), BF16), v((48, 512), BF16),
             v((16, 48, 512), BF16), v((64, 512), F32), v((256, 128), F32), v((8, 256, 128), F32),
-            v((8, 256, 128), F32),
+            v((8, 256, 128), F32), v((8, 128, 128), BF16), v((8, 128, 128), BF16),
             v((4, 16, 48, 128), BF16), v((4, 16, 48, 128), BF16), v((4, 2, 4, 4, 32, 128), BF16),
             v((4, 4, 4, 32, 128), BF16), v((4, 4, 4, 32, 128), BF16), v((4, 4, 4, 32, 128), BF16),
             v((4, 64, 128), BF16), v((128, 128), BF16), v((256, 128), F32), v((16, 16, 128), BF16),

time: 101 us -> 101 us (level)
  no operation moved by 1% of the time
where the time goes in v7:
time: 101 us; the launch traced here: 99.3 us
  Pallas kernels  98.6 us (98%)
    pallas_call x1, Pallas kernels, on_device(): pl.pallas_call(step_kernel, out_shape=(jax.ShapeDtypeStruct((64, 32, 128)...  95.9 us
    pallas_call x1, Pallas kernels, finished(): pl.pallas_call(finish_kernel, out_shape=[jax.ShapeDtypeStruct(x.shape, x....  2.67 us

profile of v7, /device:TPU:8, one launch (start us, length us, event | category | flops | bytes accessed | tf_op | source)
XLA Modules:
  0.0 99.3 jit_solution(9376478770257023963)
XLA Ops:
  0.6 95.9 %step.1 = (bf16[64,32,128]{2,1,0:T(8,128)(2,1)}, bf16[8,48,64]{2,1,0:T(8,128)(2,1)}, f32[2048,128]{1,0:T(8,128)}, f32[8,8,384]{2,1,0:T(8,128)}) custom-call(s32[512]{0:T(512)} %res_ref.1, s32[512]{0:T(512)} %chain_ref.1, s32[512]{0:T(512)} %mask_ref.1, bf16[64,32,128]{2,1,0:T(8,128)(2,1)} %pair_hbm.1, bf16[66,128]{1,0:T(8,128)(2,1)} %relpos_hbm.1, ...), custom_call_target="tpu_custom_call" | custom-call | tf_op jit(solution)/shard_map/step/pallas_call | solution.py:829
  96.6 2.7 %finish.1 = (bf16[64,32,128]{2,1,0:T(8,128)(2,1)}, bf16[8,48,64]{2,1,0:T(8,128)(2,1)}, f32[2048,128]{1,0:T(8,128)}, f32[8,8,384]{2,1,0:T(8,128)}) custom-call(bf16[64,32,128]{2,1,0:T(8,128)(2,1)} %get-tuple-element.12.refs_0_, bf16[8,48,64]{2,1,0:T(8,128)(2,1)} %get-tuple-element.13.refs_1_, f32[2048,128]{1,0:T(8,128)} %get-tuple-element.14.refs_2_, ...), custom_call_target="tpu_custom_call" | custom-call | tf_op jit(solution)/shard_map/finish/pallas_call | solution.py:809

commit v8 on v6

--- a/solution.py
+++ b/solution.py
@@ -318,10 +318,13 @@
     kv_keep = pltpu.make_async_copy(kv_own, kv_all.at[row], loc.at[4])
     kv_keep.start()
     kv_out = []
-    for o in range(1, 4):
-        to = (rmod(zlo + o, 4) * 2 + core, col, samp)
-        kv_out.append(remote(kv_own, kv_all.at[row], skv.at[o], rkv.at[o], to))
-    kv_mate = remote(kv_own, kv_all.at[row], skf.at[0], rkf.at[0], mate)
+    for w in range(2):
+        kv_out.append(remote(kv_own.at[w], kv_all.at[row, w], skf.at[w, 0], rkf.at[w, 0], mate))
+        for o in range(1, 4):
+            to = (rmod(zlo + o, 4) * 2 + core, col, samp)
+            kv_out.append(
+                remote(kv_own.at[w], kv_all.at[row, w], skv.at[w, o], rkv.at[w, o], to)
+            )
     own_a[1].wait()
     for k in range(2):
         take(recv_a.at[1, 0:15, 0:4], sa.at[1 + k], ra.at[1 + k])
@@ -403,7 +406,6 @@
                             c_src[part](to[0]), c_slot[part](row), sc.at[part], rc.at[part], to
                         ).start()
         own_c[part].start()
-    kv_mate.start()
     for copy in kv_out:
         copy.start()
     d_own = pltpu.make_async_copy(got_c.at[:, col], got_d.at[col], loc.at[7])
@@ -448,11 +450,28 @@
 
     lax.fori_loop(0, 256, key_mask, 0, unroll=4)
 
-    for o in range(1, 4):
-        came = rmod(zlo + 4 - o, 4) * 2 + core
-        remote(kv_own, kv_all.at[came], skv.at[o], rkv.at[o], mate).wait_recv()
-        remote(kv_all.at[came], kv_all.at[came], skf.at[o], rkf.at[o], mate).start()
-
+    def pass_keys(w):
+        for o in range(1, 4):
+            came = rmod(zlo + 4 - o, 4) * 2 + core
+            remote(
+                kv_own.at[w], kv_all.at[came, w], skv.at[w, o], rkv.at[w, o], mate
+            ).wait_recv()
+            remote(
+                kv_all.at[came, w], kv_all.at[came, w], skf.at[w, o], rkf.at[w, o], mate
+            ).start()
+
+    def keys_passed(w):
+        for o in range(4):
+            came = rmod(zlo + 4 - o, 4) * 2
+            remote(
+                kv_all.at[came + core, w], kv_all.at[came + 1 - core, w], skf.at[w, o],
+                rkf.at[w, o], mate,
+            ).wait_recv()
+            if o > 0:
+                remote(
+                    kv_all.at[came + core, w], kv_all.at[came + core, w], skf.at[w, o],
+                    rkf.at[w, o], mate,
+                ).wait_send()
 
     def half_of(ref, u, sh):
         tile = ref[:, pl.ds(pl.multiple_of(u * 128, 128), 128)].astype(F32)
@@ -461,12 +480,16 @@
     def keys(which, s):
         return jnp.concatenate([kv_all[r, which, s] for r in range(NROW)], 0)
 
-    def raw(u, _):
-        for sh in range(2):
-            s = 2 * u + sh
-            sraw[s] = jnp.dot(keys(0, s), half_of(q_t, u, sh), preferred_element_type=F32)
-            draw[s] = jnp.dot(keys(1, s), half_of(da_t, u, sh), preferred_element_type=F32)
-        return 0
+    def raw(w):
+        def one(u, _):
+            for sh in range(2):
+                s = 2 * u + sh
+                (sraw, draw)[w][s] = jnp.dot(
+                    keys(w, s), half_of((q_t, da_t)[w], u, sh), preferred_element_type=F32
+                )
+            return 0
+
+        lax.fori_loop(0, 4, one, 0)
 
     d_own.wait()
     take(got_d.at[0:15], sd.at[0], rd.at[0])
@@ -501,19 +524,8 @@
     col_start(e_src, e_slot, se.at[0], re.at[0])
 
     kv_keep.wait()
-    for copy in kv_out:
-        copy.wait_send()
-    kv_mate.wait_send()
-    for o in range(4):
-        came = rmod(zlo + 4 - o, 4) * 2
-        remote(
-            kv_all.at[came + core], kv_all.at[came + 1 - core], skf.at[o], rkf.at[o], mate
-        ).wait_recv()
-        if o > 0:
-            remote(
-                kv_all.at[came + core], kv_all.at[came + core], skf.at[o], rkf.at[o], mate
-            ).wait_send()
-    lax.fori_loop(0, 4, raw, 0)
+    pass_keys(0)
+
     def store(i, _):
         pairout_ref[i] = pf[pl.ds(i * 32, 32), :].astype(BF16)
         return 0
@@ -521,6 +533,13 @@
     lax.fori_loop(0, 64, store, 0, unroll=4)
     out_pair = pltpu.make_async_copy(pairout_ref, pairout_hbm, loc.at[14])
     out_pair.start()
+    keys_passed(0)
+    raw(0)
+    pass_keys(1)
+    for copy in kv_out:
+        copy.wait_send()
+    keys_passed(1)
+    raw(1)
     dbias[...] = jnp.zeros_like(dbias)
     own_e.wait()
     take(bias_got.at[0:15], se.at[0], re.at[0])
@@ -852,8 +871,8 @@
             v((64, 768), F32), v((64, 768), F32), v((64, 128), F32), v((8, 8, 384), F32),
             v((16, 8, 384), F32), v((2, 8, 384), F32), v((8, 384), F32), v((8, 8, 384), F32),
             dma((3,)), dma((3,)), dma((2,)), dma((2,)), dma((2,)), dma((2,)),
-            dma((1,)), dma((1,)), dma((1,)), dma((1,)), dma((4,)), dma((4,)),
-            dma((4,)), dma((4,)), dma((1,)), dma((1,)),
+            dma((1,)), dma((1,)), dma((1,)), dma((1,)), dma((2, 4)), dma((2, 4)),
+            dma((2, 4)), dma((2, 4)), dma((1,)), dma((1,)),
             dma((4,)), dma((4,)), dma((4,)), dma((4,)), dma((4, 4)), dma((4, 4)),
             dma((2,)), dma((2,)), dma((1,)), dma((1,)), dma((1,)), dma((1,)),
             dma((1,)), dma((1,)), dma((30,)), dma((4,)), pltpu.SemaphoreType.REGULAR,

time: 101 us -> 99.4 us (0.984)
  Pallas kernels: 98.8 us -> 97.7 us
    pallas_call x1, Pallas kernels: 96.1 us -> 95 us  [on_device(): pl.pallas_call(step_kernel, out_shape=(jax.ShapeDtypeStruct((64, 32, 128)...]
where the time goes in v8:
time: 99.4 us; the launch traced here: 98.3 us
  Pallas kernels  97.7 us (98%)
    pallas_call x1, Pallas kernels, on_device(): pl.pallas_call(step_kernel, out_shape=(jax.ShapeDtypeStruct((64, 32, 128)...  95 us
    pallas_call x1, Pallas kernels, finished(): pl.pallas_call(finish_kernel, out_shape=[jax.ShapeDtypeStruct(x.shape, x....  2.67 us

profile of v8, /device:TPU:8, one launch (start us, length us, event | category | flops | bytes accessed | tf_op | source)
XLA Modules:
  0.0 98.3 jit_solution(7219734665022921509)
XLA Ops:
  0.6 95.0 %step.1 = (bf16[64,32,128]{2,1,0:T(8,128)(2,1)}, bf16[8,48,64]{2,1,0:T(8,128)(2,1)}, f32[2048,128]{1,0:T(8,128)}, f32[8,8,384]{2,1,0:T(8,128)}) custom-call(s32[512]{0:T(512)} %res_ref.1, s32[512]{0:T(512)} %chain_ref.1, s32[512]{0:T(512)} %mask_ref.1, bf16[64,32,128]{2,1,0:T(8,128)(2,1)} %pair_hbm.1, bf16[66,128]{1,0:T(8,128)(2,1)} %relpos_hbm.1, ...), custom_call_target="tpu_custom_call" | custom-call | tf_op jit(solution)/shard_map/step/pallas_call | solution.py:838
  95.6 2.7 %finish.1 = (bf16[64,32,128]{2,1,0:T(8,128)(2,1)}, bf16[8,48,64]{2,1,0:T(8,128)(2,1)}, f32[2048,128]{1,0:T(8,128)}, f32[8,8,384]{2,1,0:T(8,128)}) custom-call(bf16[64,32,128]{2,1,0:T(8,128)(2,1)} %get-tuple-element.12.refs_0_, bf16[8,48,64]{2,1,0:T(8,128)(2,1)} %get-tuple-element.13.refs_1_, f32[2048,128]{1,0:T(8,128)} %get-tuple-element.14.refs_2_, ...), custom_call_target="tpu_custom_call" | custom-call | tf_op jit(solution)/shard_map/finish/pallas_call | solution.py:818

commit v9 on v8

--- a/solution.py
+++ b/solution.py
@@ -213,7 +213,7 @@
         zl_s[at, :] = layer_norm(jnp.concatenate(parts, 0), -1).astype(BF16)
         return 0
 
-    lax.fori_loop(0, 8, normed_rows, 0, unroll=2)
+    lax.fori_loop(0, 8, normed_rows, 0, unroll=4)
     loads[2].wait()
     tri_t[...] = tri_w[:, :512].astype(F32).T.astype(BF16)
 
@@ -489,7 +489,7 @@
                 )
             return 0
 
-        lax.fori_loop(0, 4, one, 0)
+        lax.fori_loop(0, 4, one, 0, unroll=2)
 
     d_own.wait()
     take(got_d.at[0:15], sd.at[0], rd.at[0])
@@ -498,7 +498,7 @@
         lrf[pl.ds(c * 128, 128), :] = got_d[c].reshape(128, 128).astype(F32)
         return 0
 
-    lax.fori_loop(0, 16, widen, 0)
+    lax.fori_loop(0, 16, widen, 0, unroll=4)
 
     def stage3(t, _):
         tn = layer_norm(

time: 99.4 us -> 98.2 us (0.988)
  no operation moved by 1% of the time
where the time goes in v9:
time: 98.2 us; the launch traced here: 97.7 us
  Pallas kernels  97 us (99%)
    pallas_call x1, Pallas kernels, on_device(): pl.pallas_call(step_kernel, out_shape=(jax.ShapeDtypeStruct((64, 32, 128)...  94.4 us
    pallas_call x1, Pallas kernels, finished(): pl.pallas_call(finish_kernel, out_shape=[jax.ShapeDtypeStruct(x.shape, x....  2.67 us

profile of v9, /device:TPU:8, one launch (start us, length us, event | category | flops | bytes accessed | tf_op | source)
XLA Modules:
  0.0 97.7 jit_solution(3447814211295107189)
XLA Ops:
  0.6 94.4 %step.1 = (bf16[64,32,128]{2,1,0:T(8,128)(2,1)}, bf16[8,48,64]{2,1,0:T(8,128)(2,1)}, f32[2048,128]{1,0:T(8,128)}, f32[8,8,384]{2,1,0:T(8,128)}) custom-call(s32[512]{0:T(512)} %res_ref.1, s32[512]{0:T(512)} %chain_ref.1, s32[512]{0:T(512)} %mask_ref.1, bf16[64,32,128]{2,1,0:T(8,128)(2,1)} %pair_hbm.1, bf16[66,128]{1,0:T(8,128)(2,1)} %relpos_hbm.1, ...), custom_call_target="tpu_custom_call" | custom-call | tf_op jit(solution)/shard_map/step/pallas_call | solution.py:838
  95.0 2.7 %finish.1 = (bf16[64,32,128]{2,1,0:T(8,128)(2,1)}, bf16[8,48,64]{2,1,0:T(8,128)(2,1)}, f32[2048,128]{1,0:T(8,128)}, f32[8,8,384]{2,1,0:T(8,128)}) custom-call(bf16[64,32,128]{2,1,0:T(8,128)(2,1)} %get-tuple-element.12.refs_0_, bf16[8,48,64]{2,1,0:T(8,128)(2,1)} %get-tuple-element.13.refs_1_, f32[2048,128]{1,0:T(8,128)} %get-tuple-element.14.refs_2_, ...), custom_call_target="tpu_custom_call" | custom-call | tf_op jit(solution)/shard_map/finish/pallas_call | solution.py:818
